TPU v7x, 128 devices: a whole 4x4x4 slice. The times are simulated.
128 devices in a mesh: ctx: 8 (over x, z_lo), fsdp: 16 (over z_hi, y, core).
Axes of the slice: x: 4, y: 4, z: 4 (z_hi: 2, z_lo: 2; z = z_hi * 2 + z_lo), core: 2. Of those that a mesh axis runs over, the one named last changes fastest.
Arguments:
- inputs: bfloat16 [16, 1024, 1152], P('fsdp', 'ctx'), may hold values from -6 to 6
- out_grad: bfloat16 [16, 1024, 1152], P('fsdp', 'ctx'), may hold values from -6 to 6
- positions: int32 [16, 1024], P('fsdp', 'ctx'), may hold values from 0 to 1023, as said below
- block_order: int32 [8, 2], replicated, may hold values from 0 to 15, as said below
- w_query: bfloat16 [1152, 1024], P('fsdp'), may hold values from -0.1875 to 0.1875
- w_key: bfloat16 [1152, 256], P('fsdp'), may hold values from -0.1875 to 0.1875
- w_value: bfloat16 [1152, 256], P('fsdp'), may hold values from -0.1875 to 0.1875
- w_output: bfloat16 [1024, 1152], P(None, 'fsdp'), may hold values from -0.1875 to 0.1875
- w_gate: bfloat16 [6912, 1152], P('fsdp'), may hold values from -0.1875 to 0.1875
- w_up: bfloat16 [6912, 1152], P('fsdp'), may hold values from -0.1875 to 0.1875
- w_down: bfloat16 [6912, 1152], P('fsdp'), may hold values from -0.078125 to 0.078125
- gain_in: bfloat16 [1152], P('fsdp'), may hold values from 0.099609375 to 1.8984375
- gain_query: bfloat16 [256], P('fsdp'), may hold values from 0.099609375 to 1.8984375
- gain_key: bfloat16 [256], P('fsdp'), may hold values from 0.099609375 to 1.8984375
- gain_attn: bfloat16 [1152], P('fsdp'), may hold values from 0.099609375 to 1.8984375
- gain_pre: bfloat16 [1152], P('fsdp'), may hold values from 0.099609375 to 1.8984375
- gain_post: bfloat16 [1152], P('fsdp'), may hold values from 0.099609375 to 1.8984375
Outputs:
- outputs: bfloat16 [16, 1024, 1152], P('fsdp', 'ctx')
- in_grad: bfloat16 [16, 1024, 1152], P('fsdp', 'ctx')
- grad_w_query: float32 [1152, 1024], P('fsdp')
- grad_w_key: float32 [1152, 256], P('fsdp')
- grad_w_value: float32 [1152, 256], P('fsdp')
- grad_w_output: float32 [1024, 1152], P(None, 'fsdp')
- grad_w_gate: float32 [6912, 1152], P('fsdp')
- grad_w_up: float32 [6912, 1152], P('fsdp')
- grad_w_down: float32 [6912, 1152], P('fsdp')
- grad_gain_in: float32 [1152], P('fsdp')
- grad_gain_query: float32 [256], P('fsdp')
- grad_gain_key: float32 [256], P('fsdp')
- grad_gain_attn: float32 [1152], P('fsdp')
- grad_gain_pre: float32 [1152], P('fsdp')
- grad_gain_post: float32 [1152], P('fsdp')
Inputs may be any that keep to these rules, and one draw needn't show every extreme that they name: `block_order`: row c names the two blocks of 64 tokens in device c's rows, in order; every block appears once, and a row holds blocks k and m with k + m one less than the number of blocks. `positions`: each row's offset from the start of its document in the sequence; documents begin at the sequence's first token and at random places; sequence 0 is one document.
All inputs are finite; a program needn't handle non-finite values.
Results may differ from a plain program's by a relative error of at most 0.03.
Values may be sent and summed in bfloat16 or wider, within the bound.
No kernel may reach another device: no remote copies, remote signals or barrier semaphores. Data moves between devices by JAX's collectives and lax.ppermute only.
A program may use at most 128 MiB of HBM per device.

v0:
```python
import jax
import jax.numpy as jnp
from jax import lax
from jax.sharding import PartitionSpec as P

H = 4
HD = 256


EPS = 1e-06
ROPE_BASE = 1000000.0
GELU_C = 0.7978845608028654
GELU_A = 0.044715


def norm_forward(values, gain):
    inverse = lax.rsqrt(jnp.mean(values * values, axis=-1, keepdims=True) + EPS)
    unit = values * inverse
    return (unit * gain, unit, inverse)


def norm_backward(upstream, unit, inverse, gain):
    scaled = upstream * gain
    inner = jnp.mean(scaled * unit, axis=-1, keepdims=True)
    leading = tuple(range(upstream.ndim - 1))
    return (inverse * (scaled - unit * inner), jnp.sum(upstream * unit, axis=leading))


def gelu_pair(gate):
    inner = GELU_C * (gate + GELU_A * gate * gate * gate)
    tangent = jnp.tanh(inner)
    value = 0.5 * gate * (1.0 + tangent)
    slope = 0.5 * (1.0 + tangent) + 0.5 * gate * (1.0 - tangent * tangent) * GELU_C * (
        1.0 + 3.0 * GELU_A * gate * gate
    )
    return (value, slope)


def rope_tables(positions, width):
    half = width // 2
    freqs = ROPE_BASE ** (-2.0 * jnp.arange(half, dtype=jnp.float32) / width)
    angles = positions.astype(jnp.float32)[:, None] * freqs[None, :]
    return (jnp.cos(angles), jnp.sin(angles))


def rotate(values, cosine, sine):
    half = values.shape[-1] // 2
    first = values[..., :half]
    second = values[..., half:]
    return jnp.concatenate(
        [first * cosine - second * sine, second * cosine + first * sine], axis=-1
    )


def rotate_back(values, cosine, sine):
    half = values.shape[-1] // 2
    first = values[..., :half]
    second = values[..., half:]
    return jnp.concatenate(
        [first * cosine + second * sine, second * cosine - first * sine], axis=-1
    )


def sequence_rows(order_flat, first_row, count, block):
    rows = first_row + jnp.arange(count, dtype=jnp.int32)
    slots = rows // block
    table = jnp.arange(order_flat.shape[0], dtype=jnp.int32)
    picked = jnp.sum(jnp.where(slots[:, None] == table[None, :], order_flat[None, :], 0), axis=1)
    return picked * block + rows % block


def body(
    inputs,
    out_grad,
    positions,
    block_order,
    w_query,
    w_key,
    w_value,
    w_output,
    w_gate,
    w_up,
    w_down,
    gain_in,
    gain_query,
    gain_key,
    gain_attn,
    gain_pre,
    gain_post,
):
    f32 = jnp.float32
    low = jnp.bfloat16
    tokens = inputs[0]
    local = tokens.shape[0]
    parts = lax.axis_size("ctx")
    total = local * parts
    block = local // 2
    gathered = (
        lax.all_gather(w_query, "fsdp", axis=0, tiled=True),
        lax.all_gather(w_key, "fsdp", axis=0, tiled=True),
        lax.all_gather(w_value, "fsdp", axis=0, tiled=True),
        lax.all_gather(w_output, "fsdp", axis=1, tiled=True),
        lax.all_gather(gain_in, "fsdp", axis=0, tiled=True),
        lax.all_gather(gain_query, "fsdp", axis=0, tiled=True),
        lax.all_gather(gain_key, "fsdp", axis=0, tiled=True),
        lax.all_gather(gain_attn, "fsdp", axis=0, tiled=True),
        lax.all_gather(gain_pre, "fsdp", axis=0, tiled=True),
        lax.all_gather(gain_post, "fsdp", axis=0, tiled=True),
    )
    full_query, full_key, full_value, full_output = (
        gathered[0],
        gathered[1],
        gathered[2],
        gathered[3],
    )
    norm_in, norm_query, norm_key, norm_attn, norm_pre, norm_post = [
        g.astype(f32) for g in gathered[4:]
    ]
    ctx_index = lax.axis_index("ctx")
    order_flat = block_order.reshape(-1)
    my_seq = sequence_rows(order_flat, ctx_index * local, local, block)
    all_seq = sequence_rows(order_flat, 0, total, block)
    flat_in = tokens.astype(f32)
    normed_full, unit_in, inv_in = norm_forward(flat_in, norm_in)
    normed_in = normed_full.astype(low)
    queries = jnp.dot(normed_in, full_query, preferred_element_type=f32).reshape(local, H, HD)
    keys_raw = jnp.dot(normed_in, full_key, preferred_element_type=f32)
    values = jnp.dot(normed_in, full_value, preferred_element_type=f32).astype(low)
    query_normed, query_unit, query_inv = norm_forward(queries, norm_query)
    key_normed, key_unit, key_inv = norm_forward(keys_raw, norm_key)
    cosine, sine = rope_tables(positions[0], HD)
    scale = HD ** (-0.5)
    query_rot = (rotate(query_normed, cosine[:, None, :], sine[:, None, :]) * scale).astype(low)
    key_rot = rotate(key_normed, cosine, sine).astype(low)
    key_all, value_all = (
        lax.all_gather(key_rot, "ctx", axis=0, tiled=True),
        lax.all_gather(values, "ctx", axis=0, tiled=True),
    )
    scores = jnp.einsum("qhd,kd->hqk", query_rot, key_all, preferred_element_type=f32)
    allowed = my_seq[:, None] >= all_seq[None, :]
    scores = jnp.where(allowed[None], scores, -jnp.inf)
    highest = jnp.max(scores, axis=-1, keepdims=True)
    log_total = highest + jnp.log(jnp.sum(jnp.exp(scores - highest), axis=-1, keepdims=True))
    probs_full = jnp.exp(scores - log_total)
    probs = probs_full.astype(low)
    attended = (
        jnp.einsum("hqk,kd->qhd", probs, value_all, preferred_element_type=f32)
        .reshape(local, H * HD)
        .astype(low)
    )
    branch_attn = jnp.dot(attended, full_output, preferred_element_type=f32)
    attn_normed, attn_unit, attn_inv = norm_forward(branch_attn, norm_attn)
    residual = flat_in + attn_normed
    pre_full, pre_unit, pre_inv = norm_forward(residual, norm_pre)
    normed_pre = pre_full.astype(low)
    rows_all = lax.all_gather(normed_pre, "fsdp", axis=0, tiled=True)
    gate = jnp.einsum("td,fd->tf", rows_all, w_gate, preferred_element_type=f32)
    upper = jnp.einsum("td,fd->tf", rows_all, w_up, preferred_element_type=f32)
    gelu_value, gelu_slope = gelu_pair(gate)
    hidden = (gelu_value * upper).astype(low)
    branch_ffn = lax.psum_scatter(
        jnp.dot(hidden, w_down, preferred_element_type=f32).astype(jnp.bfloat16),
        "fsdp",
        scatter_dimension=0,
        tiled=True,
    ).astype(jnp.float32)
    post_normed, post_unit, post_inv = norm_forward(branch_ffn, norm_post)
    outputs = (residual + post_normed).astype(low)
    grad_out = out_grad[0].astype(f32)
    grad_ffn_full, grad_gain_post = norm_backward(grad_out, post_unit, post_inv, norm_post)
    grad_ffn = grad_ffn_full.astype(low)
    grad_all = lax.all_gather(grad_ffn, "fsdp", axis=0, tiled=True)
    grad_hidden = jnp.einsum("td,fd->tf", grad_all, w_down, preferred_element_type=f32)
    grad_gate = (grad_hidden * upper * gelu_slope).astype(low)
    grad_up = (grad_hidden * gelu_value).astype(low)
    shard_gate = jnp.einsum("tf,td->fd", grad_gate, rows_all, preferred_element_type=f32)
    shard_up = jnp.einsum("tf,td->fd", grad_up, rows_all, preferred_element_type=f32)
    shard_down = jnp.einsum("tf,td->fd", hidden, grad_all, preferred_element_type=f32)
    grad_pre = lax.psum_scatter(
        (
            jnp.dot(grad_gate, w_gate, preferred_element_type=f32)
            + jnp.dot(grad_up, w_up, preferred_element_type=f32)
        ).astype(jnp.bfloat16),
        "fsdp",
        scatter_dimension=0,
        tiled=True,
    ).astype(jnp.float32)
    grad_from_pre, grad_gain_pre = norm_backward(grad_pre, pre_unit, pre_inv, norm_pre)
    grad_residual = grad_out + grad_from_pre
    grad_branch_full, grad_gain_attn = norm_backward(grad_residual, attn_unit, attn_inv, norm_attn)
    grad_branch = grad_branch_full.astype(low)
    term_output = jnp.einsum("tc,td->cd", attended, grad_branch, preferred_element_type=f32)
    grad_attended = jnp.einsum(
        "td,cd->tc", grad_branch, full_output, preferred_element_type=f32
    ).astype(low)
    grad_heads = grad_attended.reshape(local, H, HD)
    attended_heads = attended.reshape(local, H, HD)
    delta = jnp.transpose(jnp.sum(grad_heads.astype(f32) * attended_heads.astype(f32), axis=-1))[
        :, :, None
    ]
    grad_probs = jnp.einsum("qhd,kd->hqk", grad_heads, value_all, preferred_element_type=f32)
    grad_scores = (probs_full * (grad_probs - delta)).astype(low)
    value_term = jnp.einsum("hqk,qhd->kd", probs, grad_heads, preferred_element_type=f32)
    key_term = jnp.einsum("hqk,qhd->kd", grad_scores, query_rot, preferred_element_type=f32)
    key_value_terms = jnp.concatenate([key_term, value_term], axis=1)
    grad_query_rot = jnp.einsum("hqk,kd->qhd", grad_scores, key_all, preferred_element_type=f32)
    summed_kv = lax.psum_scatter(
        key_value_terms.astype(jnp.bfloat16), "ctx", scatter_dimension=0, tiled=True
    ).astype(jnp.float32)
    grad_key_rot = summed_kv[:, :HD]
    grad_values = summed_kv[:, HD:].astype(low)
    grad_q_normed = rotate_back(grad_query_rot * scale, cosine[:, None, :], sine[:, None, :])
    grad_q_full, grad_gain_query = norm_backward(grad_q_normed, query_unit, query_inv, norm_query)
    grad_k_normed = rotate_back(grad_key_rot, cosine, sine)
    grad_k_full, grad_gain_key = norm_backward(grad_k_normed, key_unit, key_inv, norm_key)
    grad_q_in = grad_q_full.reshape(local, H * HD).astype(low)
    grad_k_in = grad_k_full.astype(low)
    term_query = jnp.einsum("td,tc->dc", normed_in, grad_q_in, preferred_element_type=f32)
    term_key = jnp.einsum("td,tc->dc", normed_in, grad_k_in, preferred_element_type=f32)
    term_value = jnp.einsum("td,tc->dc", normed_in, grad_values, preferred_element_type=f32)
    grad_normed = (
        jnp.einsum("tc,dc->td", grad_q_in, full_query, preferred_element_type=f32)
        + jnp.einsum("tc,dc->td", grad_k_in, full_key, preferred_element_type=f32)
        + jnp.einsum("tc,dc->td", grad_values, full_value, preferred_element_type=f32)
    )
    grad_from_in, grad_gain_in = norm_backward(grad_normed, unit_in, inv_in, norm_in)
    in_grad = (grad_residual + grad_from_in).astype(low)
    shards = (
        lax.psum_scatter(
            term_query.astype(jnp.bfloat16), "fsdp", scatter_dimension=0, tiled=True
        ).astype(jnp.float32),
        lax.psum_scatter(
            term_key.astype(jnp.bfloat16), "fsdp", scatter_dimension=0, tiled=True
        ).astype(jnp.float32),
        lax.psum_scatter(
            term_value.astype(jnp.bfloat16), "fsdp", scatter_dimension=0, tiled=True
        ).astype(jnp.float32),
        lax.psum_scatter(
            term_output.astype(jnp.bfloat16), "fsdp", scatter_dimension=1, tiled=True
        ).astype(jnp.float32),
        lax.psum_scatter(
            grad_gain_in.astype(jnp.bfloat16), "fsdp", scatter_dimension=0, tiled=True
        ).astype(jnp.float32),
        lax.psum_scatter(
            grad_gain_query.astype(jnp.bfloat16), "fsdp", scatter_dimension=0, tiled=True
        ).astype(jnp.float32),
        lax.psum_scatter(
            grad_gain_key.astype(jnp.bfloat16), "fsdp", scatter_dimension=0, tiled=True
        ).astype(jnp.float32),
        lax.psum_scatter(
            grad_gain_attn.astype(jnp.bfloat16), "fsdp", scatter_dimension=0, tiled=True
        ).astype(jnp.float32),
        lax.psum_scatter(
            grad_gain_pre.astype(jnp.bfloat16), "fsdp", scatter_dimension=0, tiled=True
        ).astype(jnp.float32),
        lax.psum_scatter(
            grad_gain_post.astype(jnp.bfloat16), "fsdp", scatter_dimension=0, tiled=True
        ).astype(jnp.float32),
    )
    totals = (
        lax.psum(shards[0].astype(jnp.bfloat16), "ctx").astype(jnp.float32),
        lax.psum(shards[1].astype(jnp.bfloat16), "ctx").astype(jnp.float32),
        lax.psum(shards[2].astype(jnp.bfloat16), "ctx").astype(jnp.float32),
        lax.psum(shards[3].astype(jnp.bfloat16), "ctx").astype(jnp.float32),
        lax.psum(shard_gate.astype(jnp.bfloat16), "ctx").astype(jnp.float32),
        lax.psum(shard_up.astype(jnp.bfloat16), "ctx").astype(jnp.float32),
        lax.psum(shard_down.astype(jnp.bfloat16), "ctx").astype(jnp.float32),
        lax.psum(shards[4].astype(jnp.bfloat16), "ctx").astype(jnp.float32),
        lax.psum(shards[5].astype(jnp.bfloat16), "ctx").astype(jnp.float32),
        lax.psum(shards[6].astype(jnp.bfloat16), "ctx").astype(jnp.float32),
        lax.psum(shards[7].astype(jnp.bfloat16), "ctx").astype(jnp.float32),
        lax.psum(shards[8].astype(jnp.bfloat16), "ctx").astype(jnp.float32),
        lax.psum(shards[9].astype(jnp.bfloat16), "ctx").astype(jnp.float32),
    )
    return (
        outputs[None],
        in_grad[None],
        totals[0],
        totals[1],
        totals[2],
        totals[3],
        totals[4],
        totals[5],
        totals[6],
        totals[7],
        totals[8],
        totals[9],
        totals[10],
        totals[11],
        totals[12],
    )


def solution(mesh):
    placed = (
        P("fsdp", "ctx", None),
        P("fsdp", "ctx", None),
        P("fsdp", "ctx"),
        P(),
        P("fsdp", None),
        P("fsdp", None),
        P("fsdp", None),
        P(None, "fsdp"),
        P("fsdp", None),
        P("fsdp", None),
        P("fsdp", None),
        P("fsdp"),
        P("fsdp"),
        P("fsdp"),
        P("fsdp"),
        P("fsdp"),
        P("fsdp"),
    )
    return jax.shard_map(
        body,
        mesh=mesh,
        in_specs=placed,
        out_specs=(
            P("fsdp", "ctx", None),
            P("fsdp", "ctx", None),
            P("fsdp", None),
            P("fsdp", None),
            P("fsdp", None),
            P(None, "fsdp"),
            P("fsdp", None),
            P("fsdp", None),
            P("fsdp", None),
            P("fsdp"),
            P("fsdp"),
            P("fsdp"),
            P("fsdp"),
            P("fsdp"),
            P("fsdp"),
        ),
        check_vma=False,
    )
```

profile of v0, /device:TPU:0, one launch (start us, length us, event | category | flops | bytes accessed | tf_op | source)
XLA Modules:
  0.0 1099.8 jit_solution(11387176566763124986)
XLA Ops:
  18.5 70.8 %all-reduce.13 = (bf16[1152]{0:T(1024)(128)(2,1)S(1)}, bf16[256]{0:T(256)(128)(2,1)S(1)}, bf16[256]{0:T(256)(128)(2,1)S(1)}, bf16[1152]{0:T(1024)(128)(2,1)S(1)}...) all-reduce(bf16[1152]{0:T(1024)(128)(2,1)S(1)} %dynamic-update-slic, ...), channel_id=1, replica_groups=mesh['ctx'=8,'fsdp'=16] {'fsdp'}, use_global_device_ids=true, to_apply=%add | all-reduce | flops 5120 | bytes 20480
  89.4 22.2 %all_gather.45 = bf16[1152,256]{1,0:T(8,128)(2,1)S(1)} all-gather(bf16[72,256]{1,0:T(8,128)(2,1)} %param.22), channel_id=1, replica_groups=mesh['ctx'=8,'fsdp'=16] {'fsdp'}, dimensions={0}, use_global_device_ids=true | all-gather | bytes 626688 | tf_op jit(solution)/shard_map/all_gather | solution.py:100
  114.0 29.3 %all_gather.47 = bf16[1024,256]{1,0:T(8,128)(2,1)S(1)} all-gather(bf16[128,256]{1,0:T(8,128)(2,1)S(1)} %pad_maximum_fusion.3), channel_id=1, replica_groups=mesh['ctx'=8,'fsdp'=16] {'ctx'}, dimensions={0}, use_global_device_ids=true | all-gather | bytes 589824 | tf_op jit(solution)/shard_map/all_gather | solution.py:136
  143.3 21.2 %all_gather.43 = bf16[1152,256]{1,0:T(8,128)(2,1)S(1)} all-gather(bf16[72,256]{1,0:T(8,128)(2,1)S(1)} %copy-done.39), channel_id=1, replica_groups=mesh['ctx'=8,'fsdp'=16] {'fsdp'}, dimensions={0}, use_global_device_ids=true | all-gather | bytes 626688 | tf_op jit(solution)/shard_map/all_gather | solution.py:101
  165.6 29.2 %all_gather.44 = bf16[1024,256]{1,0:T(8,128)(2,1)S(1)} all-gather(bf16[128,256]{1,0:T(8,128)(2,1)S(1)} %convolution_convert_fusion.10), channel_id=1, replica_groups=mesh['ctx'=8,'fsdp'=16] {'ctx'}, dimensions={0}, use_global_device_ids=true | all-gather | bytes 589824 | tf_op jit(solution)/shard_map/all_gather | solution.py:137
  194.8 4.5 copy.77
  199.3 2.7 multiply_reduce_fusion.7
  205.3 2.7 multiply_reduce_fusion.3
  209.4 55.3 %all-gather.9.cloned.1.call-done = bf16[2048,1152]{1,0:T(8,128)(2,1)} async-done(((bf16[128,1152]{1,0:T(8,128)(2,1)}), bf16[2048,1152]{1,0:T(8,128)(2,1)}) %all-gather.9.cloned.1.call-update) | async-done | bytes 4718608 | tf_op jit(solution)/shard_map/all_gather | solution.py:156
  264.8 5.2 fusion.102
  270.1 4.6 multiply_convert_fusion.1
  275.9 4.6 convolution_convert_fusion
  280.6 81.5 %reduce-scatter.8.cloned.1.call-done = bf16[128,1152]{1,0:T(8,128)(2,1)} async-done(((bf16[2048,1152]{1,0:T(8,128)(2,1)}), bf16[128,1152]{1,0:T(8,128)(2,1)}) %reduce-scatter.8.cloned.1.call-update) | async-done | bytes 294928 | tf_op jit(solution)/shard_map/reduce_scatter | solution.py:161
  366.8 56.5 %all-gather.11.cloned.1.call-done = bf16[2048,1152]{1,0:T(8,128)(2,1)} async-done(((bf16[128,1152]{1,0:T(8,128)(2,1)}), bf16[2048,1152]{1,0:T(8,128)(2,1)}) %all-gather.11.cloned.1.call-update) | async-done | bytes 4718608 | tf_op jit(solution)/shard_map/all_gather | solution.py:172
  423.3 8.5 multiply_convert_fusion
  431.8 3.0 fusion.103
  434.9 4.6 add_convert_fusion
  439.6 81.6 %reduce-scatter.10.cloned.1.call-done = bf16[128,1152]{1,0:T(8,128)(2,1)} async-done(((bf16[2048,1152]{1,0:T(8,128)(2,1)}), bf16[128,1152]{1,0:T(8,128)(2,1)}) %reduce-scatter.10.cloned.1.call-update) | async-done | bytes 294928 | tf_op jit(solution)/shard_map/reduce_scatter | solution.py:179
  522.4 2.3 multiply_reduce_fusion
  534.0 38.7 %reduce-scatter.12.cloned.1.call-done = bf16[128,512]{1,0:T(8,128)(2,1)} async-done(((bf16[1024,512]{1,0:T(8,128)(2,1)}), bf16[128,512]{1,0:T(8,128)(2,1)}) %reduce-scatter.12.cloned.1.call-update) | async-done | bytes 131088 | tf_op jit(solution)/shard_map/reduce_scatter | solution.py:207
  577.8 2.2 convolution_convert_fusion.1
  581.8 2.4 convolution_convert_fusion.2
  585.6 6.5 convolution_convert_fusion.3
  592.2 3.4 convolution_convert_fusion.4
  597.5 65.1 %all-reduce.12 = (bf16[1152]{0:T(1024)(128)(2,1)S(1)}, bf16[256]{0:T(256)(128)(2,1)S(1)}, bf16[256]{0:T(256)(128)(2,1)S(1)}, bf16[1152]{0:T(1024)(128)(2,1)S(1)}...) all-reduce(bf16[1152]{0:T(1024)(128)(2,1)S(1)} %get-tuple-element.2, ...), channel_id=9, replica_groups=mesh['ctx'=8,'fsdp'=16] {'fsdp'}, use_global_device_ids=true, to_apply=%region_32.33.clone | all-reduce | flops 5120 | bytes 20480
  666.0 40.4 %reduce-scatter.16.cloned.1.call-done = bf16[72,256]{1,0:T(8,128)(2,1)} async-done(((bf16[1152,256]{1,0:T(8,128)(2,1)}), bf16[72,256]{1,0:T(8,128)(2,1)}) %reduce-scatter.16.cloned.1.call-update) | async-done | bytes 36880 | tf_op jit(solution)/shard_map/reduce_scatter | solution.py:232
  706.5 6.3 convolution_convert_fusion.5
  712.8 68.7 %reduce-scatter.20.cloned.1.call-done = bf16[1024,72]{0,1:T(8,128)(2,1)} async-done(((bf16[1024,1152]{0,1:T(8,128)(2,1)}), bf16[1024,72]{0,1:T(8,128)(2,1)}) %reduce-scatter.20.cloned.1.call-update) | async-done | bytes 147472 | tf_op jit(solution)/shard_map/reduce_scatter | solution.py:238
  781.5 75.3 %reduce-scatter.14.cloned.1.call-done = bf16[72,1024]{1,0:T(8,128)(2,1)} async-done(((bf16[1152,1024]{1,0:T(8,128)(2,1)}), bf16[72,1024]{1,0:T(8,128)(2,1)}) %reduce-scatter.14.cloned.1.call-update) | async-done | bytes 147472 | tf_op jit(solution)/shard_map/reduce_scatter | solution.py:229
  857.7 70.8 %all-reduce.19.cloned.1.call-done = (bf16[72,256]{1,0:T(8,128)(2,1)}, bf16[72,256]{1,0:T(8,128)(2,1)}, bf16[72]{0:T(256)(128)(2,1)}, bf16[16]{0:T(256)(128)(2,1)...) async-done(((bf16[72,256]{1,0:T(8,128)(2,1)}, bf16[72,256]{1,0:T(8,128)(2,1)}, bf16[72]{0:T(256)(128)(2,1)}, ...) | async-done | bytes 74384 | tf_op jit(solution)/shard_map/psum | solution.py:262
  938.2 146.2 %all-reduce.21.cloned.1.call-done = (bf16[72,1024]{1,0:T(8,128)(2,1)}, bf16[1024,72]{0,1:T(8,128)(2,1)}, bf16[432,1152]{1,0:T(8,128)(2,1)}, bf16[432,1152]{1,0:T(8,128)(2,1)}, bf16[432,1152]{1,0:T(8,128)(2,1)}) async-done(((bf16[72,1024]{1,0:T(8,128)(2,1)}, bf16[1024,72]{0,1:T(8,128)(2,1)}, bf16[432,1152]{1,0:T(8,128)(2,1)}, bf16[432,1152]{1,0:T(8,128)(2,1)}, bf16[432,1152]{1,0:T(8,128)(2,1)}), ...) | async-done | bytes 3280912 | tf_op jit(solution)/shard_map/psum | solution.py:261
  1087.8 2.7 convert_element_type.287
  (243 shorter events, 63.4 us)
Async XLA Ops:
  7.2 268.7 %copy-start = (bf16[432,1152]{1,0:T(8,128)(2,1)S(1)}, bf16[432,1152]{1,0:T(8,128)(2,1)}, u32[]{:S(2)}) copy-start(bf16[432,1152]{1,0:T(8,128)(2,1)} %param.27) | copy-start | bytes 2985988
  7.2 158.1 %copy-start.2 = (bf16[1,128,1152]{2,1,0:T(8,128)(2,1)S(1)}, bf16[1,128,1152]{2,1,0:T(8,128)(2,1)}, u32[]{:S(2)}) copy-start(bf16[1,128,1152]{2,1,0:T(8,128)(2,1)} %param.17) | copy-start | bytes 884740
  7.2 106.0 %copy-start.48 = (s32[1,128]{1,0:T(1,128)S(1)}, s32[1,128]{1,0:T(1,128)}, u32[]{:S(2)}) copy-start(s32[1,128]{1,0:T(1,128)} %param.19) | copy-start | bytes 1540
  7.2 136.1 %copy-start.39 = (bf16[72,256]{1,0:T(8,128)(2,1)S(1)}, bf16[72,256]{1,0:T(8,128)(2,1)}, u32[]{:S(2)}) copy-start(bf16[72,256]{1,0:T(8,128)(2,1)} %param.23) | copy-start | bytes 110596
  7.2 187.6 %all-gather.5.cloned.1.call-start = ((), (), s32[]{:S(2)}) async-start(), calls=%async_computation.7 | async-start | bytes 2506752 | tf_op jit(solution)/shard_map/all_gather | solution.py:99
  8.0 197.3 %all-gather.7.cloned.1.call-start = ((), (), s32[]{:S(2)}) async-start(), calls=%async_computation.8 | async-start | bytes 2506752 | tf_op jit(solution)/shard_map/all_gather | solution.py:102
  8.7 256.1 %all-gather.9.cloned.1.call-start = ((), (), s32[]{:S(2)}) async-start(), calls=%async_computation.9 | async-start | bytes 5013504 | tf_op jit(solution)/shard_map/all_gather | solution.py:156
  113.0 52.6 %copy-start.21 = (f32[128,256]{1,0:T(8,128)}, f32[128,256]{1,0:T(8,128)S(1)}, u32[]{:S(2)}) copy-start(f32[128,256]{1,0:T(8,128)S(1)} %get-tuple-element.73) | copy-start | bytes 393220
  113.3 86.0 %copy-start.40 = (f32[128]{0:T(128)}, f32[128]{0:T(128)S(1)}, u32[]{:S(2)}) copy-start(f32[128]{0:T(128)S(1)} %convert_bitcast_fusion.1) | copy-start | bytes 1540
  113.6 88.5 %copy-start.32 = (f32[128,128]{1,0:T(8,128)}, f32[128,128]{1,0:T(8,128)S(1)}, u32[]{:S(2)}) copy-start(f32[128,128]{1,0:T(8,128)S(1)} %get-tuple-element.66) | copy-start | bytes 196612
  113.6 88.5 %copy-start.34 = (f32[128,128]{1,0:T(8,128)}, f32[128,128]{1,0:T(8,128)S(1)}, u32[]{:S(2)}) copy-start(f32[128,128]{1,0:T(8,128)S(1)} %get-tuple-element.67) | copy-start | bytes 196612
  143.3 59.5 %copy-start.12 = (bf16[1024,256]{1,0:T(8,128)(2,1)}, bf16[1024,256]{1,0:T(8,128)(2,1)S(1)}, u32[]{:S(2)}) copy-start(bf16[1024,256]{1,0:T(8,128)(2,1)S(1)} %all_gather.47) | copy-start | bytes 1572868
  194.8 8.9 copy-start.36
  209.2 153.0 %reduce-scatter.8.cloned.1.call-start = ((), (), s32[]{:S(2)}) async-start(), calls=%async_computation.10 | async-start | bytes 5013504 | tf_op jit(solution)/shard_map/reduce_scatter | solution.py:161
  280.5 82.7 %copy-start.14 = (bf16[1,128,1152]{2,1,0:T(8,128)(2,1)S(1)}, bf16[1,128,1152]{2,1,0:T(8,128)(2,1)}, u32[]{:S(2)}) copy-start(bf16[1,128,1152]{2,1,0:T(8,128)(2,1)} %param.18) | copy-start | bytes 884740
  280.6 142.7 %all-gather.11.cloned.1.call-start = ((), (), s32[]{:S(2)}) async-start(), calls=%async_computation.11 | async-start | bytes 5013504 | tf_op jit(solution)/shard_map/all_gather | solution.py:172
  366.5 154.6 %reduce-scatter.10.cloned.1.call-start = ((), (), s32[]{:S(2)}) async-start(), calls=%async_computation.12 | async-start | bytes 5013504 | tf_op jit(solution)/shard_map/reduce_scatter | solution.py:179
  423.3 8.6 copy-start.45
  439.5 82.9 %copy-start.11 = (bf16[128,1152]{1,0:T(8,128)(2,1)S(1)}, bf16[128,1152]{1,0:T(8,128)(2,1)}, u32[]{:S(2)}) copy-start(bf16[128,1152]{1,0:T(8,128)(2,1)} %reduce-scatter.8.cloned.1.call-done) | copy-start | bytes 884740
  439.5 133.2 %reduce-scatter.12.cloned.1.call-start = ((), (), s32[]{:S(2)}) async-start(), calls=%async_computation.13 | async-start | bytes 1179648 | tf_op jit(solution)/shard_map/reduce_scatter | solution.py:207
  532.9 43.0 %copy-start.41 = (f32[128]{0:T(128)S(1)}, f32[128]{0:T(128)}, u32[]{:S(2)}) copy-start(f32[128]{0:T(128)} %copy-done.40) | copy-start | bytes 1540
  532.9 43.3 %copy-start.22 = (f32[128,256]{1,0:T(8,128)S(1)}, f32[128,256]{1,0:T(8,128)}, u32[]{:S(2)}) copy-start(f32[128,256]{1,0:T(8,128)} %copy-done.21) | copy-start | bytes 393220
  534.0 43.8 %copy-start.20 = (bf16[256,4,128]{2,0,1:T(8,128)(2,1)S(1)}, bf16[256,4,128]{2,0,1:T(8,128)(2,1)}, u32[]{:S(2)}) copy-start(bf16[256,4,128]{2,0,1:T(8,128)(2,1)} %copy-done.19) | copy-start | bytes 786436
  534.0 132.1 %reduce-scatter.18.cloned.1.call-start = ((), (), s32[]{:S(2)}) async-start(), calls=%async_computation.16 | async-start | bytes 626688 | tf_op jit(solution)/shard_map/reduce_scatter | solution.py:235
  574.8 131.6 %reduce-scatter.16.cloned.1.call-start = ((), (), s32[]{:S(2)}) async-start(), calls=%async_computation.15 | async-start | bytes 626688 | tf_op jit(solution)/shard_map/reduce_scatter | solution.py:232
  577.7 203.7 %reduce-scatter.20.cloned.1.call-start = ((), (), s32[]{:S(2)}) async-start(), calls=%async_computation.17 | async-start | bytes 2506752 | tf_op jit(solution)/shard_map/reduce_scatter | solution.py:238
  580.0 276.7 %reduce-scatter.14.cloned.1.call-start = ((), (), s32[]{:S(2)}) async-start(), calls=%async_computation.14 | async-start | bytes 2506752 | tf_op jit(solution)/shard_map/reduce_scatter | solution.py:229
  584.2 7.9 slice-start
  584.2 344.3 %all-reduce.19.cloned.1.call-start = ((), (), s32[]{:S(2)}) async-start(), calls=%async_computation.18 | async-start | bytes 153600 | tf_op jit(solution)/shard_map/psum | solution.py:262
  585.6 6.5 slice-start.1
  706.5 377.9 %all-reduce.21.cloned.1.call-start = ((), (), s32[]{:S(2)}) async-start(), calls=%async_computation.19 | async-start | bytes 6561792 | tf_op jit(solution)/shard_map/psum | solution.py:261
  712.8 144.0 %copy-start.10 = (f32[128,1152]{1,0:T(8,128)S(1)}, f32[128,1152]{1,0:T(8,128)}, u32[]{:S(2)}) copy-start(f32[128,1152]{1,0:T(8,128)} %copy-done.9) | copy-start | bytes 1769476
  (37 other events, 99.2 us)
Sparse Core Ops, SparseCore 0:
  10.5 51.9 all-gather.4
  64.9 48.2 all-gather.6
  209.3 55.4 all-gather.8
  280.7 81.4 reduce-scatter.7
  366.6 56.6 all-gather.10
  439.6 81.4 reduce-scatter.9
  534.1 38.6 reduce-scatter.11
  576.5 62.8 reduce-scatter.17
  643.1 63.2 reduce-scatter.15
  710.3 71.1 reduce-scatter.19
  785.5 71.2 reduce-scatter.13
  860.2 68.2 all-reduce.18
  932.3 152.0 all-reduce.20
where the time goes:
time: 1100 us
  waiting for transfers between devices  717 us (65%)
  blocking collectives  238 us (22%)
  matrix products  69.1 us (6%)
  other arithmetic  35.6 us (3%)
  local copies, waits for them, and re-layouts  22.2 us (2%)
  between operations  17.4 us (2%)
    psum x1, waiting for transfers between devices, body(): lax.psum(shards[0].astype(jnp.bfloat16), 'ctx').astype(jnp.float32)  146 us
    unnamed x2, blocking collectives  136 us
    reduce_scatter x1, waiting for transfers between devices, body(): lax.psum_scatter((jnp.dot(grad_gate, w_gate, preferred_element_type=f32)...  81.6 us
    reduce_scatter x1, waiting for transfers between devices, body(): lax.psum_scatter(jnp.dot(hidden, w_down, preferred_element_type=f32).asty...  81.5 us
    reduce_scatter x1, waiting for transfers between devices, body(): lax.psum_scatter(term_query.astype(jnp.bfloat16), 'fsdp', scatter_dimensi...  75.3 us
    psum x1, waiting for transfers between devices, body(): lax.psum(shards[1].astype(jnp.bfloat16), 'ctx').astype(jnp.float32)  70.8 us
    reduce_scatter x1, waiting for transfers between devices, body(): lax.psum_scatter(term_output.astype(jnp.bfloat16), 'fsdp', scatter_dimens...  68.7 us
    all_gather x1, waiting for transfers between devices, body(): grad_all = lax.all_gather(grad_ffn, 'fsdp', axis=0, tiled=True)  56.5 us
  transfers between devices with their start and end apart: 13, of which 10 were waited for; matrix products, arithmetic and copies ran while one was open for 6% of the time, Pallas kernels for 0%

commit v1 on v0

--- a/solution.py
+++ b/solution.py
@@ -67,6 +67,10 @@
     table = jnp.arange(order_flat.shape[0], dtype=jnp.int32)
     picked = jnp.sum(jnp.where(slots[:, None] == table[None, :], order_flat[None, :], 0), axis=1)
     return picked * block + rows % block
+
+
+def pad_rows(shard, rows):
+    return jnp.pad(shard, (0, rows - shard.shape[0]))
 
 
 def body(
@@ -93,29 +97,46 @@
     tokens = inputs[0]
     local = tokens.shape[0]
     parts = lax.axis_size("ctx")
+    groups = lax.axis_size("fsdp")
     total = local * parts
     block = local // 2
-    gathered = (
-        lax.all_gather(w_query, "fsdp", axis=0, tiled=True),
-        lax.all_gather(w_key, "fsdp", axis=0, tiled=True),
-        lax.all_gather(w_value, "fsdp", axis=0, tiled=True),
-        lax.all_gather(w_output, "fsdp", axis=1, tiled=True),
-        lax.all_gather(gain_in, "fsdp", axis=0, tiled=True),
-        lax.all_gather(gain_query, "fsdp", axis=0, tiled=True),
-        lax.all_gather(gain_key, "fsdp", axis=0, tiled=True),
-        lax.all_gather(gain_attn, "fsdp", axis=0, tiled=True),
-        lax.all_gather(gain_pre, "fsdp", axis=0, tiled=True),
-        lax.all_gather(gain_post, "fsdp", axis=0, tiled=True),
-    )
-    full_query, full_key, full_value, full_output = (
-        gathered[0],
-        gathered[1],
-        gathered[2],
-        gathered[3],
-    )
-    norm_in, norm_query, norm_key, norm_attn, norm_pre, norm_post = [
-        g.astype(f32) for g in gathered[4:]
-    ]
+    width_shard = w_query.shape[0]
+    qw = w_query.shape[1]
+    kw = w_key.shape[1]
+    gain_cols = jnp.stack(
+        [
+            gain_in,
+            gain_attn,
+            gain_pre,
+            gain_post,
+            pad_rows(gain_query, width_shard),
+            pad_rows(gain_key, width_shard),
+        ],
+        axis=1,
+    )
+    gain_cols = jnp.pad(gain_cols, ((0, 0), (0, 128 - gain_cols.shape[1])))
+    packed = jnp.concatenate([w_query, w_key, w_value, w_output.T, gain_cols], axis=1)
+    packed_all = lax.all_gather(packed, "fsdp", axis=0, tiled=True)
+    o1 = qw
+    o2 = o1 + kw
+    o3 = o2 + kw
+    o4 = o3 + w_output.shape[0]
+    full_query = packed_all[:, :o1]
+    full_key = packed_all[:, o1:o2]
+    full_value = packed_all[:, o2:o3]
+    full_output_t = packed_all[:, o3:o4]
+    gains_all = packed_all[:, o4:].astype(f32)
+    head_shard = gain_query.shape[0]
+
+    def head_gain(col):
+        return col.reshape(groups, width_shard)[:, :head_shard].reshape(-1)
+
+    norm_in = gains_all[:, 0]
+    norm_attn = gains_all[:, 1]
+    norm_pre = gains_all[:, 2]
+    norm_post = gains_all[:, 3]
+    norm_query = head_gain(gains_all[:, 4])
+    norm_key = head_gain(gains_all[:, 5])
     ctx_index = lax.axis_index("ctx")
     order_flat = block_order.reshape(-1)
     my_seq = sequence_rows(order_flat, ctx_index * local, local, block)
@@ -132,10 +153,11 @@
     scale = HD ** (-0.5)
     query_rot = (rotate(query_normed, cosine[:, None, :], sine[:, None, :]) * scale).astype(low)
     key_rot = rotate(key_normed, cosine, sine).astype(low)
-    key_all, value_all = (
-        lax.all_gather(key_rot, "ctx", axis=0, tiled=True),
-        lax.all_gather(values, "ctx", axis=0, tiled=True),
-    )
+    kv_all = lax.all_gather(
+        jnp.concatenate([key_rot, values], axis=1), "ctx", axis=0, tiled=True
+    )
+    key_all = kv_all[:, :HD]
+    value_all = kv_all[:, HD:]
     scores = jnp.einsum("qhd,kd->hqk", query_rot, key_all, preferred_element_type=f32)
     allowed = my_seq[:, None] >= all_seq[None, :]
     scores = jnp.where(allowed[None], scores, -jnp.inf)
@@ -148,7 +170,7 @@
         .reshape(local, H * HD)
         .astype(low)
     )
-    branch_attn = jnp.dot(attended, full_output, preferred_element_type=f32)
+    branch_attn = jnp.einsum("tc,dc->td", attended, full_output_t, preferred_element_type=f32)
     attn_normed, attn_unit, attn_inv = norm_forward(branch_attn, norm_attn)
     residual = flat_in + attn_normed
     pre_full, pre_unit, pre_inv = norm_forward(residual, norm_pre)
@@ -189,9 +211,9 @@
     grad_residual = grad_out + grad_from_pre
     grad_branch_full, grad_gain_attn = norm_backward(grad_residual, attn_unit, attn_inv, norm_attn)
     grad_branch = grad_branch_full.astype(low)
-    term_output = jnp.einsum("tc,td->cd", attended, grad_branch, preferred_element_type=f32)
+    term_output_t = jnp.einsum("td,tc->dc", grad_branch, attended, preferred_element_type=f32)
     grad_attended = jnp.einsum(
-        "td,cd->tc", grad_branch, full_output, preferred_element_type=f32
+        "td,dc->tc", grad_branch, full_output_t, preferred_element_type=f32
     ).astype(low)
     grad_heads = grad_attended.reshape(local, H, HD)
     attended_heads = attended.reshape(local, H, HD)
@@ -225,69 +247,47 @@
     )
     grad_from_in, grad_gain_in = norm_backward(grad_normed, unit_in, inv_in, norm_in)
     in_grad = (grad_residual + grad_from_in).astype(low)
-    shards = (
-        lax.psum_scatter(
-            term_query.astype(jnp.bfloat16), "fsdp", scatter_dimension=0, tiled=True
-        ).astype(jnp.float32),
-        lax.psum_scatter(
-            term_key.astype(jnp.bfloat16), "fsdp", scatter_dimension=0, tiled=True
-        ).astype(jnp.float32),
-        lax.psum_scatter(
-            term_value.astype(jnp.bfloat16), "fsdp", scatter_dimension=0, tiled=True
-        ).astype(jnp.float32),
-        lax.psum_scatter(
-            term_output.astype(jnp.bfloat16), "fsdp", scatter_dimension=1, tiled=True
-        ).astype(jnp.float32),
-        lax.psum_scatter(
-            grad_gain_in.astype(jnp.bfloat16), "fsdp", scatter_dimension=0, tiled=True
-        ).astype(jnp.float32),
-        lax.psum_scatter(
-            grad_gain_query.astype(jnp.bfloat16), "fsdp", scatter_dimension=0, tiled=True
-        ).astype(jnp.float32),
-        lax.psum_scatter(
-            grad_gain_key.astype(jnp.bfloat16), "fsdp", scatter_dimension=0, tiled=True
-        ).astype(jnp.float32),
-        lax.psum_scatter(
-            grad_gain_attn.astype(jnp.bfloat16), "fsdp", scatter_dimension=0, tiled=True
-        ).astype(jnp.float32),
-        lax.psum_scatter(
-            grad_gain_pre.astype(jnp.bfloat16), "fsdp", scatter_dimension=0, tiled=True
-        ).astype(jnp.float32),
-        lax.psum_scatter(
-            grad_gain_post.astype(jnp.bfloat16), "fsdp", scatter_dimension=0, tiled=True
-        ).astype(jnp.float32),
-    )
-    totals = (
-        lax.psum(shards[0].astype(jnp.bfloat16), "ctx").astype(jnp.float32),
-        lax.psum(shards[1].astype(jnp.bfloat16), "ctx").astype(jnp.float32),
-        lax.psum(shards[2].astype(jnp.bfloat16), "ctx").astype(jnp.float32),
-        lax.psum(shards[3].astype(jnp.bfloat16), "ctx").astype(jnp.float32),
-        lax.psum(shard_gate.astype(jnp.bfloat16), "ctx").astype(jnp.float32),
-        lax.psum(shard_up.astype(jnp.bfloat16), "ctx").astype(jnp.float32),
-        lax.psum(shard_down.astype(jnp.bfloat16), "ctx").astype(jnp.float32),
-        lax.psum(shards[4].astype(jnp.bfloat16), "ctx").astype(jnp.float32),
-        lax.psum(shards[5].astype(jnp.bfloat16), "ctx").astype(jnp.float32),
-        lax.psum(shards[6].astype(jnp.bfloat16), "ctx").astype(jnp.float32),
-        lax.psum(shards[7].astype(jnp.bfloat16), "ctx").astype(jnp.float32),
-        lax.psum(shards[8].astype(jnp.bfloat16), "ctx").astype(jnp.float32),
-        lax.psum(shards[9].astype(jnp.bfloat16), "ctx").astype(jnp.float32),
-    )
+
+    def head_col(g):
+        return jnp.pad(g.reshape(groups, head_shard), ((0, 0), (0, width_shard - head_shard))).reshape(-1)
+
+    grad_gain_cols = jnp.stack(
+        [
+            grad_gain_in,
+            grad_gain_attn,
+            grad_gain_pre,
+            grad_gain_post,
+            head_col(grad_gain_query),
+            head_col(grad_gain_key),
+        ],
+        axis=1,
+    )
+    grad_gain_cols = jnp.pad(grad_gain_cols, ((0, 0), (0, 128 - grad_gain_cols.shape[1])))
+    grad_packed = jnp.concatenate(
+        [term_query, term_key, term_value, term_output_t, grad_gain_cols], axis=1
+    ).astype(low)
+    grad_shard = lax.psum_scatter(grad_packed, "fsdp", scatter_dimension=0, tiled=True)
+    totals = lax.psum(
+        (grad_shard, shard_gate.astype(low), shard_up.astype(low), shard_down.astype(low)), "ctx"
+    )
+    grad_shard = totals[0].astype(f32)
+    gcols = grad_shard[:, o4:]
     return (
         outputs[None],
         in_grad[None],
-        totals[0],
-        totals[1],
-        totals[2],
-        totals[3],
-        totals[4],
-        totals[5],
-        totals[6],
-        totals[7],
-        totals[8],
-        totals[9],
-        totals[10],
-        totals[11],
-        totals[12],
+        grad_shard[:, :o1],
+        grad_shard[:, o1:o2],
+        grad_shard[:, o2:o3],
+        grad_shard[:, o3:o4].T,
+        totals[1].astype(f32),
+        totals[2].astype(f32),
+        totals[3].astype(f32),
+        gcols[:, 0],
+        gcols[:head_shard, 4],
+        gcols[:head_shard, 5],
+        gcols[:, 1],
+        gcols[:, 2],
+        gcols[:, 3],
     )
 
 

time: 1100 us -> 856 us (0.78)
  blocking collectives: 238 us -> 0 us
  waiting for transfers between devices: 717 us -> 704 us
    reduce_scatter x4 -> x0, waiting for transfers between devices: 184 us -> none  [the longest x1 75.3 us: body(): lax.psum_scatter(term_query.astype(jnp.bfloat16), 'fsdp', scatter_dimensi...]
    unnamed x13 -> x10, waiting for transfers between devices: 1.56 us -> 139 us
    unnamed x2 -> x0, blocking collectives: 136 us -> none
    all_gather x4 -> x0, blocking collectives: 102 us -> none  [the longest x1 29.3 us: body(): lax.all_gather(key_rot, 'ctx', axis=0, tiled=True)]
    all_gather x2, waiting for transfers between devices: 0.02 us -> 89.9 us  [the longest x1 63.6 us: body(): packed_all = lax.all_gather(packed, 'fsdp', axis=0, tiled=True)]
    psum x2 -> x1, waiting for transfers between devices: 217 us -> 168 us  [body(): lax.psum((grad_shard, shard_gate.astype(low), shard_up.astype(low), shard...]
  transfers between devices with their start and end apart: 13 -> 9, of which waited for: 10 -> 9; matrix products, arithmetic and copies ran while one was open for 6% -> 5% of each run, Pallas kernels for 0% -> 0%
where the time goes in v1:
time: 856 us; the launch traced here: 854 us
  waiting for transfers between devices  704 us (82%)
  matrix products  78.1 us (9%)
  local copies, waits for them, and re-layouts  30 us (4%)
  other arithmetic  25.5 us (3%)
  between operations  15.5 us (2%)
    psum x1, waiting for transfers between devices, body(): lax.psum((grad_shard, shard_gate.astype(low), shard_up.astype(low), shard...  168 us
    unnamed x10, waiting for transfers between devices  139 us
    reduce_scatter x1, waiting for transfers between devices, body(): lax.psum_scatter((jnp.dot(grad_gate, w_gate, preferred_element_type=f32)...  81.6 us
    reduce_scatter x1, waiting for transfers between devices, body(): lax.psum_scatter(jnp.dot(hidden, w_down, preferred_element_type=f32).asty...  81.4 us
    all_gather x1, waiting for transfers between devices, body(): packed_all = lax.all_gather(packed, 'fsdp', axis=0, tiled=True)  63.6 us
    all_gather x1, waiting for transfers between devices, body(): rows_all = lax.all_gather(normed_pre, 'fsdp', axis=0, tiled=True)  57.8 us
    all_gather x1, waiting for transfers between devices, body(): grad_all = lax.all_gather(grad_ffn, 'fsdp', axis=0, tiled=True)  56.5 us
    reduce_scatter x1, waiting for transfers between devices, body(): lax.psum_scatter(key_value_terms.astype(jnp.bfloat16), 'ctx', scatter_dim...  30.1 us
  transfers between devices with their start and end apart: 9, of which 9 were waited for; matrix products, arithmetic and copies ran while one was open for 5% of the time, Pallas kernels for 0%

profile of v1, /device:TPU:0, one launch (start us, length us, event | category | flops | bytes accessed | tf_op | source)
XLA Modules:
  0.0 854.2 jit_solution(1116612158823631737)
XLA Ops:
  16.0 63.6 %all-gather.5.cloned.1.call-done = bf16[1152,2688]{1,0:T(8,128)(2,1)} async-done(((bf16[72,2688]{1,0:T(8,128)(2,1)}), bf16[1152,2688]{1,0:T(8,128)(2,1)}) %all-gather.5.cloned.1.call-update) | async-done | bytes 6193168 | tf_op jit(solution)/shard_map/all_gather | solution.py:119
  87.6 3.3 slice_bitcast_fusion
  90.9 4.4 copy.93
  95.3 2.6 multiply_reduce_fusion.7
  98.2 26.3 %all-gather.7.cloned.1.call-done = bf16[1024,512]{1,0:T(8,128)(2,1)} async-done(((bf16[128,512]{1,0:T(8,128)(2,1)}), bf16[1024,512]{1,0:T(8,128)(2,1)}) %all-gather.7.cloned.1.call-update) | async-done | bytes 1048592 | tf_op jit(solution)/shard_map/all_gather | solution.py:156
  127.5 2.7 multiply_reduce_fusion.3
  131.6 57.8 %all-gather.9.cloned.1.call-done = bf16[2048,1152]{1,0:T(8,128)(2,1)} async-done(((bf16[128,1152]{1,0:T(8,128)(2,1)}), bf16[2048,1152]{1,0:T(8,128)(2,1)}) %all-gather.9.cloned.1.call-update) | async-done | bytes 4718608 | tf_op jit(solution)/shard_map/all_gather | solution.py:178
  189.5 5.2 fusion.115
  194.8 4.7 multiply_convert_fusion.1
  200.7 4.5 convolution_convert_fusion
  205.3 81.4 %reduce-scatter.5.cloned.1.call-done = bf16[128,1152]{1,0:T(8,128)(2,1)} async-done(((bf16[2048,1152]{1,0:T(8,128)(2,1)}), bf16[128,1152]{1,0:T(8,128)(2,1)}) %reduce-scatter.5.cloned.1.call-update) | async-done | bytes 294928 | tf_op jit(solution)/shard_map/reduce_scatter | solution.py:183
  289.7 1.9 fusion.41
  292.0 56.5 %all-gather.11.cloned.1.call-done = bf16[2048,1152]{1,0:T(8,128)(2,1)} async-done(((bf16[128,1152]{1,0:T(8,128)(2,1)}), bf16[2048,1152]{1,0:T(8,128)(2,1)}) %all-gather.11.cloned.1.call-update) | async-done | bytes 4718608 | tf_op jit(solution)/shard_map/all_gather | solution.py:194
  348.4 8.5 multiply_convert_fusion
  357.0 3.0 fusion.116
  360.0 4.6 add_convert_fusion
  364.7 81.6 %reduce-scatter.7.cloned.1.call-done = bf16[128,1152]{1,0:T(8,128)(2,1)} async-done(((bf16[2048,1152]{1,0:T(8,128)(2,1)}), bf16[128,1152]{1,0:T(8,128)(2,1)}) %reduce-scatter.7.cloned.1.call-update) | async-done | bytes 294928 | tf_op jit(solution)/shard_map/reduce_scatter | solution.py:201
  447.6 2.1 multiply_reduce_fusion
  450.0 2.2 fusion.24
  452.5 2.3 fusion.22
  454.8 2.2 fusion.12
  462.4 2.3 fusion.1
  464.7 2.6 fusion.17
  467.3 30.1 %reduce-scatter.9.cloned.1.call-done = bf16[128,512]{1,0:T(8,128)(2,1)} async-done(((bf16[1024,512]{1,0:T(8,128)(2,1)}), bf16[128,512]{1,0:T(8,128)(2,1)}) %reduce-scatter.9.cloned.1.call-update) | async-done | bytes 131088 | tf_op jit(solution)/shard_map/reduce_scatter | solution.py:229
  504.7 2.2 fusion
  509.4 6.4 convolution_convert_fusion.3
  515.8 5.9 convolution_convert_fusion.4
  521.7 3.4 convolution_convert_fusion.5
  525.1 138.4 %all-reduce.11.cloned.1.call-done = bf16[1152,2688]{0,1:T(8,128)(2,1)} async-done(((bf16[1152,2688]{0,1:T(8,128)(2,1)}), bf16[1152,2688]{0,1:T(8,128)(2,1)}) %all-reduce.11.cloned.1.call-update) | async-done | bytes 6193168
  663.5 2.5 constant_dynamic-slice_fusion
  666.9 167.8 %all-reduce.13.cloned.1.call-done = (bf16[72,2688]{0,1:T(8,128)(2,1)}, bf16[432,1152]{1,0:T(8,128)(2,1)}, bf16[432,1152]{1,0:T(8,128)(2,1)}, bf16[432,1152]{1,0:T(8,128)(2,1)}) async-done(((bf16[72,2688]{0,1:T(8,128)(2,1)}, bf16[432,1152]{1,0:T(8,128)(2,1)}, bf16[432,1152]{1,0:T(8,128)(2,1)}, bf16[432,1152]{1,0:T(8,128)(2,1)}), (bf16[72,2688]{0,1:T(8,128)(2,1)}, bf16[432,1152]{1,0:T(8,128)(2,1)}, ...) | async-done | bytes 3373072 | tf_op jit(solution)/shard_map/psum | solution.py:270
  842.2 2.7 convert_element_type.194
  (241 shorter events, 52.8 us)
Async XLA Ops:
  7.2 193.5 %copy-start = (bf16[432,1152]{1,0:T(8,128)(2,1)S(1)}, bf16[432,1152]{1,0:T(8,128)(2,1)}, u32[]{:S(2)}) copy-start(bf16[432,1152]{1,0:T(8,128)(2,1)} %param.27) | copy-start | bytes 2985988
  7.2 75.4 %copy-start.2 = (bf16[1,128,1152]{2,1,0:T(8,128)(2,1)S(1)}, bf16[1,128,1152]{2,1,0:T(8,128)(2,1)}, u32[]{:S(2)}) copy-start(bf16[1,128,1152]{2,1,0:T(8,128)(2,1)} %param.17) | copy-start | bytes 884740
  7.2 72.4 %all-gather.5.cloned.1.call-start = ((), (), s32[]{:S(2)}) async-start(), calls=%async_computation.3 | async-start | bytes 6580224 | tf_op jit(solution)/shard_map/all_gather | solution.py:119
  13.1 111.4 %all-gather.7.cloned.1.call-start = ((), (), s32[]{:S(2)}) async-start(), calls=%async_computation.4 | async-start | bytes 1179648 | tf_op jit(solution)/shard_map/all_gather | solution.py:156
  14.0 70.7 %copy-start.40 = (f32[128]{0:T(128)}, f32[128]{0:T(128)S(1)}, u32[]{:S(2)}) copy-start(f32[128]{0:T(128)S(1)} %multiply_power_fusion) | copy-start | bytes 1540
  16.0 68.8 %copy-start.42 = (f32[128]{0:T(128)}, f32[128]{0:T(128)S(1)}, u32[]{:S(2)}) copy-start(f32[128]{0:T(128)S(1)} %convert_bitcast_fusion.1) | copy-start | bytes 1540
  16.0 79.3 %copy-start.30 = (f32[128]{0:T(128)}, f32[128]{0:T(128)S(1)}, u32[]{:S(2)}) copy-start(f32[128]{0:T(128)S(1)} %add_rsqrt_fusion.5) | copy-start | bytes 1540
  82.4 47.9 %copy-start.20 = (f32[1152]{0:T(1024)}, f32[1152]{0:T(1024)S(1)}, u32[]{:S(2)}) copy-start(f32[1152]{0:T(1024)S(1)} %get-tuple-element.87) | copy-start | bytes 13828
  82.4 48.2 %copy-start.23 = (f32[1152]{0:T(1024)}, f32[1152]{0:T(1024)S(1)}, u32[]{:S(2)}) copy-start(f32[1152]{0:T(1024)S(1)} %get-tuple-element.86) | copy-start | bytes 13828
  87.1 102.4 %all-gather.9.cloned.1.call-start = ((), (), s32[]{:S(2)}) async-start(), calls=%async_computation.5 | async-start | bytes 5013504 | tf_op jit(solution)/shard_map/all_gather | solution.py:178
  87.4 39.2 %copy-start.11 = (pred[128,1024]{0,1:T(8,128)(4,1)}, pred[128,1024]{0,1:T(8,128)(4,1)S(1)}, u32[]{:S(2)}) copy-start(pred[128,1024]{0,1:T(8,128)(4,1)S(1)} %broadcast_compare_fusion) | copy-start | bytes 393220
  98.2 29.0 %copy-start.14 = (f32[128,4,128]{2,0,1:T(8,128)}, f32[128,4,128]{2,0,1:T(8,128)S(1)}, u32[]{:S(2)}) copy-start(f32[128,4,128]{2,0,1:T(8,128)S(1)} %get-tuple-element.112) | copy-start | bytes 786436
  130.2 64.5 %copy-start.34 = (f32[128]{0:T(128)}, f32[128]{0:T(128)S(1)}, u32[]{:S(2)}) copy-start(f32[128]{0:T(128)S(1)} %add_rsqrt_fusion.3) | copy-start | bytes 1540
  130.5 64.2 %copy-start.36 = (f32[128]{0:T(128)}, f32[128]{0:T(128)S(1)}, u32[]{:S(2)}) copy-start(f32[128]{0:T(128)S(1)} %add_rsqrt_fusion.2) | copy-start | bytes 1540
  131.4 155.4 %reduce-scatter.5.cloned.1.call-start = ((), (), s32[]{:S(2)}) async-start(), calls=%async_computation.6 | async-start | bytes 5013504 | tf_op jit(solution)/shard_map/reduce_scatter | solution.py:183
  205.3 82.6 %copy-start.4 = (bf16[1,128,1152]{2,1,0:T(8,128)(2,1)S(1)}, bf16[1,128,1152]{2,1,0:T(8,128)(2,1)}, u32[]{:S(2)}) copy-start(bf16[1,128,1152]{2,1,0:T(8,128)(2,1)} %param.18) | copy-start | bytes 884740
  205.3 143.2 %all-gather.11.cloned.1.call-start = ((), (), s32[]{:S(2)}) async-start(), calls=%async_computation.7 | async-start | bytes 5013504 | tf_op jit(solution)/shard_map/all_gather | solution.py:194
  291.7 154.6 %reduce-scatter.7.cloned.1.call-start = ((), (), s32[]{:S(2)}) async-start(), calls=%async_computation.8 | async-start | bytes 5013504 | tf_op jit(solution)/shard_map/reduce_scatter | solution.py:201
  364.6 81.7 %copy-start.24 = (f32[1152]{0:T(1024)S(1)}, f32[1152]{0:T(1024)}, u32[]{:S(2)}) copy-start(f32[1152]{0:T(1024)} %copy-done.23) | copy-start | bytes 13828
  364.6 81.7 %copy-start.37 = (f32[128]{0:T(128)S(1)}, f32[128]{0:T(128)}, u32[]{:S(2)}) copy-start(f32[128]{0:T(128)} %copy-done.36) | copy-start | bytes 1540
  364.6 83.0 %copy-start.3 = (bf16[128,1152]{1,0:T(8,128)(2,1)S(1)}, bf16[128,1152]{1,0:T(8,128)(2,1)}, u32[]{:S(2)}) copy-start(bf16[128,1152]{1,0:T(8,128)(2,1)} %reduce-scatter.5.cloned.1.call-done) | copy-start | bytes 884740
  364.6 83.0 %copy-start.21 = (f32[1152]{0:T(1024)S(1)}, f32[1152]{0:T(1024)}, u32[]{:S(2)}) copy-start(f32[1152]{0:T(1024)} %copy-done.20) | copy-start | bytes 13828
  364.6 83.0 %copy-start.22 = (f32[1152]{0:T(1024)S(1)}, f32[1152]{0:T(1024)}, u32[]{:S(2)}) copy-start(f32[1152]{0:T(1024)} %get-tuple-element.85) | copy-start | bytes 13828
  364.6 83.0 %copy-start.35 = (f32[128]{0:T(128)S(1)}, f32[128]{0:T(128)}, u32[]{:S(2)}) copy-start(f32[128]{0:T(128)} %copy-done.34) | copy-start | bytes 1540
  364.6 83.0 %copy-start.39 = (f32[128]{0:T(128)S(1)}, f32[128]{0:T(128)}, u32[]{:S(2)}) copy-start(f32[128]{0:T(128)} %copy-done.38) | copy-start | bytes 1540
  364.7 132.8 %reduce-scatter.9.cloned.1.call-start = ((), (), s32[]{:S(2)}) async-start(), calls=%async_computation.9 | async-start | bytes 1179648 | tf_op jit(solution)/shard_map/reduce_scatter | solution.py:229
  459.1 204.4 %all-reduce.11.cloned.1.call-start = ((), (), s32[]{:S(2)}) async-start(), calls=%async_computation.10 | async-start | bytes 12386304
  462.4 36.0 %copy-start.41 = (f32[128]{0:T(128)S(1)}, f32[128]{0:T(128)}, u32[]{:S(2)}) copy-start(f32[128]{0:T(128)} %copy-done.40) | copy-start | bytes 1540
  462.4 36.0 %copy-start.43 = (f32[128]{0:T(128)S(1)}, f32[128]{0:T(128)}, u32[]{:S(2)}) copy-start(f32[128]{0:T(128)} %copy-done.42) | copy-start | bytes 1540
  462.4 36.3 %copy-start.26 = (f32[256]{0:T(256)S(1)}, f32[256]{0:T(256)}, u32[]{:S(2)}) copy-start(f32[256]{0:T(256)} %copy-done.25) | copy-start | bytes 3076
  462.4 36.3 %copy-start.33 = (f32[128]{0:T(128)S(1)}, f32[128]{0:T(128)}, u32[]{:S(2)}) copy-start(f32[128]{0:T(128)} %copy-done.32) | copy-start | bytes 1540
  507.7 327.0 %all-reduce.13.cloned.1.call-start = ((), (), s32[]{:S(2)}) async-start(), calls=%async_computation.11 | async-start | bytes 7348224 | tf_op jit(solution)/shard_map/psum | solution.py:270
  (39 other events, 188.7 us)
Sparse Core Ops, SparseCore 0:
  13.2 66.3 all-gather.4
  87.2 37.2 all-gather.6
  131.5 57.9 all-gather.8
  205.4 81.3 reduce-scatter.4
  291.8 56.5 all-gather.10
  364.8 81.4 reduce-scatter.6
  459.2 38.1 reduce-scatter.8
  507.9 155.5 all-reduce.10
  667.4 167.2 all-reduce.12

commit v2 on v1

--- a/solution.py
+++ b/solution.py
@@ -211,7 +211,7 @@
     grad_residual = grad_out + grad_from_pre
     grad_branch_full, grad_gain_attn = norm_backward(grad_residual, attn_unit, attn_inv, norm_attn)
     grad_branch = grad_branch_full.astype(low)
-    term_output_t = jnp.einsum("td,tc->dc", grad_branch, attended, preferred_element_type=f32)
+    term_output = jnp.einsum("tc,td->cd", attended, grad_branch, preferred_element_type=f32)
     grad_attended = jnp.einsum(
         "td,dc->tc", grad_branch, full_output_t, preferred_element_type=f32
     ).astype(low)
@@ -237,9 +237,9 @@
     grad_k_full, grad_gain_key = norm_backward(grad_k_normed, key_unit, key_inv, norm_key)
     grad_q_in = grad_q_full.reshape(local, H * HD).astype(low)
     grad_k_in = grad_k_full.astype(low)
-    term_query = jnp.einsum("td,tc->dc", normed_in, grad_q_in, preferred_element_type=f32)
-    term_key = jnp.einsum("td,tc->dc", normed_in, grad_k_in, preferred_element_type=f32)
-    term_value = jnp.einsum("td,tc->dc", normed_in, grad_values, preferred_element_type=f32)
+    term_query = jnp.einsum("tc,td->cd", grad_q_in, normed_in, preferred_element_type=f32)
+    term_key = jnp.einsum("tc,td->cd", grad_k_in, normed_in, preferred_element_type=f32)
+    term_value = jnp.einsum("tc,td->cd", grad_values, normed_in, preferred_element_type=f32)
     grad_normed = (
         jnp.einsum("tc,dc->td", grad_q_in, full_query, preferred_element_type=f32)
         + jnp.einsum("tc,dc->td", grad_k_in, full_key, preferred_element_type=f32)
@@ -251,7 +251,7 @@
     def head_col(g):
         return jnp.pad(g.reshape(groups, head_shard), ((0, 0), (0, width_shard - head_shard))).reshape(-1)
 
-    grad_gain_cols = jnp.stack(
+    grad_gain_rows = jnp.stack(
         [
             grad_gain_in,
             grad_gain_attn,
@@ -262,32 +262,36 @@
         ],
         axis=1,
     )
-    grad_gain_cols = jnp.pad(grad_gain_cols, ((0, 0), (0, 128 - grad_gain_cols.shape[1])))
-    grad_packed = jnp.concatenate(
-        [term_query, term_key, term_value, term_output_t, grad_gain_cols], axis=1
-    ).astype(low)
-    grad_shard = lax.psum_scatter(grad_packed, "fsdp", scatter_dimension=0, tiled=True)
+    grad_gain_rows = jnp.pad(grad_gain_rows, ((0, 0), (0, 8 - grad_gain_rows.shape[1]))).T
+    grad_packed = jnp.concatenate([term_query, term_key, term_value, term_output], axis=0).astype(low)
+    grad_shard = jnp.concatenate(
+        [
+            lax.psum_scatter(grad_packed, "fsdp", scatter_dimension=1, tiled=True),
+            lax.psum_scatter(grad_gain_rows.astype(low), "fsdp", scatter_dimension=1, tiled=True),
+        ],
+        axis=0,
+    )
     totals = lax.psum(
         (grad_shard, shard_gate.astype(low), shard_up.astype(low), shard_down.astype(low)), "ctx"
     )
     grad_shard = totals[0].astype(f32)
-    gcols = grad_shard[:, o4:]
+    grows = grad_shard[o4:]
     return (
         outputs[None],
         in_grad[None],
-        grad_shard[:, :o1],
-        grad_shard[:, o1:o2],
-        grad_shard[:, o2:o3],
-        grad_shard[:, o3:o4].T,
+        grad_shard[:o1].T,
+        grad_shard[o1:o2].T,
+        grad_shard[o2:o3].T,
+        grad_shard[o3:o4],
         totals[1].astype(f32),
         totals[2].astype(f32),
         totals[3].astype(f32),
-        gcols[:, 0],
-        gcols[:head_shard, 4],
-        gcols[:head_shard, 5],
-        gcols[:, 1],
-        gcols[:, 2],
-        gcols[:, 3],
+        grows[0],
+        grows[4, :head_shard],
+        grows[5, :head_shard],
+        grows[1],
+        grows[2],
+        grows[3],
     )
 
 

time: 856 us -> 790 us (0.923)
  waiting for transfers between devices: 704 us -> 562 us
  blocking collectives: 0 us -> 65.5 us
    unnamed x10, waiting for transfers between devices: 139 us -> 0.15 us
    unnamed x0 -> x1, blocking collectives: none -> 65.5 us
    unnamed x136 -> x144, local copies, waits for them, and re-layouts: 14.1 us -> 21.9 us
  transfers between devices with their start and end apart: 9 -> 9, of which waited for: 9 -> 8; matrix products, arithmetic and copies ran while one was open for 5% -> 5% of each run, Pallas kernels for 0% -> 0%
where the time goes in v2:
time: 790 us; the launch traced here: 787 us
  waiting for transfers between devices  562 us (71%)
  matrix products  75.1 us (10%)
  blocking collectives  65.5 us (8%)
  local copies, waits for them, and re-layouts  36.2 us (5%)
  other arithmetic  32.3 us (4%)
  between operations  15.6 us (2%)
    psum x1, waiting for transfers between devices, body(): lax.psum((grad_shard, shard_gate.astype(low), shard_up.astype(low), shard...  164 us
    reduce_scatter x1, waiting for transfers between devices, body(): lax.psum_scatter(jnp.dot(hidden, w_down, preferred_element_type=f32).asty...  81.6 us
    reduce_scatter x1, waiting for transfers between devices, body(): lax.psum_scatter((jnp.dot(grad_gate, w_gate, preferred_element_type=f32)...  81.6 us
    unnamed x1, blocking collectives  65.5 us
    all_gather x1, waiting for transfers between devices, body(): packed_all = lax.all_gather(packed, 'fsdp', axis=0, tiled=True)  63.6 us
    all_gather x1, waiting for transfers between devices, body(): rows_all = lax.all_gather(normed_pre, 'fsdp', axis=0, tiled=True)  57.6 us
    all_gather x1, waiting for transfers between devices, body(): grad_all = lax.all_gather(grad_ffn, 'fsdp', axis=0, tiled=True)  56.5 us
    reduce_scatter x1, waiting for transfers between devices, body(): lax.psum_scatter(key_value_terms.astype(jnp.bfloat16), 'ctx', scatter_dim...  30.8 us
  transfers between devices with their start and end apart: 9, of which 8 were waited for; matrix products, arithmetic and copies ran while one was open for 5% of the time, Pallas kernels for 0%

profile of v2, /device:TPU:0, one launch (start us, length us, event | category | flops | bytes accessed | tf_op | source)
XLA Modules:
  0.0 787.5 jit_solution(4538969616345073679)
XLA Ops:
  16.0 63.6 %all-gather.5.cloned.1.call-done = bf16[1152,2688]{1,0:T(8,128)(2,1)} async-done(((bf16[72,2688]{1,0:T(8,128)(2,1)}), bf16[1152,2688]{1,0:T(8,128)(2,1)}) %all-gather.5.cloned.1.call-update) | async-done | bytes 6193168 | tf_op jit(solution)/shard_map/all_gather | solution.py:119
  87.0 3.3 slice_bitcast_fusion
  90.3 4.3 copy.93
  94.7 2.6 multiply_reduce_fusion.7
  97.6 26.3 %all-gather.7.cloned.1.call-done = bf16[1024,512]{1,0:T(8,128)(2,1)} async-done(((bf16[128,512]{1,0:T(8,128)(2,1)}), bf16[1024,512]{1,0:T(8,128)(2,1)}) %all-gather.7.cloned.1.call-update) | async-done | bytes 1048592 | tf_op jit(solution)/shard_map/all_gather | solution.py:156
  126.9 2.7 multiply_reduce_fusion.3
  131.1 57.6 %all-gather.9.cloned.1.call-done = bf16[2048,1152]{1,0:T(8,128)(2,1)} async-done(((bf16[128,1152]{1,0:T(8,128)(2,1)}), bf16[2048,1152]{1,0:T(8,128)(2,1)}) %all-gather.9.cloned.1.call-update) | async-done | bytes 4718608 | tf_op jit(solution)/shard_map/all_gather | solution.py:178
  188.6 5.2 fusion.110
  194.0 4.7 multiply_convert_fusion.1
  199.9 4.5 convolution_convert_fusion
  204.5 81.6 %reduce-scatter.8.cloned.1.call-done = bf16[128,1152]{1,0:T(8,128)(2,1)} async-done(((bf16[2048,1152]{1,0:T(8,128)(2,1)}), bf16[128,1152]{1,0:T(8,128)(2,1)}) %reduce-scatter.8.cloned.1.call-update) | async-done | bytes 294928 | tf_op jit(solution)/shard_map/reduce_scatter | solution.py:183
  291.3 56.5 %all-gather.11.cloned.1.call-done = bf16[2048,1152]{1,0:T(8,128)(2,1)} async-done(((bf16[128,1152]{1,0:T(8,128)(2,1)}), bf16[2048,1152]{1,0:T(8,128)(2,1)}) %all-gather.11.cloned.1.call-update) | async-done | bytes 4718608 | tf_op jit(solution)/shard_map/all_gather | solution.py:194
  347.8 8.5 %multiply_convert_fusion = (bf16[2048,432]{0,1:T(8,128)(2,1)S(1)}, bf16[2048,432]{0,1:T(8,128)(2,1)S(1)}) fusion(f32[2048,432]{0,1:T(8,128)} %copy-done.61, f32[2048,432]{0,1:T(8,128)} %get-tuple-element.132, bf16[2048,1152]{1,0:T(8,128)(2,1)} %all-gather.11.cloned.1.call-done, bf16[432,1152]{1,0:T(8,128)(2,1)S(1)} %copy-done), kind=kOutput, calls=%fused_computation.14 | convolution fusion | flops 2058780672 | bytes 16330752 | tf_op jit(solution)/shard_map/td,fd->tf/dot_general | solution.py:195
  356.4 3.0 fusion.111
  359.4 4.6 add_convert_fusion
  364.0 81.6 %reduce-scatter.10.cloned.1.call-done = bf16[128,1152]{1,0:T(8,128)(2,1)} async-done(((bf16[2048,1152]{1,0:T(8,128)(2,1)}), bf16[128,1152]{1,0:T(8,128)(2,1)}) %reduce-scatter.10.cloned.1.call-update) | async-done | bytes 294928 | tf_op jit(solution)/shard_map/reduce_scatter | solution.py:201
  447.5 2.7 multiply_reduce_fusion
  450.4 2.2 fusion.20
  453.0 2.2 fusion.18
  455.3 2.2 fusion.8
  462.7 2.2 convolution_convert_fusion.1
  464.8 2.3 convolution_convert_fusion.2
  467.1 30.8 %reduce-scatter.12.cloned.1.call-done = bf16[128,512]{1,0:T(8,128)(2,1)} async-done(((bf16[1024,512]{1,0:T(8,128)(2,1)}), bf16[128,512]{1,0:T(8,128)(2,1)}) %reduce-scatter.12.cloned.1.call-update) | async-done | bytes 131088 | tf_op jit(solution)/shard_map/reduce_scatter | solution.py:229
  501.3 4.6 pad_maximum_fusion
  505.9 8.9 %copy.126 = bf16[2560,1152]{0,1:T(8,128)(2,1)} copy(bf16[2560,1152]{1,0:T(8,128)(2,1)} %pad_maximum_fusion) | data formatting | bytes 11796480
  516.8 6.4 convolution_convert_fusion.3
  523.2 3.4 convolution_convert_fusion.4
  526.6 3.4 convolution_convert_fusion.5
  530.3 2.7 fusion.13
  536.4 65.5 %all-reduce.6 = bf16[8,1152]{1,0:T(8,128)(2,1)S(1)} all-reduce(bf16[8,1152]{1,0:T(8,128)(2,1)S(1)} %pad_bitcast_fusion), channel_id=6, replica_groups=mesh['ctx'=8,'fsdp'=16] {'fsdp'}, use_global_device_ids=true, to_apply=%region_27.28.clone | all-reduce | flops 9216 | bytes 36864
  605.3 163.6 %all-reduce.10.cloned.1.call-done = (bf16[2568,72]{1,0:T(8,128)(2,1)}, bf16[432,1152]{1,0:T(8,128)(2,1)}, bf16[432,1152]{1,0:T(8,128)(2,1)}, bf16[432,1152]{1,0:T(8,128)(2,1)}) async-done(((bf16[2568,72]{1,0:T(8,128)(2,1)}, bf16[432,1152]{1,0:T(8,128)(2,1)}, bf16[432,1152]{1,0:T(8,128)(2,1)}, bf16[432,1152]{1,0:T(8,128)(2,1)}), (bf16[2568,72]{1,0:T(8,128)(2,1)}, bf16[432,1152]{1,0:T(8,128)(2,1)}, ...) | async-done | bytes 3355792 | tf_op jit(solution)/shard_map/psum | solution.py:274
  775.4 2.7 convert_element_type.199
  (252 shorter events, 55.1 us)
Async XLA Ops:
  7.2 192.7 %copy-start = (bf16[432,1152]{1,0:T(8,128)(2,1)S(1)}, bf16[432,1152]{1,0:T(8,128)(2,1)}, u32[]{:S(2)}) copy-start(bf16[432,1152]{1,0:T(8,128)(2,1)} %param.27) | copy-start | bytes 2985988
  7.2 75.4 %copy-start.2 = (bf16[1,128,1152]{2,1,0:T(8,128)(2,1)S(1)}, bf16[1,128,1152]{2,1,0:T(8,128)(2,1)}, u32[]{:S(2)}) copy-start(bf16[1,128,1152]{2,1,0:T(8,128)(2,1)} %param.17) | copy-start | bytes 884740
  7.2 72.4 %all-gather.5.cloned.1.call-start = ((), (), s32[]{:S(2)}) async-start(), calls=%async_computation.4 | async-start | bytes 6580224 | tf_op jit(solution)/shard_map/all_gather | solution.py:119
  13.1 110.8 %all-gather.7.cloned.1.call-start = ((), (), s32[]{:S(2)}) async-start(), calls=%async_computation.5 | async-start | bytes 1179648 | tf_op jit(solution)/shard_map/all_gather | solution.py:156
  14.0 70.2 %copy-start.43 = (f32[128]{0:T(128)}, f32[128]{0:T(128)S(1)}, u32[]{:S(2)}) copy-start(f32[128]{0:T(128)S(1)} %multiply_power_fusion) | copy-start | bytes 1540
  16.0 68.2 %copy-start.45 = (f32[128]{0:T(128)}, f32[128]{0:T(128)S(1)}, u32[]{:S(2)}) copy-start(f32[128]{0:T(128)S(1)} %convert_bitcast_fusion.1) | copy-start | bytes 1540
  16.0 78.7 %copy-start.26 = (f32[128]{0:T(128)}, f32[128]{0:T(128)S(1)}, u32[]{:S(2)}) copy-start(f32[128]{0:T(128)S(1)} %add_rsqrt_fusion.5) | copy-start | bytes 1540
  82.4 47.3 %copy-start.21 = (f32[1152]{0:T(1024)}, f32[1152]{0:T(1024)S(1)}, u32[]{:S(2)}) copy-start(f32[1152]{0:T(1024)S(1)} %get-tuple-element.87) | copy-start | bytes 13828
  82.4 47.6 %copy-start.24 = (f32[1152]{0:T(1024)}, f32[1152]{0:T(1024)S(1)}, u32[]{:S(2)}) copy-start(f32[1152]{0:T(1024)S(1)} %get-tuple-element.86) | copy-start | bytes 13828
  86.6 102.1 %all-gather.9.cloned.1.call-start = ((), (), s32[]{:S(2)}) async-start(), calls=%async_computation.6 | async-start | bytes 5013504 | tf_op jit(solution)/shard_map/all_gather | solution.py:178
  86.8 39.1 %copy-start.12 = (pred[128,1024]{0,1:T(8,128)(4,1)}, pred[128,1024]{0,1:T(8,128)(4,1)S(1)}, u32[]{:S(2)}) copy-start(pred[128,1024]{0,1:T(8,128)(4,1)S(1)} %broadcast_compare_fusion) | copy-start | bytes 393220
  126.9 67.0 %copy-start.7 = (bf16[256,4,128]{2,0,1:T(8,128)(2,1)}, bf16[256,4,128]{2,0,1:T(8,128)(2,1)S(1)}, u32[]{:S(2)}) copy-start(bf16[256,4,128]{2,0,1:T(8,128)(2,1)S(1)} %convolution_convert_fusion.8) | copy-start | bytes 786436
  129.6 64.3 %copy-start.37 = (f32[128]{0:T(128)}, f32[128]{0:T(128)S(1)}, u32[]{:S(2)}) copy-start(f32[128]{0:T(128)S(1)} %add_rsqrt_fusion.3) | copy-start | bytes 1540
  129.9 64.0 %copy-start.39 = (f32[128]{0:T(128)}, f32[128]{0:T(128)S(1)}, u32[]{:S(2)}) copy-start(f32[128]{0:T(128)S(1)} %add_rsqrt_fusion.2) | copy-start | bytes 1540
  130.8 155.3 %reduce-scatter.8.cloned.1.call-start = ((), (), s32[]{:S(2)}) async-start(), calls=%async_computation.7 | async-start | bytes 5013504 | tf_op jit(solution)/shard_map/reduce_scatter | solution.py:183
  204.4 82.8 %copy-start.5 = (bf16[1,128,1152]{2,1,0:T(8,128)(2,1)S(1)}, bf16[1,128,1152]{2,1,0:T(8,128)(2,1)}, u32[]{:S(2)}) copy-start(bf16[1,128,1152]{2,1,0:T(8,128)(2,1)} %param.18) | copy-start | bytes 884740
  204.4 143.3 %all-gather.11.cloned.1.call-start = ((), (), s32[]{:S(2)}) async-start(), calls=%async_computation.8 | async-start | bytes 5013504 | tf_op jit(solution)/shard_map/all_gather | solution.py:194
  291.0 154.6 %reduce-scatter.10.cloned.1.call-start = ((), (), s32[]{:S(2)}) async-start(), calls=%async_computation.9 | async-start | bytes 5013504 | tf_op jit(solution)/shard_map/reduce_scatter | solution.py:201
  363.9 81.7 %copy-start.25 = (f32[1152]{0:T(1024)S(1)}, f32[1152]{0:T(1024)}, u32[]{:S(2)}) copy-start(f32[1152]{0:T(1024)} %copy-done.24) | copy-start | bytes 13828
  363.9 81.7 %copy-start.40 = (f32[128]{0:T(128)S(1)}, f32[128]{0:T(128)}, u32[]{:S(2)}) copy-start(f32[128]{0:T(128)} %copy-done.39) | copy-start | bytes 1540
  363.9 83.6 %copy-start.4 = (bf16[128,1152]{1,0:T(8,128)(2,1)S(1)}, bf16[128,1152]{1,0:T(8,128)(2,1)}, u32[]{:S(2)}) copy-start(bf16[128,1152]{1,0:T(8,128)(2,1)} %reduce-scatter.8.cloned.1.call-done) | copy-start | bytes 884740
  363.9 83.6 %copy-start.22 = (f32[1152]{0:T(1024)S(1)}, f32[1152]{0:T(1024)}, u32[]{:S(2)}) copy-start(f32[1152]{0:T(1024)} %copy-done.21) | copy-start | bytes 13828
  363.9 83.6 %copy-start.23 = (f32[1152]{0:T(1024)S(1)}, f32[1152]{0:T(1024)}, u32[]{:S(2)}) copy-start(f32[1152]{0:T(1024)} %get-tuple-element.85) | copy-start | bytes 13828
  363.9 83.6 %copy-start.38 = (f32[128]{0:T(128)S(1)}, f32[128]{0:T(128)}, u32[]{:S(2)}) copy-start(f32[128]{0:T(128)} %copy-done.37) | copy-start | bytes 1540
  364.0 83.5 %copy-start.42 = (f32[128]{0:T(128)S(1)}, f32[128]{0:T(128)}, u32[]{:S(2)}) copy-start(f32[128]{0:T(128)} %copy-done.41) | copy-start | bytes 1540
  364.0 133.9 %reduce-scatter.12.cloned.1.call-start = ((), (), s32[]{:S(2)}) async-start(), calls=%async_computation.10 | async-start | bytes 1179648 | tf_op jit(solution)/shard_map/reduce_scatter | solution.py:229
  459.6 142.5 %reduce-scatter.14.cloned.1.call-start = ((), (), s32[]{:S(2)}) async-start(), calls=%async_computation.11 | async-start | bytes 6266880
  462.4 36.5 %copy-start.44 = (f32[128]{0:T(128)S(1)}, f32[128]{0:T(128)}, u32[]{:S(2)}) copy-start(f32[128]{0:T(128)} %copy-done.43) | copy-start | bytes 1540
  462.4 36.5 %copy-start.46 = (f32[128]{0:T(128)S(1)}, f32[128]{0:T(128)}, u32[]{:S(2)}) copy-start(f32[128]{0:T(128)} %copy-done.45) | copy-start | bytes 1540
  462.5 36.9 %copy-start.29 = (f32[256]{0:T(256)S(1)}, f32[256]{0:T(256)}, u32[]{:S(2)}) copy-start(f32[256]{0:T(256)} %copy-done.28) | copy-start | bytes 3076
  462.5 36.9 %copy-start.36 = (f32[128]{0:T(128)S(1)}, f32[128]{0:T(128)}, u32[]{:S(2)}) copy-start(f32[128]{0:T(128)} %copy-done.35) | copy-start | bytes 1540
  514.8 254.1 %all-reduce.10.cloned.1.call-start = ((), (), s32[]{:S(2)}) async-start(), calls=%async_computation.12 | async-start | bytes 7286784 | tf_op jit(solution)/shard_map/psum | solution.py:274
  (42 other events, 222.4 us)
Sparse Core Ops, SparseCore 0:
  13.2 66.3 all-gather.4
  86.7 37.2 all-gather.6
  130.9 57.6 all-gather.8
  204.6 81.4 reduce-scatter.7
  291.2 56.5 all-gather.10
  364.1 81.4 reduce-scatter.9
  459.7 38.1 reduce-scatter.11
  515.0 86.9 reduce-scatter.13
  606.1 162.7 all-reduce.9

commit v3 on v2

--- a/solution.py
+++ b/solution.py
@@ -271,8 +271,20 @@
         ],
         axis=0,
     )
-    totals = lax.psum(
-        (grad_shard, shard_gate.astype(low), shard_up.astype(low), shard_down.astype(low)), "ctx"
+    ffn_units = shard_gate.shape[0]
+    ffn_parts = jnp.concatenate([shard_gate, shard_up, shard_down], axis=0).astype(low)
+    ffn_parts = ffn_parts.reshape(parts, -1, ffn_parts.shape[1])
+    ffn_mine = jnp.sum(
+        lax.all_to_all(ffn_parts, "ctx", 0, 0).astype(f32), axis=0
+    ).astype(low)
+    ffn_sums = lax.all_to_all(
+        jnp.broadcast_to(ffn_mine[None], ffn_parts.shape), "ctx", 0, 0
+    ).reshape(3 * ffn_units, -1).astype(f32)
+    totals = (
+        lax.psum(grad_shard, "ctx"),
+        ffn_sums[:ffn_units],
+        ffn_sums[ffn_units : 2 * ffn_units],
+        ffn_sums[2 * ffn_units :],
     )
     grad_shard = totals[0].astype(f32)
     grows = grad_shard[o4:]

time: 790 us -> 795 us (level)
  waiting for transfers between devices: 562 us -> 501 us
  blocking collectives: 65.5 us -> 106 us
  local copies, waits for them, and re-layouts: 36.2 us -> 50.8 us
    psum x1, waiting for transfers between devices: 164 us -> 72 us  [body(): lax.psum(grad_shard, 'ctx')]
    all_to_all x0 -> x1, blocking collectives: none -> 40.2 us  [body(): lax.all_to_all(ffn_parts, 'ctx', 0, 0).astype(f32)]
    all_to_all x0 -> x1, waiting for transfers between devices: none -> 36.3 us  [body(): lax.all_to_all(jnp.broadcast_to(ffn_mine[None], ffn_parts.shape), 'ctx',...]
  transfers between devices with their start and end apart: 9 -> 10, of which waited for: 8 -> 9; matrix products, arithmetic and copies ran while one was open for 5% -> 8% of each run, Pallas kernels for 0% -> 0%
where the time goes in v3:
time: 795 us; the launch traced here: 789 us
  waiting for transfers between devices  501 us (63%)
  blocking collectives  106 us (13%)
  matrix products  77.2 us (10%)
  local copies, waits for them, and re-layouts  50.8 us (6%)
  other arithmetic  31.1 us (4%)
  between operations  15.9 us (2%)
    reduce_scatter x1, waiting for transfers between devices, body(): lax.psum_scatter(jnp.dot(hidden, w_down, preferred_element_type=f32).asty...  81.6 us
    reduce_scatter x1, waiting for transfers between devices, body(): lax.psum_scatter((jnp.dot(grad_gate, w_gate, preferred_element_type=f32)...  81.6 us
    psum x1, waiting for transfers between devices, body(): lax.psum(grad_shard, 'ctx')  72 us
    unnamed x1, blocking collectives  65.6 us
    all_gather x1, waiting for transfers between devices, body(): packed_all = lax.all_gather(packed, 'fsdp', axis=0, tiled=True)  63.6 us
    all_gather x1, waiting for transfers between devices, body(): rows_all = lax.all_gather(normed_pre, 'fsdp', axis=0, tiled=True)  57.5 us
    all_gather x1, waiting for transfers between devices, body(): grad_all = lax.all_gather(grad_ffn, 'fsdp', axis=0, tiled=True)  56.5 us
    all_to_all x1, blocking collectives, body(): lax.all_to_all(ffn_parts, 'ctx', 0, 0).astype(f32)  40.2 us
  transfers between devices with their start and end apart: 10, of which 9 were waited for; matrix products, arithmetic and copies ran while one was open for 8% of the time, Pallas kernels for 0%

profile of v3, /device:TPU:0, one launch (start us, length us, event | category | flops | bytes accessed | tf_op | source)
XLA Modules:
  0.0 788.6 jit_solution(4052207933449687637)
XLA Ops:
  16.0 63.6 %all-gather.5.cloned.1.call-done = bf16[1152,2688]{1,0:T(8,128)(2,1)} async-done(((bf16[72,2688]{1,0:T(8,128)(2,1)}), bf16[1152,2688]{1,0:T(8,128)(2,1)}) %all-gather.5.cloned.1.call-update) | async-done | bytes 6193168 | tf_op jit(solution)/shard_map/all_gather | solution.py:119
  86.9 3.4 slice_bitcast_fusion
  90.3 4.4 copy.93
  94.8 2.6 multiply_reduce_fusion.7
  97.7 26.2 %all-gather.7.cloned.1.call-done = bf16[1024,512]{1,0:T(8,128)(2,1)} async-done(((bf16[128,512]{1,0:T(8,128)(2,1)}), bf16[1024,512]{1,0:T(8,128)(2,1)}) %all-gather.7.cloned.1.call-update) | async-done | bytes 1048592 | tf_op jit(solution)/shard_map/all_gather | solution.py:156
  126.9 2.7 multiply_reduce_fusion.3
  132.2 57.5 %all-gather.9.cloned.1.call-done = bf16[2048,1152]{1,0:T(8,128)(2,1)} async-done(((bf16[128,1152]{1,0:T(8,128)(2,1)}), bf16[2048,1152]{1,0:T(8,128)(2,1)}) %all-gather.9.cloned.1.call-update) | async-done | bytes 4718608 | tf_op jit(solution)/shard_map/all_gather | solution.py:178
  189.7 5.2 fusion.111
  195.0 4.6 multiply_convert_fusion.1
  200.8 4.7 convolution_convert_fusion
  205.6 81.6 %reduce-scatter.8.cloned.1.call-done = bf16[128,1152]{1,0:T(8,128)(2,1)} async-done(((bf16[2048,1152]{1,0:T(8,128)(2,1)}), bf16[128,1152]{1,0:T(8,128)(2,1)}) %reduce-scatter.8.cloned.1.call-update) | async-done | bytes 294928 | tf_op jit(solution)/shard_map/reduce_scatter | solution.py:183
  292.3 56.5 %all-gather.11.cloned.1.call-done = bf16[2048,1152]{1,0:T(8,128)(2,1)} async-done(((bf16[128,1152]{1,0:T(8,128)(2,1)}), bf16[2048,1152]{1,0:T(8,128)(2,1)}) %all-gather.11.cloned.1.call-update) | async-done | bytes 4718608 | tf_op jit(solution)/shard_map/all_gather | solution.py:194
  348.8 8.5 %multiply_convert_fusion = (bf16[2048,432]{0,1:T(8,128)(2,1)S(1)}, bf16[2048,432]{0,1:T(8,128)(2,1)S(1)}) fusion(f32[2048,432]{0,1:T(8,128)} %copy-done.63, f32[2048,432]{0,1:T(8,128)} %get-tuple-element.131, bf16[2048,1152]{1,0:T(8,128)(2,1)} %all-gather.11.cloned.1.call-done, bf16[432,1152]{1,0:T(8,128)(2,1)S(1)} %copy-done), kind=kOutput, calls=%fused_computation.14 | convolution fusion | flops 2058780672 | bytes 16330752 | tf_op jit(solution)/shard_map/td,fd->tf/dot_general | solution.py:195
  357.4 3.0 fusion.112
  360.4 4.6 add_convert_fusion
  365.1 81.6 %reduce-scatter.10.cloned.1.call-done = bf16[128,1152]{1,0:T(8,128)(2,1)} async-done(((bf16[2048,1152]{1,0:T(8,128)(2,1)}), bf16[128,1152]{1,0:T(8,128)(2,1)}) %reduce-scatter.10.cloned.1.call-update) | async-done | bytes 294928 | tf_op jit(solution)/shard_map/reduce_scatter | solution.py:201
  448.6 2.7 multiply_reduce_fusion
  460.9 6.4 convolution_convert_fusion.3
  473.2 25.6 %reduce-scatter.12.cloned.1.call-done = bf16[128,512]{1,0:T(8,128)(2,1)} async-done(((bf16[1024,512]{1,0:T(8,128)(2,1)}), bf16[128,512]{1,0:T(8,128)(2,1)}) %reduce-scatter.12.cloned.1.call-update) | async-done | bytes 131088 | tf_op jit(solution)/shard_map/reduce_scatter | solution.py:229
  502.2 4.6 pad_maximum_fusion
  506.8 8.9 %copy.126 = bf16[2560,1152]{0,1:T(8,128)(2,1)} copy(bf16[2560,1152]{1,0:T(8,128)(2,1)} %pad_maximum_fusion) | data formatting | bytes 11796480
  515.7 5.4 convolution_convert_fusion.4
  521.2 5.1 convolution_convert_fusion.5
  528.1 3.7 convert_element_type.193
  531.8 40.2 %all_to_all.10 = bf16[8,162,1152]{2,1,0:T(8,128)(2,1)} all-to-all(bf16[8,162,1152]{2,1,0:T(8,128)(2,1)} %convert_element_type.193), channel_id=1, replica_groups=mesh['ctx'=8,'fsdp'=16] {'ctx'}, dimensions={0} | all-to-all | bytes 5971968 | tf_op jit(solution)/shard_map/all_to_all | solution.py:278
  576.4 5.0 all-to-all-start.1
  582.9 36.3 %all-to-all-done.1 = bf16[8,162,1152]{2,1,0:T(8,128)(2,1)} async-done(((bf16[8,162,1152]{2,1,0:T(8,128)(2,1)}), bf16[8,162,1152]{2,1,0:T(8,128)(2,1)}, u32[]{:S(2)}, u32[]{:S(2)}) %all-to-all-start.1) | async-done | bytes 2986016 | tf_op jit(solution)/shard_map/all_to_all | solution.py:280
  619.3 4.3 reshape.329
  623.6 5.5 fusion.110
  629.3 2.6 fusion.13
  635.2 65.6 %all-reduce.6 = bf16[8,1152]{1,0:T(8,128)(2,1)S(1)} all-reduce(bf16[8,1152]{1,0:T(8,128)(2,1)S(1)} %pad_bitcast_fusion), channel_id=6, replica_groups=mesh['ctx'=8,'fsdp'=16] {'fsdp'}, use_global_device_ids=true, to_apply=%region_27.28.clone | all-reduce | flops 9216 | bytes 36864
  704.1 72.0 %all-reduce.9.cloned.1.call-done = bf16[2568,72]{1,0:T(8,128)(2,1)} async-done(((bf16[2568,72]{1,0:T(8,128)(2,1)}), bf16[2568,72]{1,0:T(8,128)(2,1)}) %all-reduce.9.cloned.1.call-update) | async-done | bytes 369808 | tf_op jit(solution)/shard_map/psum | solution.py:284
  (257 shorter events, 67.9 us)
Async XLA Ops:
  7.2 193.7 %copy-start = (bf16[432,1152]{1,0:T(8,128)(2,1)S(1)}, bf16[432,1152]{1,0:T(8,128)(2,1)}, u32[]{:S(2)}) copy-start(bf16[432,1152]{1,0:T(8,128)(2,1)} %param.27) | copy-start | bytes 2985988
  7.2 75.2 %copy-start.2 = (bf16[1,128,1152]{2,1,0:T(8,128)(2,1)S(1)}, bf16[1,128,1152]{2,1,0:T(8,128)(2,1)}, u32[]{:S(2)}) copy-start(bf16[1,128,1152]{2,1,0:T(8,128)(2,1)} %param.17) | copy-start | bytes 884740
  7.2 72.4 %all-gather.5.cloned.1.call-start = ((), (), s32[]{:S(2)}) async-start(), calls=%async_computation.6 | async-start | bytes 6580224 | tf_op jit(solution)/shard_map/all_gather | solution.py:119
  13.1 110.9 %all-gather.7.cloned.1.call-start = ((), (), s32[]{:S(2)}) async-start(), calls=%async_computation.7 | async-start | bytes 1179648 | tf_op jit(solution)/shard_map/all_gather | solution.py:156
  14.0 70.2 %copy-start.44 = (f32[128]{0:T(128)}, f32[128]{0:T(128)S(1)}, u32[]{:S(2)}) copy-start(f32[128]{0:T(128)S(1)} %multiply_power_fusion) | copy-start | bytes 1540
  15.3 79.5 %copy-start.28 = (f32[128]{0:T(128)}, f32[128]{0:T(128)S(1)}, u32[]{:S(2)}) copy-start(f32[128]{0:T(128)S(1)} %add_rsqrt_fusion.5) | copy-start | bytes 1540
  16.0 68.2 %copy-start.46 = (f32[128]{0:T(128)}, f32[128]{0:T(128)S(1)}, u32[]{:S(2)}) copy-start(f32[128]{0:T(128)S(1)} %convert_bitcast_fusion.1) | copy-start | bytes 1540
  82.4 47.3 %copy-start.23 = (f32[1152]{0:T(1024)}, f32[1152]{0:T(1024)S(1)}, u32[]{:S(2)}) copy-start(f32[1152]{0:T(1024)S(1)} %get-tuple-element.87) | copy-start | bytes 13828
  82.4 207.8 %copy-start.25 = (f32[1152]{0:T(1024)}, f32[1152]{0:T(1024)S(1)}, u32[]{:S(2)}) copy-start(f32[1152]{0:T(1024)S(1)} %get-tuple-element.85) | copy-start | bytes 13828
  82.4 364.3 %copy-start.27 = (f32[1152]{0:T(1024)}, f32[1152]{0:T(1024)S(1)}, u32[]{:S(2)}) copy-start(f32[1152]{0:T(1024)S(1)} %get-tuple-element.86) | copy-start | bytes 13828
  86.6 103.1 %all-gather.9.cloned.1.call-start = ((), (), s32[]{:S(2)}) async-start(), calls=%async_computation.8 | async-start | bytes 5013504 | tf_op jit(solution)/shard_map/all_gather | solution.py:178
  86.8 39.1 %copy-start.14 = (pred[128,1024]{0,1:T(8,128)(4,1)}, pred[128,1024]{0,1:T(8,128)(4,1)S(1)}, u32[]{:S(2)}) copy-start(pred[128,1024]{0,1:T(8,128)(4,1)S(1)} %broadcast_compare_fusion) | copy-start | bytes 393220
  126.9 68.1 %copy-start.10 = (bf16[256,4,128]{2,0,1:T(8,128)(2,1)}, bf16[256,4,128]{2,0,1:T(8,128)(2,1)S(1)}, u32[]{:S(2)}) copy-start(bf16[256,4,128]{2,0,1:T(8,128)(2,1)S(1)} %convolution_convert_fusion.8) | copy-start | bytes 786436
  129.7 65.3 %copy-start.39 = (f32[128]{0:T(128)}, f32[128]{0:T(128)S(1)}, u32[]{:S(2)}) copy-start(f32[128]{0:T(128)S(1)} %add_rsqrt_fusion.3) | copy-start | bytes 1540
  130.7 316.0 %copy-start.41 = (f32[128]{0:T(128)}, f32[128]{0:T(128)S(1)}, u32[]{:S(2)}) copy-start(f32[128]{0:T(128)S(1)} %add_rsqrt_fusion.2) | copy-start | bytes 1540
  131.6 155.6 %reduce-scatter.8.cloned.1.call-start = ((), (), s32[]{:S(2)}) async-start(), calls=%async_computation.9 | async-start | bytes 5013504 | tf_op jit(solution)/shard_map/reduce_scatter | solution.py:183
  205.5 82.8 %copy-start.7 = (bf16[1,128,1152]{2,1,0:T(8,128)(2,1)S(1)}, bf16[1,128,1152]{2,1,0:T(8,128)(2,1)}, u32[]{:S(2)}) copy-start(bf16[1,128,1152]{2,1,0:T(8,128)(2,1)} %param.18) | copy-start | bytes 884740
  205.5 143.3 %all-gather.11.cloned.1.call-start = ((), (), s32[]{:S(2)}) async-start(), calls=%async_computation.10 | async-start | bytes 5013504 | tf_op jit(solution)/shard_map/all_gather | solution.py:194
  288.3 69.1 %copy-start.42 = (f32[128]{0:T(128)}, f32[128]{0:T(128)S(1)}, u32[]{:S(2)}) copy-start(f32[128]{0:T(128)S(1)} %add_rsqrt_fusion.1) | copy-start | bytes 1540
  292.1 154.6 %reduce-scatter.10.cloned.1.call-start = ((), (), s32[]{:S(2)}) async-start(), calls=%async_computation.11 | async-start | bytes 5013504 | tf_op jit(solution)/shard_map/reduce_scatter | solution.py:201
  365.0 83.6 %copy-start.5 = (f32[128,1152]{1,0:T(8,128)S(1)}, f32[128,1152]{1,0:T(8,128)}, u32[]{:S(2)}) copy-start(f32[128,1152]{1,0:T(8,128)} %copy-done.4) | copy-start | bytes 1769476
  365.0 83.6 %copy-start.6 = (bf16[128,1152]{1,0:T(8,128)(2,1)S(1)}, bf16[128,1152]{1,0:T(8,128)(2,1)}, u32[]{:S(2)}) copy-start(bf16[128,1152]{1,0:T(8,128)(2,1)} %reduce-scatter.8.cloned.1.call-done) | copy-start | bytes 884740
  365.0 83.6 %copy-start.24 = (f32[1152]{0:T(1024)S(1)}, f32[1152]{0:T(1024)}, u32[]{:S(2)}) copy-start(f32[1152]{0:T(1024)} %copy-done.23) | copy-start | bytes 13828
  365.0 83.6 %copy-start.26 = (f32[1152]{0:T(1024)S(1)}, f32[1152]{0:T(1024)}, u32[]{:S(2)}) copy-start(f32[1152]{0:T(1024)} %copy-done.25) | copy-start | bytes 13828
  365.0 83.6 %copy-start.40 = (f32[128]{0:T(128)S(1)}, f32[128]{0:T(128)}, u32[]{:S(2)}) copy-start(f32[128]{0:T(128)} %copy-done.39) | copy-start | bytes 1540
  365.0 83.6 %copy-start.43 = (f32[128]{0:T(128)S(1)}, f32[128]{0:T(128)}, u32[]{:S(2)}) copy-start(f32[128]{0:T(128)} %copy-done.42) | copy-start | bytes 1540
  365.1 133.7 %reduce-scatter.12.cloned.1.call-start = ((), (), s32[]{:S(2)}) async-start(), calls=%async_computation.12 | async-start | bytes 1179648 | tf_op jit(solution)/shard_map/reduce_scatter | solution.py:229
  460.6 240.2 %reduce-scatter.14.cloned.1.call-start = ((), (), s32[]{:S(2)}) async-start(), calls=%async_computation.14 | async-start | bytes 6266880
  468.5 31.7 %copy-start.31 = (f32[256]{0:T(256)S(1)}, f32[256]{0:T(256)}, u32[]{:S(2)}) copy-start(f32[256]{0:T(256)} %copy-done.30) | copy-start | bytes 3076
  576.4 42.9 %all-to-all-start.1 = ((bf16[8,162,1152]{2,1,0:T(8,128)(2,1)}), bf16[8,162,1152]{2,1,0:T(8,128)(2,1)}, u32[]{:S(2)}, u32[]{:S(2)}) async-start(bf16[8,162,1152]{2,1,0:T(8,128)(2,1)} %broadcast_in_dim.53), calls=%async_computation.4 | async-start | bytes 6193152 | tf_op jit(solution)/shard_map/all_to_all | solution.py:280
  581.4 194.7 %all-reduce.9.cloned.1.call-start = ((), (), s32[]{:S(2)}) async-start(), calls=%async_computation.13 | async-start | bytes 1314816 | tf_op jit(solution)/shard_map/psum | solution.py:284
  703.2 78.6 %copy-start.1 = (bf16[432,1152]{1,0:T(8,128)(2,1)S(1)}, bf16[432,1152]{1,0:T(8,128)(2,1)}, u32[]{:S(2)}) copy-start(bf16[432,1152]{1,0:T(8,128)(2,1)} %param.27) | copy-start | bytes 2985988
  (43 other events, 307.7 us)
Sparse Core Ops, SparseCore 0:
  13.2 66.3 all-gather.4
  86.7 37.2 all-gather.6
  131.7 57.9 all-gather.8
  205.6 81.4 reduce-scatter.7
  292.2 56.5 all-gather.10
  365.2 81.4 reduce-scatter.9
  460.7 38.0 reduce-scatter.11
  515.8 129.7 reduce-scatter.13
  703.3 72.7 all-reduce.8

commit v4 on v2

--- a/solution.py
+++ b/solution.py
@@ -251,7 +251,7 @@
     def head_col(g):
         return jnp.pad(g.reshape(groups, head_shard), ((0, 0), (0, width_shard - head_shard))).reshape(-1)
 
-    grad_gain_rows = jnp.stack(
+    gain_block = jnp.stack(
         [
             grad_gain_in,
             grad_gain_attn,
@@ -260,19 +260,34 @@
             head_col(grad_gain_query),
             head_col(grad_gain_key),
         ],
-        axis=1,
-    )
-    grad_gain_rows = jnp.pad(grad_gain_rows, ((0, 0), (0, 8 - grad_gain_rows.shape[1]))).T
+        axis=0,
+    )
+    gain_block = jnp.pad(gain_block, ((0, 8 - gain_block.shape[0]), (0, 0))).astype(low)
+    gain_block = jnp.transpose(gain_block.reshape(8, groups, width_shard), (1, 0, 2))
+    gain_shard = jnp.sum(lax.all_to_all(gain_block, "fsdp", 0, 0).astype(f32), axis=0)
+
+    def ctx_sum(x):
+        chunks = x.reshape(parts, -1, x.shape[1])
+        mine = jnp.sum(lax.all_to_all(chunks, "ctx", 0, 0).astype(f32), axis=0).astype(low)
+        return lax.all_to_all(jnp.broadcast_to(mine[None], chunks.shape), "ctx", 0, 0).reshape(x.shape)
+
+    ffn_units = shard_gate.shape[0]
+    ffn_sums = ctx_sum(
+        jnp.concatenate([shard_gate, shard_up, shard_down], axis=0).astype(low)
+    ).astype(f32)
     grad_packed = jnp.concatenate([term_query, term_key, term_value, term_output], axis=0).astype(low)
     grad_shard = jnp.concatenate(
         [
             lax.psum_scatter(grad_packed, "fsdp", scatter_dimension=1, tiled=True),
-            lax.psum_scatter(grad_gain_rows.astype(low), "fsdp", scatter_dimension=1, tiled=True),
+            gain_shard.astype(low),
         ],
         axis=0,
     )
-    totals = lax.psum(
-        (grad_shard, shard_gate.astype(low), shard_up.astype(low), shard_down.astype(low)), "ctx"
+    totals = (
+        ctx_sum(grad_shard),
+        ffn_sums[:ffn_units],
+        ffn_sums[ffn_units : 2 * ffn_units],
+        ffn_sums[2 * ffn_units :],
     )
     grad_shard = totals[0].astype(f32)
     grows = grad_shard[o4:]

time: 790 us -> 692 us (0.88)
  waiting for transfers between devices: 562 us -> 450 us
  blocking collectives: 65.5 us -> 41.4 us
  starting transfers between devices: 1.04 us -> 20.5 us
  local copies, waits for them, and re-layouts: 36.2 us -> 52 us
    psum x1 -> x0, waiting for transfers between devices: 164 us -> none  [body(): lax.psum((grad_shard, shard_gate.astype(low), shard_up.astype(low), shard...]
    unnamed x1 -> x0, blocking collectives: 65.5 us -> none
    all_to_all x0 -> x4, waiting for transfers between devices: none -> 43.1 us  [the longest x2 37.7 us: ctx_sum(): lax.all_to_all(jnp.broadcast_to(mine[None], chunks.shape), 'ctx', 0, 0)]
    all_to_all x0 -> x1, blocking collectives: none -> 41.4 us  [ctx_sum(): lax.all_to_all(chunks, 'ctx', 0, 0).astype(f32)]
    all_to_all x0 -> x4, starting transfers between devices: none -> 19.2 us  [the longest x2 8.42 us: ctx_sum(): lax.all_to_all(jnp.broadcast_to(mine[None], chunks.shape), 'ctx', 0, 0)]
    unnamed x10 -> x9, waiting for transfers between devices: 0.15 us -> 9.48 us
    convert_element_type x1 -> x4, local copies, waits for them, and re-layouts: 0.01 us -> 8.32 us  [the longest x1 4.31 us: body(): ffn_sums = ctx_sum(jnp.concatenate([shard_gate, shard_up, shard_down], ax...]
    unnamed x144 -> x140, local copies, waits for them, and re-layouts: 21.9 us -> 18.3 us
  transfers between devices with their start and end apart: 9 -> 12, of which waited for: 8 -> 12; matrix products, arithmetic and copies ran while one was open for 5% -> 9% of each run, Pallas kernels for 0% -> 0%
where the time goes in v4:
time: 692 us; the launch traced here: 685 us
  waiting for transfers between devices  450 us (65%)
  matrix products  75.5 us (11%)
  local copies, waits for them, and re-layouts  52 us (8%)
  blocking collectives  41.4 us (6%)
  other arithmetic  29.2 us (4%)
  starting transfers between devices  20.5 us (3%)
  between operations  15.6 us (2%)
    reduce_scatter x1, waiting for transfers between devices, body(): lax.psum_scatter((jnp.dot(grad_gate, w_gate, preferred_element_type=f32)...  81.6 us
    reduce_scatter x1, waiting for transfers between devices, body(): lax.psum_scatter(jnp.dot(hidden, w_down, preferred_element_type=f32).asty...  81.6 us
    all_gather x1, waiting for transfers between devices, body(): packed_all = lax.all_gather(packed, 'fsdp', axis=0, tiled=True)  63.6 us
    all_gather x1, waiting for transfers between devices, body(): rows_all = lax.all_gather(normed_pre, 'fsdp', axis=0, tiled=True)  57.5 us
    all_gather x1, waiting for transfers between devices, body(): grad_all = lax.all_gather(grad_ffn, 'fsdp', axis=0, tiled=True)  56.5 us
    all_to_all x1, blocking collectives, ctx_sum(): lax.all_to_all(chunks, 'ctx', 0, 0).astype(f32)  41.4 us
    all_to_all x2, waiting for transfers between devices, ctx_sum(): lax.all_to_all(jnp.broadcast_to(mine[None], chunks.shape), 'ctx', 0, 0)  37.7 us
    reduce_scatter x1, waiting for transfers between devices, body(): lax.psum_scatter(key_value_terms.astype(jnp.bfloat16), 'ctx', scatter_dim...  30.7 us
  transfers between devices with their start and end apart: 12, of which 12 were waited for; matrix products, arithmetic and copies ran while one was open for 9% of the time, Pallas kernels for 0%

profile of v4, /device:TPU:0, one launch (start us, length us, event | category | flops | bytes accessed | tf_op | source)
XLA Modules:
  0.0 684.6 jit_solution(13830200131307429831)
XLA Ops:
  16.0 63.6 %all-gather.5.cloned.1.call-done = bf16[1152,2688]{1,0:T(8,128)(2,1)} async-done(((bf16[72,2688]{1,0:T(8,128)(2,1)}), bf16[1152,2688]{1,0:T(8,128)(2,1)}) %all-gather.5.cloned.1.call-update) | async-done | bytes 6193168 | tf_op jit(solution)/shard_map/all_gather | solution.py:119
  86.9 3.4 slice_bitcast_fusion
  90.2 4.3 copy.104
  97.6 26.3 %all-gather.7.cloned.1.call-done = bf16[1024,512]{1,0:T(8,128)(2,1)} async-done(((bf16[128,512]{1,0:T(8,128)(2,1)}), bf16[1024,512]{1,0:T(8,128)(2,1)}) %all-gather.7.cloned.1.call-update) | async-done | bytes 1048592 | tf_op jit(solution)/shard_map/all_gather | solution.py:156
  132.2 57.5 %all-gather.9.cloned.1.call-done = bf16[2048,1152]{1,0:T(8,128)(2,1)} async-done(((bf16[128,1152]{1,0:T(8,128)(2,1)}), bf16[2048,1152]{1,0:T(8,128)(2,1)}) %all-gather.9.cloned.1.call-update) | async-done | bytes 4718608 | tf_op jit(solution)/shard_map/all_gather | solution.py:178
  189.7 5.2 fusion.112
  195.0 4.7 multiply_convert_fusion.1
  200.9 4.6 convolution_convert_fusion
  205.6 81.6 %reduce-scatter.7.cloned.1.call-done = bf16[128,1152]{1,0:T(8,128)(2,1)} async-done(((bf16[2048,1152]{1,0:T(8,128)(2,1)}), bf16[128,1152]{1,0:T(8,128)(2,1)}) %reduce-scatter.7.cloned.1.call-update) | async-done | bytes 294928 | tf_op jit(solution)/shard_map/reduce_scatter | solution.py:183
  292.3 56.5 %all-gather.11.cloned.1.call-done = bf16[2048,1152]{1,0:T(8,128)(2,1)} async-done(((bf16[128,1152]{1,0:T(8,128)(2,1)}), bf16[2048,1152]{1,0:T(8,128)(2,1)}) %all-gather.11.cloned.1.call-update) | async-done | bytes 4718608 | tf_op jit(solution)/shard_map/all_gather | solution.py:194
  348.9 8.5 %multiply_convert_fusion = (bf16[2048,432]{0,1:T(8,128)(2,1)S(1)}, bf16[2048,432]{0,1:T(8,128)(2,1)S(1)}) fusion(f32[2048,432]{0,1:T(8,128)} %copy-done.62, f32[2048,432]{0,1:T(8,128)} %get-tuple-element.73, bf16[2048,1152]{1,0:T(8,128)(2,1)} %all-gather.11.cloned.1.call-done, bf16[432,1152]{1,0:T(8,128)(2,1)S(1)} %copy-done), kind=kOutput, calls=%fused_computation.14 | convolution fusion | flops 2058780672 | bytes 16330752 | tf_op jit(solution)/shard_map/td,fd->tf/dot_general | solution.py:195
  357.4 3.0 fusion.113
  360.5 4.6 add_convert_fusion
  365.2 81.6 %reduce-scatter.9.cloned.1.call-done = bf16[128,1152]{1,0:T(8,128)(2,1)} async-done(((bf16[2048,1152]{1,0:T(8,128)(2,1)}), bf16[128,1152]{1,0:T(8,128)(2,1)}) %reduce-scatter.9.cloned.1.call-update) | async-done | bytes 294928 | tf_op jit(solution)/shard_map/reduce_scatter | solution.py:201
  448.7 2.7 multiply_reduce_fusion
  468.3 30.7 %reduce-scatter.11.cloned.1.call-done = bf16[128,512]{1,0:T(8,128)(2,1)} async-done(((bf16[1024,512]{1,0:T(8,128)(2,1)}), bf16[128,512]{1,0:T(8,128)(2,1)}) %reduce-scatter.11.cloned.1.call-update) | async-done | bytes 131088 | tf_op jit(solution)/shard_map/reduce_scatter | solution.py:229
  502.3 4.6 pad_maximum_fusion
  507.0 8.9 %copy.139 = bf16[2560,1152]{0,1:T(8,128)(2,1)} copy(bf16[2560,1152]{1,0:T(8,128)(2,1)} %pad_maximum_fusion) | data formatting | bytes 11796480
  515.9 5.5 convolution_convert_fusion.3
  521.4 5.2 convolution_convert_fusion.4
  531.0 3.7 convert_element_type.197
  534.7 41.4 %all_to_all.25 = bf16[8,162,1152]{2,1,0:T(8,128)(2,1)} all-to-all(bf16[8,162,1152]{2,1,0:T(8,128)(2,1)} %convert_element_type.197), channel_id=1, replica_groups=mesh['ctx'=8,'fsdp'=16] {'ctx'}, dimensions={0} | all-to-all | bytes 5971968 | tf_op jit(solution)/shard_map/all_to_all | solution.py:271
  580.5 4.8 all-to-all-start.4
  592.9 31.1 %all-to-all-done.4 = bf16[8,162,1152]{2,1,0:T(8,128)(2,1)} async-done(((bf16[8,162,1152]{2,1,0:T(8,128)(2,1)}), bf16[8,162,1152]{2,1,0:T(8,128)(2,1)}, u32[]{:S(2)}, u32[]{:S(2)}) %all-to-all-start.4) | async-done | bytes 2986016 | tf_op jit(solution)/shard_map/all_to_all | solution.py:272
  624.0 6.8 all-to-all-start
  630.8 4.3 reshape.342
  635.1 3.3 all-to-all-done
  638.4 9.3 %reduce-scatter.13.cloned.1.call-done = bf16[72,2560]{1,0:T(8,128)(2,1)} async-done(((bf16[1152,2560]{1,0:T(8,128)(2,1)}), bf16[72,2560]{1,0:T(8,128)(2,1)}) %reduce-scatter.13.cloned.1.call-update) | async-done | bytes 368656
  650.4 4.0 all-to-all-start.1
  654.4 5.5 fusion.110
  663.0 3.6 all-to-all-start.2
  667.5 6.7 all-to-all-done.2
  (263 shorter events, 81.5 us)
Async XLA Ops:
  7.2 193.7 %copy-start = (bf16[432,1152]{1,0:T(8,128)(2,1)S(1)}, bf16[432,1152]{1,0:T(8,128)(2,1)}, u32[]{:S(2)}) copy-start(bf16[432,1152]{1,0:T(8,128)(2,1)} %param.27) | copy-start | bytes 2985988
  7.2 75.2 %copy-start.2 = (bf16[1,128,1152]{2,1,0:T(8,128)(2,1)S(1)}, bf16[1,128,1152]{2,1,0:T(8,128)(2,1)}, u32[]{:S(2)}) copy-start(bf16[1,128,1152]{2,1,0:T(8,128)(2,1)} %param.17) | copy-start | bytes 884740
  7.2 72.4 %all-gather.5.cloned.1.call-start = ((), (), s32[]{:S(2)}) async-start(), calls=%async_computation.9 | async-start | bytes 6580224 | tf_op jit(solution)/shard_map/all_gather | solution.py:119
  13.1 110.9 %all-gather.7.cloned.1.call-start = ((), (), s32[]{:S(2)}) async-start(), calls=%async_computation.10 | async-start | bytes 1179648 | tf_op jit(solution)/shard_map/all_gather | solution.py:156
  14.0 70.2 %copy-start.45 = (f32[128]{0:T(128)}, f32[128]{0:T(128)S(1)}, u32[]{:S(2)}) copy-start(f32[128]{0:T(128)S(1)} %multiply_power_fusion) | copy-start | bytes 1540
  15.3 79.4 %copy-start.28 = (f32[128]{0:T(128)}, f32[128]{0:T(128)S(1)}, u32[]{:S(2)}) copy-start(f32[128]{0:T(128)S(1)} %add_rsqrt_fusion.5) | copy-start | bytes 1540
  16.0 68.2 %copy-start.47 = (f32[128]{0:T(128)}, f32[128]{0:T(128)S(1)}, u32[]{:S(2)}) copy-start(f32[128]{0:T(128)S(1)} %convert_bitcast_fusion.1) | copy-start | bytes 1540
  82.4 47.3 %copy-start.23 = (f32[1152]{0:T(1024)}, f32[1152]{0:T(1024)S(1)}, u32[]{:S(2)}) copy-start(f32[1152]{0:T(1024)S(1)} %get-tuple-element.33) | copy-start | bytes 13828
  82.4 207.8 %copy-start.25 = (f32[1152]{0:T(1024)}, f32[1152]{0:T(1024)S(1)}, u32[]{:S(2)}) copy-start(f32[1152]{0:T(1024)S(1)} %get-tuple-element.31) | copy-start | bytes 13828
  82.4 364.4 %copy-start.27 = (f32[1152]{0:T(1024)}, f32[1152]{0:T(1024)S(1)}, u32[]{:S(2)}) copy-start(f32[1152]{0:T(1024)S(1)} %get-tuple-element.32) | copy-start | bytes 13828
  86.6 103.1 %all-gather.9.cloned.1.call-start = ((), (), s32[]{:S(2)}) async-start(), calls=%async_computation.11 | async-start | bytes 5013504 | tf_op jit(solution)/shard_map/all_gather | solution.py:178
  86.8 39.1 %copy-start.13 = (pred[128,1024]{0,1:T(8,128)(4,1)}, pred[128,1024]{0,1:T(8,128)(4,1)S(1)}, u32[]{:S(2)}) copy-start(pred[128,1024]{0,1:T(8,128)(4,1)S(1)} %broadcast_compare_fusion) | copy-start | bytes 393220
  126.9 68.1 %copy-start.10 = (bf16[256,4,128]{2,0,1:T(8,128)(2,1)}, bf16[256,4,128]{2,0,1:T(8,128)(2,1)S(1)}, u32[]{:S(2)}) copy-start(bf16[256,4,128]{2,0,1:T(8,128)(2,1)S(1)} %convolution_convert_fusion.8) | copy-start | bytes 786436
  129.7 65.3 %copy-start.40 = (f32[128]{0:T(128)}, f32[128]{0:T(128)S(1)}, u32[]{:S(2)}) copy-start(f32[128]{0:T(128)S(1)} %add_rsqrt_fusion.3) | copy-start | bytes 1540
  130.7 316.0 %copy-start.42 = (f32[128]{0:T(128)}, f32[128]{0:T(128)S(1)}, u32[]{:S(2)}) copy-start(f32[128]{0:T(128)S(1)} %add_rsqrt_fusion.2) | copy-start | bytes 1540
  131.6 155.6 %reduce-scatter.7.cloned.1.call-start = ((), (), s32[]{:S(2)}) async-start(), calls=%async_computation.12 | async-start | bytes 5013504 | tf_op jit(solution)/shard_map/reduce_scatter | solution.py:183
  205.5 82.8 %copy-start.7 = (bf16[1,128,1152]{2,1,0:T(8,128)(2,1)S(1)}, bf16[1,128,1152]{2,1,0:T(8,128)(2,1)}, u32[]{:S(2)}) copy-start(bf16[1,128,1152]{2,1,0:T(8,128)(2,1)} %param.18) | copy-start | bytes 884740
  205.5 143.3 %all-gather.11.cloned.1.call-start = ((), (), s32[]{:S(2)}) async-start(), calls=%async_computation.13 | async-start | bytes 5013504 | tf_op jit(solution)/shard_map/all_gather | solution.py:194
  288.3 69.1 %copy-start.43 = (f32[128]{0:T(128)}, f32[128]{0:T(128)S(1)}, u32[]{:S(2)}) copy-start(f32[128]{0:T(128)S(1)} %add_rsqrt_fusion.1) | copy-start | bytes 1540
  292.1 154.7 %reduce-scatter.9.cloned.1.call-start = ((), (), s32[]{:S(2)}) async-start(), calls=%async_computation.14 | async-start | bytes 5013504 | tf_op jit(solution)/shard_map/reduce_scatter | solution.py:201
  365.0 83.6 %copy-start.5 = (f32[128,1152]{1,0:T(8,128)S(1)}, f32[128,1152]{1,0:T(8,128)}, u32[]{:S(2)}) copy-start(f32[128,1152]{1,0:T(8,128)} %copy-done.4) | copy-start | bytes 1769476
  365.0 83.6 %copy-start.6 = (bf16[128,1152]{1,0:T(8,128)(2,1)S(1)}, bf16[128,1152]{1,0:T(8,128)(2,1)}, u32[]{:S(2)}) copy-start(bf16[128,1152]{1,0:T(8,128)(2,1)} %reduce-scatter.7.cloned.1.call-done) | copy-start | bytes 884740
  365.0 83.6 %copy-start.24 = (f32[1152]{0:T(1024)S(1)}, f32[1152]{0:T(1024)}, u32[]{:S(2)}) copy-start(f32[1152]{0:T(1024)} %copy-done.23) | copy-start | bytes 13828
  365.0 83.6 %copy-start.26 = (f32[1152]{0:T(1024)S(1)}, f32[1152]{0:T(1024)}, u32[]{:S(2)}) copy-start(f32[1152]{0:T(1024)} %copy-done.25) | copy-start | bytes 13828
  365.1 83.6 %copy-start.41 = (f32[128]{0:T(128)S(1)}, f32[128]{0:T(128)}, u32[]{:S(2)}) copy-start(f32[128]{0:T(128)} %copy-done.40) | copy-start | bytes 1540
  365.1 83.6 %copy-start.44 = (f32[128]{0:T(128)S(1)}, f32[128]{0:T(128)}, u32[]{:S(2)}) copy-start(f32[128]{0:T(128)} %copy-done.43) | copy-start | bytes 1540
  365.1 133.9 %reduce-scatter.11.cloned.1.call-start = ((), (), s32[]{:S(2)}) async-start(), calls=%async_computation.15 | async-start | bytes 1179648 | tf_op jit(solution)/shard_map/reduce_scatter | solution.py:229
  460.7 187.0 %reduce-scatter.13.cloned.1.call-start = ((), (), s32[]{:S(2)}) async-start(), calls=%async_computation.16 | async-start | bytes 6266880
  580.5 43.5 %all-to-all-start.4 = ((bf16[8,162,1152]{2,1,0:T(8,128)(2,1)}), bf16[8,162,1152]{2,1,0:T(8,128)(2,1)}, u32[]{:S(2)}, u32[]{:S(2)}) async-start(bf16[8,162,1152]{2,1,0:T(8,128)(2,1)} %broadcast_in_dim.56), calls=%async_computation.7 | async-start | bytes 6193152 | tf_op jit(solution)/shard_map/all_to_all | solution.py:272
  624.0 14.4 %all-to-all-start = ((bf16[16,8,72]{2,1,0:T(8,128)(2,1)}), bf16[16,8,72]{2,1,0:T(8,128)(2,1)S(1)}, u32[]{:S(2)}, u32[]{:S(2)}) async-start(bf16[16,8,72]{2,1,0:T(8,128)(2,1)} %copy.118), calls=%async_computation.3 | async-start | bytes 65536 | tf_op jit(solution)/shard_map/all_to_all | solution.py:267
  650.4 11.6 %all-to-all-start.1 = ((bf16[8,321,72]{1,2,0:T(8,128)(2,1)}), bf16[8,321,72]{1,2,0:T(8,128)(2,1)S(1)}, u32[]{:S(2)}, u32[]{:S(2)}) async-start(bf16[8,321,72]{1,2,0:T(8,128)(2,1)} %copy.120), calls=%async_computation.4 | async-start | bytes 884736 | tf_op jit(solution)/shard_map/all_to_all | solution.py:271
  663.0 11.3 %all-to-all-start.2 = ((bf16[8,321,72]{1,2,0:T(8,128)(2,1)}), bf16[8,321,72]{1,2,0:T(8,128)(2,1)S(1)}, u32[]{:S(2)}, u32[]{:S(2)}) async-start(bf16[8,321,72]{1,2,0:T(8,128)(2,1)} %broadcast_in_dim.55), calls=%async_computation.5 | async-start | bytes 884736 | tf_op jit(solution)/shard_map/all_to_all | solution.py:272
  (46 other events, 398.1 us)
Sparse Core Ops, SparseCore 0:
  13.2 66.3 all-gather.4
  86.7 37.2 all-gather.6
  131.7 57.9 all-gather.8
  205.7 81.4 reduce-scatter.6
  292.2 56.5 all-gather.10
  365.2 81.5 reduce-scatter.8
  460.9 38.0 reduce-scatter.10
  516.0 131.7 reduce-scatter.12

commit v5 on v4

--- a/solution.py
+++ b/solution.py
@@ -71,6 +71,16 @@
 
 def pad_rows(shard, rows):
     return jnp.pad(shard, (0, rows - shard.shape[0]))
+
+
+def a2a_sum(x, axis_name, count):
+    pieces = lax.all_to_all(x.reshape(count, -1, *x.shape[1:]), axis_name, 0, 0)
+    return jnp.sum(pieces.astype(jnp.float32), axis=0)
+
+
+def a2a_gather(x, axis_name, count):
+    copies = jnp.broadcast_to(x[None], (count,) + x.shape)
+    return lax.all_to_all(copies, axis_name, 0, 0).reshape(count * x.shape[0], *x.shape[1:])
 
 
 def body(
@@ -153,9 +163,7 @@
     scale = HD ** (-0.5)
     query_rot = (rotate(query_normed, cosine[:, None, :], sine[:, None, :]) * scale).astype(low)
     key_rot = rotate(key_normed, cosine, sine).astype(low)
-    kv_all = lax.all_gather(
-        jnp.concatenate([key_rot, values], axis=1), "ctx", axis=0, tiled=True
-    )
+    kv_all = a2a_gather(jnp.concatenate([key_rot, values], axis=1), "ctx", parts)
     key_all = kv_all[:, :HD]
     value_all = kv_all[:, HD:]
     scores = jnp.einsum("qhd,kd->hqk", query_rot, key_all, preferred_element_type=f32)
@@ -180,12 +188,9 @@
     upper = jnp.einsum("td,fd->tf", rows_all, w_up, preferred_element_type=f32)
     gelu_value, gelu_slope = gelu_pair(gate)
     hidden = (gelu_value * upper).astype(low)
-    branch_ffn = lax.psum_scatter(
-        jnp.dot(hidden, w_down, preferred_element_type=f32).astype(jnp.bfloat16),
-        "fsdp",
-        scatter_dimension=0,
-        tiled=True,
-    ).astype(jnp.float32)
+    branch_ffn = a2a_sum(
+        jnp.dot(hidden, w_down, preferred_element_type=f32).astype(jnp.bfloat16), "fsdp", groups
+    )
     post_normed, post_unit, post_inv = norm_forward(branch_ffn, norm_post)
     outputs = (residual + post_normed).astype(low)
     grad_out = out_grad[0].astype(f32)
@@ -198,15 +203,14 @@
     shard_gate = jnp.einsum("tf,td->fd", grad_gate, rows_all, preferred_element_type=f32)
     shard_up = jnp.einsum("tf,td->fd", grad_up, rows_all, preferred_element_type=f32)
     shard_down = jnp.einsum("tf,td->fd", hidden, grad_all, preferred_element_type=f32)
-    grad_pre = lax.psum_scatter(
+    grad_pre = a2a_sum(
         (
             jnp.dot(grad_gate, w_gate, preferred_element_type=f32)
             + jnp.dot(grad_up, w_up, preferred_element_type=f32)
         ).astype(jnp.bfloat16),
         "fsdp",
-        scatter_dimension=0,
-        tiled=True,
-    ).astype(jnp.float32)
+        groups,
+    )
     grad_from_pre, grad_gain_pre = norm_backward(grad_pre, pre_unit, pre_inv, norm_pre)
     grad_residual = grad_out + grad_from_pre
     grad_branch_full, grad_gain_attn = norm_backward(grad_residual, attn_unit, attn_inv, norm_attn)
@@ -226,9 +230,7 @@
     key_term = jnp.einsum("hqk,qhd->kd", grad_scores, query_rot, preferred_element_type=f32)
     key_value_terms = jnp.concatenate([key_term, value_term], axis=1)
     grad_query_rot = jnp.einsum("hqk,kd->qhd", grad_scores, key_all, preferred_element_type=f32)
-    summed_kv = lax.psum_scatter(
-        key_value_terms.astype(jnp.bfloat16), "ctx", scatter_dimension=0, tiled=True
-    ).astype(jnp.float32)
+    summed_kv = a2a_sum(key_value_terms.astype(jnp.bfloat16), "ctx", parts)
     grad_key_rot = summed_kv[:, :HD]
     grad_values = summed_kv[:, HD:].astype(low)
     grad_q_normed = rotate_back(grad_query_rot * scale, cosine[:, None, :], sine[:, None, :])

time: 692 us -> 619 us (0.89)
  waiting for transfers between devices: 450 us -> 304 us
  blocking collectives: 41.4 us -> 105 us
  starting transfers between devices: 20.5 us -> 34.9 us
  matrix products: 75.5 us -> 66.8 us
    reduce_scatter x3 -> x0, waiting for transfers between devices: 194 us -> none  [the longest x1 81.6 us: body(): lax.psum_scatter((jnp.dot(grad_gate, w_gate, preferred_element_type=f32)...]
    all_to_all x0 -> x3, waiting for transfers between devices: none -> 80.7 us  [the longest x2 67.7 us: a2a_sum(): pieces = lax.all_to_all(x.reshape(count, -1, *x.shape[1:]), axis_name, 0, 0)]
    all_to_all x0 -> x1, blocking collectives: none -> 61.1 us  [a2a_sum(): pieces = lax.all_to_all(x.reshape(count, -1, *x.shape[1:]), axis_name, 0, 0)]
    all_gather x1 -> x0, waiting for transfers between devices: 26.3 us -> none  [body(): lax.all_gather(jnp.concatenate([key_rot, values], axis=1), 'ctx', axis=0,...]
    all_to_all x0 -> x3, starting transfers between devices: none -> 13.8 us  [the longest x2 9.5 us: a2a_sum(): pieces = lax.all_to_all(x.reshape(count, -1, *x.shape[1:]), axis_name, 0, 0)]
    unnamed x9 -> x5, waiting for transfers between devices: 9.48 us -> 0.08 us
    unnamed x140 -> x108, local copies, waits for them, and re-layouts: 18.3 us -> 18 us
  transfers between devices with their start and end apart: 12 -> 11, of which waited for: 12 -> 10; matrix products, arithmetic and copies ran while one was open for 9% -> 9% of each run, Pallas kernels for 0% -> 0%
where the time goes in v5:
time: 619 us; the launch traced here: 612 us
  waiting for transfers between devices  304 us (49%)
  blocking collectives  105 us (17%)
  matrix products  66.8 us (11%)
  local copies, waits for them, and re-layouts  54.4 us (9%)
  starting transfers between devices  34.9 us (6%)
  other arithmetic  31.3 us (5%)
  between operations  15.4 us (2%)
    all_to_all x2, waiting for transfers between devices, a2a_sum(): pieces = lax.all_to_all(x.reshape(count, -1, *x.shape[1:]), axis_name, 0, 0)  67.7 us
    all_gather x1, waiting for transfers between devices, body(): packed_all = lax.all_gather(packed, 'fsdp', axis=0, tiled=True)  63.4 us
    all_to_all x1, blocking collectives, a2a_sum(): pieces = lax.all_to_all(x.reshape(count, -1, *x.shape[1:]), axis_name, 0, 0)  61.1 us
    all_gather x1, waiting for transfers between devices, body(): grad_all = lax.all_gather(grad_ffn, 'fsdp', axis=0, tiled=True)  55.3 us
    all_gather x1, waiting for transfers between devices, body(): rows_all = lax.all_gather(normed_pre, 'fsdp', axis=0, tiled=True)  54.6 us
    all_to_all x1, blocking collectives, ctx_sum(): lax.all_to_all(chunks, 'ctx', 0, 0).astype(f32)  44.3 us
    all_to_all x2, waiting for transfers between devices, ctx_sum(): lax.all_to_all(jnp.broadcast_to(mine[None], chunks.shape), 'ctx', 0, 0)  43 us
    unnamed x108, local copies, waits for them, and re-layouts  18 us
  transfers between devices with their start and end apart: 11, of which 10 were waited for; matrix products, arithmetic and copies ran while one was open for 9% of the time, Pallas kernels for 0%

profile of v5, /device:TPU:0, one launch (start us, length us, event | category | flops | bytes accessed | tf_op | source)
XLA Modules:
  0.0 612.2 jit_solution(17631443692298647112)
XLA Ops:
  16.2 63.4 %all-gather.4.cloned.1.call-done = bf16[1152,2688]{1,0:T(8,128)(2,1)} async-done(((bf16[72,2688]{1,0:T(8,128)(2,1)}), bf16[1152,2688]{1,0:T(8,128)(2,1)}) %all-gather.4.cloned.1.call-update) | async-done | bytes 6193168 | tf_op jit(solution)/shard_map/all_gather | solution.py:129
  84.0 3.3 slice_bitcast_fusion
  87.3 4.3 copy.90
  94.8 4.3 all-to-all-start
  102.9 13.0 %all-to-all-done = bf16[8,128,512]{2,1,0:T(8,128)(2,1)S(1)} async-done(((bf16[8,128,512]{2,1,0:T(8,128)(2,1)}), bf16[8,128,512]{2,1,0:T(8,128)(2,1)S(1)}, u32[]{:S(2)}, u32[]{:S(2)}) %all-to-all-start) | async-done | bytes 1048608 | tf_op jit(solution)/shard_map/all_to_all | solution.py:83
  122.5 54.6 %all-gather.6.cloned.1.call-done = bf16[2048,1152]{1,0:T(8,128)(2,1)} async-done(((bf16[128,1152]{1,0:T(8,128)(2,1)}), bf16[2048,1152]{1,0:T(8,128)(2,1)}) %all-gather.6.cloned.1.call-update) | async-done | bytes 4718608 | tf_op jit(solution)/shard_map/all_gather | solution.py:186
  177.1 5.2 fusion.103
  182.4 4.7 multiply_convert_fusion.1
  187.1 3.2 convolution_convert_fusion
  190.3 61.1 %all_to_all.45 = bf16[16,128,1152]{2,1,0:T(8,128)(2,1)S(1)} all-to-all(bf16[16,128,1152]{2,1,0:T(8,128)(2,1)S(1)} %bitcast.185), channel_id=1, replica_groups=mesh['ctx'=8,'fsdp'=16] {'fsdp'}, dimensions={0} | all-to-all | bytes 9437184 | tf_op jit(solution)/shard_map/all_to_all | solution.py:77
  253.8 55.3 %all-gather.8.cloned.1.call-done = bf16[2048,1152]{1,0:T(8,128)(2,1)} async-done(((bf16[128,1152]{1,0:T(8,128)(2,1)}), bf16[2048,1152]{1,0:T(8,128)(2,1)}) %all-gather.8.cloned.1.call-update) | async-done | bytes 4718608 | tf_op jit(solution)/shard_map/all_gather | solution.py:199
  309.1 8.5 %multiply_convert_fusion = (bf16[2048,432]{0,1:T(8,128)(2,1)S(1)}, bf16[2048,432]{0,1:T(8,128)(2,1)S(1)}) fusion(f32[2048,432]{0,1:T(8,128)} %copy-done.46, f32[2048,432]{0,1:T(8,128)} %get-tuple-element.74, bf16[2048,1152]{1,0:T(8,128)(2,1)} %all-gather.8.cloned.1.call-done, bf16[432,1152]{1,0:T(8,128)(2,1)S(1)} %copy-done), kind=kOutput, calls=%fused_computation.16 | convolution fusion | flops 2058780672 | bytes 16330752 | tf_op jit(solution)/shard_map/td,fd->tf/dot_general | solution.py:200
  320.7 4.6 add_convert_fusion
  325.2 4.8 all-to-all-start.2
  333.2 60.1 %all-to-all-done.2 = bf16[16,128,1152]{2,1,0:T(8,128)(2,1)} async-done(((bf16[16,128,1152]{2,1,0:T(8,128)(2,1)}), bf16[16,128,1152]{2,1,0:T(8,128)(2,1)}, u32[]{:S(2)}, u32[]{:S(2)}) %all-to-all-start.2) | async-done | bytes 4718624 | tf_op jit(solution)/shard_map/all_to_all | solution.py:77
  409.8 4.7 all-to-all-start.3
  422.9 7.7 %all-to-all-done.3 = bf16[8,128,512]{2,1,0:T(8,128)(2,1)S(1)} async-done(((bf16[8,128,512]{2,1,0:T(8,128)(2,1)}), bf16[8,128,512]{2,1,0:T(8,128)(2,1)S(1)}, u32[]{:S(2)}, u32[]{:S(2)}) %all-to-all-start.3) | async-done | bytes 1048608 | tf_op jit(solution)/shard_map/all_to_all | solution.py:77
  432.2 4.6 pad_maximum_fusion
  436.8 8.9 %copy.117 = bf16[2560,1152]{0,1:T(8,128)(2,1)} copy(bf16[2560,1152]{1,0:T(8,128)(2,1)} %pad_maximum_fusion) | data formatting | bytes 11796480
  445.7 5.5 convolution_convert_fusion.3
  458.1 3.6 convert_element_type.202
  461.6 44.3 %all_to_all.46 = bf16[8,162,1152]{2,1,0:T(8,128)(2,1)} all-to-all(bf16[8,162,1152]{2,1,0:T(8,128)(2,1)} %convert_element_type.202), channel_id=1, replica_groups=mesh['ctx'=8,'fsdp'=16] {'ctx'}, dimensions={0} | all-to-all | bytes 5971968 | tf_op jit(solution)/shard_map/all_to_all | solution.py:273
  510.3 5.3 all-to-all-start.8
  522.4 35.6 %all-to-all-done.8 = bf16[8,162,1152]{2,1,0:T(8,128)(2,1)} async-done(((bf16[8,162,1152]{2,1,0:T(8,128)(2,1)}), bf16[8,162,1152]{2,1,0:T(8,128)(2,1)}, u32[]{:S(2)}, u32[]{:S(2)}) %all-to-all-start.8) | async-done | bytes 2986016 | tf_op jit(solution)/shard_map/all_to_all | solution.py:274
  558.0 8.2 %all-to-all-start.4 = ((bf16[16,8,72]{2,1,0:T(8,128)(2,1)}), bf16[16,8,72]{2,1,0:T(8,128)(2,1)S(1)}, u32[]{:S(2)}, u32[]{:S(2)}) async-start(bf16[16,8,72]{2,1,0:T(8,128)(2,1)} %copy.100), calls=%async_computation.4 | async-start | bytes 65536 | tf_op jit(solution)/shard_map/all_to_all | solution.py:269
  566.2 4.3 reshape.360
  570.5 3.3 all-to-all-done.4
  576.5 3.5 all-to-all-start.5
  580.0 5.5 fusion.101
  585.5 3.5 all-to-all-done.5
  589.9 3.5 all-to-all-start.6
  594.4 7.4 %all-to-all-done.6 = bf16[8,321,72]{1,2,0:T(8,128)(2,1)S(1)} async-done(((bf16[8,321,72]{1,2,0:T(8,128)(2,1)}), bf16[8,321,72]{1,2,0:T(8,128)(2,1)S(1)}, u32[]{:S(2)}, u32[]{:S(2)}) %all-to-all-start.6) | async-done | bytes 369824 | tf_op jit(solution)/shard_map/all_to_all | solution.py:274
  (231 shorter events, 87.0 us)
Async XLA Ops:
  7.2 179.9 %copy-start = (bf16[432,1152]{1,0:T(8,128)(2,1)S(1)}, bf16[432,1152]{1,0:T(8,128)(2,1)}, u32[]{:S(2)}) copy-start(bf16[432,1152]{1,0:T(8,128)(2,1)} %param.27) | copy-start | bytes 2985988
  7.2 75.2 %copy-start.2 = (bf16[1,128,1152]{2,1,0:T(8,128)(2,1)S(1)}, bf16[1,128,1152]{2,1,0:T(8,128)(2,1)}, u32[]{:S(2)}) copy-start(bf16[1,128,1152]{2,1,0:T(8,128)(2,1)} %param.17) | copy-start | bytes 884740
  7.2 72.4 %all-gather.4.cloned.1.call-start = ((), (), s32[]{:S(2)}) async-start(), calls=%async_computation.10 | async-start | bytes 6580224 | tf_op jit(solution)/shard_map/all_gather | solution.py:129
  13.9 78.0 %copy-start.34 = (f32[128]{0:T(128)}, f32[128]{0:T(128)S(1)}, u32[]{:S(2)}) copy-start(f32[128]{0:T(128)S(1)} %multiply_power_fusion) | copy-start | bytes 1540
  15.9 76.0 %copy-start.36 = (f32[128]{0:T(128)}, f32[128]{0:T(128)S(1)}, u32[]{:S(2)}) copy-start(f32[128]{0:T(128)S(1)} %convert_bitcast_fusion.1) | copy-start | bytes 1540
  16.2 100.7 %copy-start.24 = (pred[128,1024]{0,1:T(8,128)(4,1)}, pred[128,1024]{0,1:T(8,128)(4,1)S(1)}, u32[]{:S(2)}) copy-start(pred[128,1024]{0,1:T(8,128)(4,1)S(1)} %broadcast_compare_fusion.1) | copy-start | bytes 393220
  92.3 10.5 %copy-start.20 = (f32[128,128]{1,0:T(8,128)}, f32[128,128]{1,0:T(8,128)S(1)}, u32[]{:S(2)}) copy-start(f32[128,128]{1,0:T(8,128)S(1)} %get-tuple-element.61) | copy-start | bytes 196612
  92.3 10.5 %copy-start.22 = (f32[128,128]{1,0:T(8,128)}, f32[128,128]{1,0:T(8,128)S(1)}, u32[]{:S(2)}) copy-start(f32[128,128]{1,0:T(8,128)S(1)} %get-tuple-element.62) | copy-start | bytes 196612
  94.8 21.1 %all-to-all-start = ((bf16[8,128,512]{2,1,0:T(8,128)(2,1)}), bf16[8,128,512]{2,1,0:T(8,128)(2,1)S(1)}, u32[]{:S(2)}, u32[]{:S(2)}) async-start(bf16[8,128,512]{2,1,0:T(8,128)(2,1)} %broadcast_in_dim.52), calls=%async_computation | async-start | bytes 2097152 | tf_op jit(solution)/shard_map/all_to_all | solution.py:83
  99.1 77.9 %all-gather.6.cloned.1.call-start = ((), (), s32[]{:S(2)}) async-start(), calls=%async_computation.11 | async-start | bytes 5013504 | tf_op jit(solution)/shard_map/all_gather | solution.py:186
  102.9 13.9 %copy-start.25 = (f32[128,4,128]{2,0,1:T(8,128)}, f32[128,4,128]{2,0,1:T(8,128)S(1)}, u32[]{:S(2)}) copy-start(f32[128,4,128]{2,0,1:T(8,128)S(1)} %get-tuple-element.53) | copy-start | bytes 786436
  102.9 15.4 %copy-start.27 = (f32[128,4,128]{2,0,1:T(8,128)}, f32[128,4,128]{2,0,1:T(8,128)S(1)}, u32[]{:S(2)}) copy-start(f32[128,4,128]{2,0,1:T(8,128)S(1)} %get-tuple-element.54) | copy-start | bytes 786436
  117.7 212.6 %copy-start.29 = (f32[4,128]{1,0:T(4,128)}, f32[4,128]{1,0:T(4,128)S(1)}, u32[]{:S(2)}) copy-start(f32[4,128]{1,0:T(4,128)S(1)} %log_add_fusion) | copy-start | bytes 6148
  118.3 64.0 %copy-start.15 = (bf16[256,4,128]{2,0,1:T(8,128)(2,1)}, bf16[256,4,128]{2,0,1:T(8,128)(2,1)S(1)}, u32[]{:S(2)}) copy-start(bf16[256,4,128]{2,0,1:T(8,128)(2,1)S(1)} %convolution_convert_fusion.8) | copy-start | bytes 786436
  121.1 275.6 %copy-start.10 = (f32[128,1152]{1,0:T(8,128)}, f32[128,1152]{1,0:T(8,128)S(1)}, u32[]{:S(2)}) copy-start(f32[128,1152]{1,0:T(8,128)S(1)} %get-tuple-element.72) | copy-start | bytes 1769476
  121.1 275.6 %copy-start.31 = (f32[128]{0:T(128)}, f32[128]{0:T(128)S(1)}, u32[]{:S(2)}) copy-start(f32[128]{0:T(128)S(1)} %add_rsqrt_fusion.3) | copy-start | bytes 1540
  122.3 186.8 %all-gather.8.cloned.1.call-start = ((), (), s32[]{:S(2)}) async-start(), calls=%async_computation.12 | async-start | bytes 5013504 | tf_op jit(solution)/shard_map/all_gather | solution.py:199
  309.1 8.6 %copy-start.39 = (bf16[432,1152]{1,0:T(8,128)(2,1)S(1)}, bf16[432,1152]{1,0:T(8,128)(2,1)}, u32[]{:S(2)}) copy-start(bf16[432,1152]{1,0:T(8,128)(2,1)} %param.25) | copy-start | bytes 2985988
  325.2 68.1 %all-to-all-start.2 = ((bf16[16,128,1152]{2,1,0:T(8,128)(2,1)}), bf16[16,128,1152]{2,1,0:T(8,128)(2,1)}, u32[]{:S(2)}, u32[]{:S(2)}) async-start(bf16[16,128,1152]{2,1,0:T(8,128)(2,1)} %bitcast.184), calls=%async_computation.2 | async-start | bytes 9437184 | tf_op jit(solution)/shard_map/all_to_all | solution.py:77
  397.1 9.3 %copy-start.8 = (f32[128,1152]{1,0:T(8,128)}, f32[128,1152]{1,0:T(8,128)S(1)}, u32[]{:S(2)}) copy-start(f32[128,1152]{1,0:T(8,128)S(1)} %get-tuple-element.39) | copy-start | bytes 1769476
  409.8 8.5 %copy-start.16 = (bf16[256,4,128]{2,0,1:T(8,128)(2,1)S(1)}, bf16[256,4,128]{2,0,1:T(8,128)(2,1)}, u32[]{:S(2)}) copy-start(bf16[256,4,128]{2,0,1:T(8,128)(2,1)} %copy-done.15) | copy-start | bytes 786436
  409.8 20.7 %all-to-all-start.3 = ((bf16[8,128,512]{2,1,0:T(8,128)(2,1)}), bf16[8,128,512]{2,1,0:T(8,128)(2,1)S(1)}, u32[]{:S(2)}, u32[]{:S(2)}) async-start(bf16[8,128,512]{2,1,0:T(8,128)(2,1)} %pad_maximum_fusion.2), calls=%async_computation.3 | async-start | bytes 2097152 | tf_op jit(solution)/shard_map/all_to_all | solution.py:77
  414.5 159.4 %reduce-scatter.4.cloned.1.call-start = ((), (), s32[]{:S(2)}) async-start(), calls=%async_computation.13 | async-start | bytes 6266880
  418.3 12.4 %copy-start.35 = (f32[128]{0:T(128)S(1)}, f32[128]{0:T(128)}, u32[]{:S(2)}) copy-start(f32[128]{0:T(128)} %copy-done.34) | copy-start | bytes 1540
  418.3 12.4 %copy-start.37 = (f32[128]{0:T(128)S(1)}, f32[128]{0:T(128)}, u32[]{:S(2)}) copy-start(f32[128]{0:T(128)} %copy-done.36) | copy-start | bytes 1540
  418.3 13.1 %copy-start.33 = (f32[128]{0:T(128)S(1)}, f32[128]{0:T(128)}, u32[]{:S(2)}) copy-start(f32[128]{0:T(128)} %copy-done.32) | copy-start | bytes 1540
  510.3 47.7 %all-to-all-start.8 = ((bf16[8,162,1152]{2,1,0:T(8,128)(2,1)}), bf16[8,162,1152]{2,1,0:T(8,128)(2,1)}, u32[]{:S(2)}, u32[]{:S(2)}) async-start(bf16[8,162,1152]{2,1,0:T(8,128)(2,1)} %broadcast_in_dim.65), calls=%async_computation.8 | async-start | bytes 6193152 | tf_op jit(solution)/shard_map/all_to_all | solution.py:274
  558.0 15.8 %all-to-all-start.4 = ((bf16[16,8,72]{2,1,0:T(8,128)(2,1)}), bf16[16,8,72]{2,1,0:T(8,128)(2,1)S(1)}, u32[]{:S(2)}, u32[]{:S(2)}) async-start(bf16[16,8,72]{2,1,0:T(8,128)(2,1)} %copy.100), calls=%async_computation.4 | async-start | bytes 65536 | tf_op jit(solution)/shard_map/all_to_all | solution.py:269
  576.5 12.5 %all-to-all-start.5 = ((bf16[8,321,72]{1,2,0:T(8,128)(2,1)}), bf16[8,321,72]{1,2,0:T(8,128)(2,1)S(1)}, u32[]{:S(2)}, u32[]{:S(2)}) async-start(bf16[8,321,72]{1,2,0:T(8,128)(2,1)} %copy.102), calls=%async_computation.5 | async-start | bytes 884736 | tf_op jit(solution)/shard_map/all_to_all | solution.py:273
  580.0 13.4 %copy-start.9 = (f32[128,1152]{1,0:T(8,128)S(1)}, f32[128,1152]{1,0:T(8,128)}, u32[]{:S(2)}) copy-start(f32[128,1152]{1,0:T(8,128)} %copy-done.8) | copy-start | bytes 1769476
  589.1 16.0 %copy-start.1 = (bf16[432,1152]{1,0:T(8,128)(2,1)S(1)}, bf16[432,1152]{1,0:T(8,128)(2,1)}, u32[]{:S(2)}) copy-start(bf16[432,1152]{1,0:T(8,128)(2,1)} %param.27) | copy-start | bytes 2985988
  589.9 11.9 %all-to-all-start.6 = ((bf16[8,321,72]{1,2,0:T(8,128)(2,1)}), bf16[8,321,72]{1,2,0:T(8,128)(2,1)S(1)}, u32[]{:S(2)}, u32[]{:S(2)}) async-start(bf16[8,321,72]{1,2,0:T(8,128)(2,1)} %broadcast_in_dim.64), calls=%async_computation.6 | async-start | bytes 884736 | tf_op jit(solution)/shard_map/all_to_all | solution.py:274
  (29 other events, 119.4 us)
Sparse Core Ops, SparseCore 0:
  13.2 66.3 all-gather.3
  122.4 54.6 all-gather.5
  253.9 55.1 all-gather.7
  445.8 122.2 reduce-scatter.3

commit v6 on v5

--- a/solution.py
+++ b/solution.py
@@ -125,8 +125,9 @@
         axis=1,
     )
     gain_cols = jnp.pad(gain_cols, ((0, 0), (0, 128 - gain_cols.shape[1])))
-    packed = jnp.concatenate([w_query, w_key, w_value, w_output.T, gain_cols], axis=1)
+    packed = jnp.concatenate([w_query, w_key, w_value, gain_cols], axis=1)
     packed_all = lax.all_gather(packed, "fsdp", axis=0, tiled=True)
+    full_output_t = lax.all_gather(w_output.T, "fsdp", axis=0, tiled=True)
     o1 = qw
     o2 = o1 + kw
     o3 = o2 + kw
@@ -134,8 +135,7 @@
     full_query = packed_all[:, :o1]
     full_key = packed_all[:, o1:o2]
     full_value = packed_all[:, o2:o3]
-    full_output_t = packed_all[:, o3:o4]
-    gains_all = packed_all[:, o4:].astype(f32)
+    gains_all = packed_all[:, o3:].astype(f32)
     head_shard = gain_query.shape[0]
 
     def head_gain(col):
@@ -203,19 +203,19 @@
     shard_gate = jnp.einsum("tf,td->fd", grad_gate, rows_all, preferred_element_type=f32)
     shard_up = jnp.einsum("tf,td->fd", grad_up, rows_all, preferred_element_type=f32)
     shard_down = jnp.einsum("tf,td->fd", hidden, grad_all, preferred_element_type=f32)
-    grad_pre = a2a_sum(
-        (
-            jnp.dot(grad_gate, w_gate, preferred_element_type=f32)
-            + jnp.dot(grad_up, w_up, preferred_element_type=f32)
-        ).astype(jnp.bfloat16),
-        "fsdp",
-        groups,
-    )
+    pre_partial = (
+        jnp.dot(grad_gate, w_gate, preferred_element_type=f32)
+        + jnp.dot(grad_up, w_up, preferred_element_type=f32)
+    ).astype(jnp.bfloat16)
+    shard_gate, shard_up, shard_down, pre_partial = lax.optimization_barrier(
+        (shard_gate.astype(low), shard_up.astype(low), shard_down.astype(low), pre_partial)
+    )
+    grad_pre = a2a_sum(pre_partial, "fsdp", groups)
     grad_from_pre, grad_gain_pre = norm_backward(grad_pre, pre_unit, pre_inv, norm_pre)
     grad_residual = grad_out + grad_from_pre
     grad_branch_full, grad_gain_attn = norm_backward(grad_residual, attn_unit, attn_inv, norm_attn)
     grad_branch = grad_branch_full.astype(low)
-    term_output = jnp.einsum("tc,td->cd", attended, grad_branch, preferred_element_type=f32)
+    term_output = jnp.einsum("tc,td->dc", attended, grad_branch, preferred_element_type=f32)
     grad_attended = jnp.einsum(
         "td,dc->tc", grad_branch, full_output_t, preferred_element_type=f32
     ).astype(low)
@@ -231,6 +231,8 @@
     key_value_terms = jnp.concatenate([key_term, value_term], axis=1)
     grad_query_rot = jnp.einsum("hqk,kd->qhd", grad_scores, key_all, preferred_element_type=f32)
     summed_kv = a2a_sum(key_value_terms.astype(jnp.bfloat16), "ctx", parts)
+    ffn_sums = lax.psum((shard_gate, shard_up, shard_down), "ctx")
+    ffn_sums, summed_kv = lax.optimization_barrier((ffn_sums, summed_kv))
     grad_key_rot = summed_kv[:, :HD]
     grad_values = summed_kv[:, HD:].astype(low)
     grad_q_normed = rotate_back(grad_query_rot * scale, cosine[:, None, :], sine[:, None, :])
@@ -239,9 +241,9 @@
     grad_k_full, grad_gain_key = norm_backward(grad_k_normed, key_unit, key_inv, norm_key)
     grad_q_in = grad_q_full.reshape(local, H * HD).astype(low)
     grad_k_in = grad_k_full.astype(low)
-    term_query = jnp.einsum("tc,td->cd", grad_q_in, normed_in, preferred_element_type=f32)
-    term_key = jnp.einsum("tc,td->cd", grad_k_in, normed_in, preferred_element_type=f32)
-    term_value = jnp.einsum("tc,td->cd", grad_values, normed_in, preferred_element_type=f32)
+    term_query = jnp.einsum("tc,td->dc", grad_q_in, normed_in, preferred_element_type=f32)
+    term_key = jnp.einsum("tc,td->dc", grad_k_in, normed_in, preferred_element_type=f32)
+    term_value = jnp.einsum("tc,td->dc", grad_values, normed_in, preferred_element_type=f32)
     grad_normed = (
         jnp.einsum("tc,dc->td", grad_q_in, full_query, preferred_element_type=f32)
         + jnp.einsum("tc,dc->td", grad_k_in, full_key, preferred_element_type=f32)
@@ -262,34 +264,24 @@
             head_col(grad_gain_query),
             head_col(grad_gain_key),
         ],
-        axis=0,
-    )
-    gain_block = jnp.pad(gain_block, ((0, 8 - gain_block.shape[0]), (0, 0))).astype(low)
-    gain_block = jnp.transpose(gain_block.reshape(8, groups, width_shard), (1, 0, 2))
-    gain_shard = jnp.sum(lax.all_to_all(gain_block, "fsdp", 0, 0).astype(f32), axis=0)
+        axis=1,
+    )
+    gain_block = jnp.pad(gain_block, ((0, 0), (0, 8 - gain_block.shape[1])))
 
     def ctx_sum(x):
         chunks = x.reshape(parts, -1, x.shape[1])
         mine = jnp.sum(lax.all_to_all(chunks, "ctx", 0, 0).astype(f32), axis=0).astype(low)
         return lax.all_to_all(jnp.broadcast_to(mine[None], chunks.shape), "ctx", 0, 0).reshape(x.shape)
 
-    ffn_units = shard_gate.shape[0]
-    ffn_sums = ctx_sum(
-        jnp.concatenate([shard_gate, shard_up, shard_down], axis=0).astype(low)
-    ).astype(f32)
-    grad_packed = jnp.concatenate([term_query, term_key, term_value, term_output], axis=0).astype(low)
-    grad_shard = jnp.concatenate(
-        [
-            lax.psum_scatter(grad_packed, "fsdp", scatter_dimension=1, tiled=True),
-            gain_shard.astype(low),
-        ],
-        axis=0,
-    )
+    grad_packed = jnp.concatenate(
+        [term_query, term_key, term_value, term_output, gain_block], axis=1
+    ).astype(low)
+    grad_shard = a2a_sum(grad_packed, "fsdp", groups).astype(low).T
     totals = (
         ctx_sum(grad_shard),
-        ffn_sums[:ffn_units],
-        ffn_sums[ffn_units : 2 * ffn_units],
-        ffn_sums[2 * ffn_units :],
+        ffn_sums[0].astype(f32),
+        ffn_sums[1].astype(f32),
+        ffn_sums[2].astype(f32),
     )
     grad_shard = totals[0].astype(f32)
     grows = grad_shard[o4:]

time: 619 us -> 675 us (1.090)
  waiting for transfers between devices: 304 us -> 360 us
  blocking collectives: 105 us -> 141 us
  local copies, waits for them, and re-layouts: 54.4 us -> 26.9 us
  starting transfers between devices: 34.9 us -> 24.3 us
    psum x0 -> x1, waiting for transfers between devices: none -> 80.3 us  [body(): ffn_sums = lax.psum((shard_gate, shard_up, shard_down), 'ctx')]
    all_to_all x1 -> x2, blocking collectives: 61.1 us -> 141 us  [a2a_sum(): pieces = lax.all_to_all(x.reshape(count, -1, *x.shape[1:]), axis_name, 0, 0)]
    all_to_all x1 -> x0, blocking collectives: 44.3 us -> none  [ctx_sum(): lax.all_to_all(chunks, 'ctx', 0, 0).astype(f32)]
    all_to_all x2 -> x1, waiting for transfers between devices: 43 us -> 6.94 us  [ctx_sum(): lax.all_to_all(jnp.broadcast_to(mine[None], chunks.shape), 'ctx', 0, 0)]
    all_to_all x2, waiting for transfers between devices: 67.7 us -> 81.7 us  [a2a_sum(): pieces = lax.all_to_all(x.reshape(count, -1, *x.shape[1:]), axis_name, 0, 0)]
    unnamed x108 -> x139, local copies, waits for them, and re-layouts: 18 us -> 4.32 us
    all_gather x0 -> x1, waiting for transfers between devices: none -> 9.71 us  [body(): full_output_t = lax.all_gather(w_output.T, 'fsdp', axis=0, tiled=True)]
    all_gather x1, waiting for transfers between devices: 63.4 us -> 54 us  [body(): packed_all = lax.all_gather(packed, 'fsdp', axis=0, tiled=True)]
  transfers between devices with their start and end apart: 11 -> 10, of which waited for: 10 -> 10; matrix products, arithmetic and copies ran while one was open for 9% -> 8% of each run, Pallas kernels for 0% -> 0%
where the time goes in v6:
time: 675 us; the launch traced here: 668 us
  waiting for transfers between devices  360 us (53%)
  blocking collectives  141 us (21%)
  matrix products  69.1 us (10%)
  other arithmetic  32 us (5%)
  local copies, waits for them, and re-layouts  26.9 us (4%)
  starting transfers between devices  24.3 us (4%)
  between operations  15.1 us (2%)
    all_to_all x2, blocking collectives, a2a_sum(): pieces = lax.all_to_all(x.reshape(count, -1, *x.shape[1:]), axis_name, 0, 0)  141 us
    all_to_all x2, waiting for transfers between devices, a2a_sum(): pieces = lax.all_to_all(x.reshape(count, -1, *x.shape[1:]), axis_name, 0, 0)  81.7 us
    psum x1, waiting for transfers between devices, body(): ffn_sums = lax.psum((shard_gate, shard_up, shard_down), 'ctx')  80.3 us
    all_gather x1, waiting for transfers between devices, body(): rows_all = lax.all_gather(normed_pre, 'fsdp', axis=0, tiled=True)  56.9 us
    all_gather x1, waiting for transfers between devices, body(): grad_all = lax.all_gather(grad_ffn, 'fsdp', axis=0, tiled=True)  55.3 us
    all_gather x1, waiting for transfers between devices, body(): packed_all = lax.all_gather(packed, 'fsdp', axis=0, tiled=True)  54 us
  transfers between devices with their start and end apart: 10, of which 10 were waited for; matrix products, arithmetic and copies ran while one was open for 8% of the time, Pallas kernels for 0%

profile of v6, /device:TPU:0, one launch (start us, length us, event | category | flops | bytes accessed | tf_op | source)
XLA Modules:
  0.0 668.0 jit_solution(15433093147298678339)
XLA Ops:
  14.4 54.0 %all-gather.5.cloned.1.call-done = bf16[1152,1664]{1,0:T(8,128)(2,1)} async-done(((bf16[72,1664]{1,0:T(8,128)(2,1)}), bf16[1152,1664]{1,0:T(8,128)(2,1)}) %all-gather.5.cloned.1.call-update) | async-done | bytes 3833872 | tf_op jit(solution)/shard_map/all_gather | solution.py:129
  68.4 3.3 slice_bitcast_fusion
  71.7 4.3 copy.108
  84.7 4.3 all-to-all-start
  93.2 12.6 %all-to-all-done = bf16[8,128,512]{2,1,0:T(8,128)(2,1)S(1)} async-done(((bf16[8,128,512]{2,1,0:T(8,128)(2,1)}), bf16[8,128,512]{2,1,0:T(8,128)(2,1)S(1)}, u32[]{:S(2)}, u32[]{:S(2)}) %all-to-all-start) | async-done | bytes 1048608 | tf_op jit(solution)/shard_map/all_to_all | solution.py:83
  109.5 9.7 %all-gather.7.cloned.1.call-done = bf16[1152,1024]{1,0:T(8,128)(2,1)} async-done(((bf16[72,1024]{1,0:T(8,128)(2,1)}), bf16[1152,1024]{1,0:T(8,128)(2,1)}) %all-gather.7.cloned.1.call-update) | async-done | bytes 2359312 | tf_op jit(solution)/shard_map/all_gather | solution.py:130
  123.6 56.9 %all-gather.9.cloned.1.call-done = bf16[2048,1152]{1,0:T(8,128)(2,1)} async-done(((bf16[128,1152]{1,0:T(8,128)(2,1)}), bf16[2048,1152]{1,0:T(8,128)(2,1)}) %all-gather.9.cloned.1.call-update) | async-done | bytes 4718608 | tf_op jit(solution)/shard_map/all_gather | solution.py:186
  180.5 5.2 fusion.99
  185.8 4.6 multiply_convert_fusion.1
  190.5 3.2 convolution_convert_fusion
  193.7 61.1 %all_to_all.35 = bf16[16,128,1152]{2,1,0:T(8,128)(2,1)S(1)} all-to-all(bf16[16,128,1152]{2,1,0:T(8,128)(2,1)S(1)} %bitcast.205), channel_id=1, replica_groups=mesh['ctx'=8,'fsdp'=16] {'fsdp'}, dimensions={0} | all-to-all | bytes 9437184 | tf_op jit(solution)/shard_map/all_to_all | solution.py:77
  257.6 55.3 %all-gather.11.cloned.1.call-done = bf16[2048,1152]{1,0:T(8,128)(2,1)} async-done(((bf16[128,1152]{1,0:T(8,128)(2,1)}), bf16[2048,1152]{1,0:T(8,128)(2,1)}) %all-gather.11.cloned.1.call-update) | async-done | bytes 4718608 | tf_op jit(solution)/shard_map/all_gather | solution.py:199
  312.9 8.5 %multiply_convert_fusion = (bf16[2048,432]{0,1:T(8,128)(2,1)S(1)}, bf16[2048,432]{0,1:T(8,128)(2,1)S(1)}) fusion(f32[2048,432]{0,1:T(8,128)} %copy-done.61, f32[2048,432]{0,1:T(8,128)} %get-tuple-element.91, bf16[2048,1152]{1,0:T(8,128)(2,1)} %all-gather.11.cloned.1.call-done, bf16[432,1152]{1,0:T(8,128)(2,1)S(1)} %copy-done), kind=kOutput, calls=%fused_computation.13 | convolution fusion | flops 2058780672 | bytes 16330752 | tf_op jit(solution)/shard_map/td,fd->tf/dot_general | solution.py:200
  321.5 2.9 fusion.100
  324.5 4.8 add_convert_fusion
  329.3 3.4 convolution_convert_fusion.3
  332.7 3.4 convolution_convert_fusion.2
  336.1 3.4 convolution_convert_fusion.1
  339.5 4.7 all-to-all-start.2
  345.6 2.9 fusion.8
  349.2 70.5 %all-to-all-done.2 = bf16[16,128,1152]{2,1,0:T(8,128)(2,1)} async-done(((bf16[16,128,1152]{2,1,0:T(8,128)(2,1)}), bf16[16,128,1152]{2,1,0:T(8,128)(2,1)}, u32[]{:S(2)}, u32[]{:S(2)}) %all-to-all-start.2) | async-done | bytes 4718624 | tf_op jit(solution)/shard_map/all_to_all | solution.py:77
  419.6 3.1 convert_reduce_fusion
  429.8 6.3 all-to-all-start.3
  440.0 3.3 convert_dynamic-update-slice_fusion.1
  445.9 11.3 %all-to-all-done.3 = bf16[8,128,512]{2,1,0:T(8,128)(2,1)S(1)} async-done(((bf16[8,128,512]{2,1,0:T(8,128)(2,1)}), bf16[8,128,512]{2,1,0:T(8,128)(2,1)S(1)}, u32[]{:S(2)}, u32[]{:S(2)}) %all-to-all-start.3) | async-done | bytes 1048608 | tf_op jit(solution)/shard_map/all_to_all | solution.py:77
  457.3 80.3 %all-reduce.9.cloned.1.call-done = (bf16[432,1152]{1,0:T(8,128)(2,1)}, bf16[432,1152]{1,0:T(8,128)(2,1)}, bf16[432,1152]{1,0:T(8,128)(2,1)}) async-done(((bf16[432,1152]{1,0:T(8,128)(2,1)}, bf16[432,1152]{1,0:T(8,128)(2,1)}, bf16[432,1152]{1,0:T(8,128)(2,1)}), (bf16[432,1152]{1,0:T(8,128)(2,1)}, bf16[432,1152]{1,0:T(8,128)(2,1)}, bf16[432,1152]{1,0:T(8,128)(2,1)})) %all-reduce.9.cloned.1.call-update) | async-done | bytes 2986000 | tf_op jit(solution)/shard_map/psum | solution.py:234
  547.7 79.6 %all_to_all.36 = bf16[16,72,2568]{2,1,0:T(8,128)(2,1)} all-to-all(bf16[16,72,2568]{2,1,0:T(8,128)(2,1)} %constant_dynamic-update-slice_fusion), channel_id=1, replica_groups=mesh['ctx'=8,'fsdp'=16] {'fsdp'}, dimensions={0} | all-to-all | bytes 11833344 | tf_op jit(solution)/shard_map/all_to_all | solution.py:77
  627.3 3.9 reduce_sum.274
  632.6 4.1 all-to-all-start.5
  639.3 2.7 convert_element_type.211
  645.8 4.2 all-to-all-start.6
  651.0 6.9 %all-to-all-done.6 = bf16[8,321,72]{1,2,0:T(8,128)(2,1)S(1)} async-done(((bf16[8,321,72]{1,2,0:T(8,128)(2,1)}), bf16[8,321,72]{1,2,0:T(8,128)(2,1)S(1)}, u32[]{:S(2)}, u32[]{:S(2)}) %all-to-all-start.6) | async-done | bytes 369824 | tf_op jit(solution)/shard_map/all_to_all | solution.py:274
  (261 shorter events, 68.0 us)
Async XLA Ops:
  7.2 183.3 %copy-start = (bf16[432,1152]{1,0:T(8,128)(2,1)S(1)}, bf16[432,1152]{1,0:T(8,128)(2,1)}, u32[]{:S(2)}) copy-start(bf16[432,1152]{1,0:T(8,128)(2,1)} %param.27) | copy-start | bytes 2985988
  7.2 61.2 %all-gather.5.cloned.1.call-start = ((), (), s32[]{:S(2)}) async-start(), calls=%async_computation.7 | async-start | bytes 4073472 | tf_op jit(solution)/shard_map/all_gather | solution.py:129
  10.5 108.6 %all-gather.7.cloned.1.call-start = ((), (), s32[]{:S(2)}) async-start(), calls=%async_computation.8 | async-start | bytes 2506752 | tf_op jit(solution)/shard_map/all_gather | solution.py:130
  11.3 70.5 %copy-start.50 = (f32[128]{0:T(128)}, f32[128]{0:T(128)S(1)}, u32[]{:S(2)}) copy-start(f32[128]{0:T(128)S(1)} %multiply_power_fusion) | copy-start | bytes 1540
  12.3 63.8 %copy-start.54 = (s32[128]{0:T(128)}, s32[128]{0:T(128)S(1)}, u32[]{:S(2)}) copy-start(s32[128]{0:T(128)S(1)} %fusion.88) | copy-start | bytes 1540
  13.5 75.6 %copy-start.39 = (f32[128]{0:T(128)}, f32[128]{0:T(128)S(1)}, u32[]{:S(2)}) copy-start(f32[128]{0:T(128)S(1)} %add_rsqrt_fusion.5) | copy-start | bytes 1540
  14.2 67.7 %copy-start.52 = (f32[128]{0:T(128)}, f32[128]{0:T(128)S(1)}, u32[]{:S(2)}) copy-start(f32[128]{0:T(128)S(1)} %convert_bitcast_fusion.1) | copy-start | bytes 1540
  14.4 93.5 %copy-start.18 = (pred[128,1024]{0,1:T(8,128)(4,1)}, pred[128,1024]{0,1:T(8,128)(4,1)S(1)}, u32[]{:S(2)}) copy-start(pred[128,1024]{0,1:T(8,128)(4,1)S(1)} %broadcast_compare_fusion.1) | copy-start | bytes 393220
  84.7 21.1 %all-to-all-start = ((bf16[8,128,512]{2,1,0:T(8,128)(2,1)}), bf16[8,128,512]{2,1,0:T(8,128)(2,1)S(1)}, u32[]{:S(2)}, u32[]{:S(2)}) async-start(bf16[8,128,512]{2,1,0:T(8,128)(2,1)} %broadcast_in_dim.50), calls=%async_computation | async-start | bytes 2097152 | tf_op jit(solution)/shard_map/all_to_all | solution.py:83
  89.0 91.5 %all-gather.9.cloned.1.call-start = ((), (), s32[]{:S(2)}) async-start(), calls=%async_computation.9 | async-start | bytes 5013504 | tf_op jit(solution)/shard_map/all_gather | solution.py:186
  93.2 14.6 %copy-start.20 = (f32[128,4,128]{2,0,1:T(8,128)}, f32[128,4,128]{2,0,1:T(8,128)S(1)}, u32[]{:S(2)}) copy-start(f32[128,4,128]{2,0,1:T(8,128)S(1)} %get-tuple-element.69) | copy-start | bytes 786436
  108.8 13.0 %copy-start.26 = (f32[1152]{0:T(1024)S(1)}, f32[1152]{0:T(1024)}, u32[]{:S(2)}) copy-start(f32[1152]{0:T(1024)} %get-tuple-element.49) | copy-start | bytes 13828
  108.8 13.3 %copy-start.28 = (f32[1152]{0:T(1024)S(1)}, f32[1152]{0:T(1024)}, u32[]{:S(2)}) copy-start(f32[1152]{0:T(1024)} %get-tuple-element.48) | copy-start | bytes 13828
  121.8 64.0 %copy-start.44 = (f32[128]{0:T(128)}, f32[128]{0:T(128)S(1)}, u32[]{:S(2)}) copy-start(f32[128]{0:T(128)S(1)} %add_rsqrt_fusion.3) | copy-start | bytes 1540
  122.1 63.7 %copy-start.48 = (f32[128]{0:T(128)}, f32[128]{0:T(128)S(1)}, u32[]{:S(2)}) copy-start(f32[128]{0:T(128)S(1)} %add_rsqrt_fusion.2) | copy-start | bytes 1540
  123.0 189.9 %all-gather.11.cloned.1.call-start = ((), (), s32[]{:S(2)}) async-start(), calls=%async_computation.10 | async-start | bytes 5013504 | tf_op jit(solution)/shard_map/all_gather | solution.py:199
  339.5 80.1 %all-to-all-start.2 = ((bf16[16,128,1152]{2,1,0:T(8,128)(2,1)}), bf16[16,128,1152]{2,1,0:T(8,128)(2,1)}, u32[]{:S(2)}, u32[]{:S(2)}) async-start(bf16[16,128,1152]{2,1,0:T(8,128)(2,1)} %bitcast.204), calls=%async_computation.2 | async-start | bytes 9437184 | tf_op jit(solution)/shard_map/all_to_all | solution.py:77
  344.3 193.3 %all-reduce.9.cloned.1.call-start = ((), (), s32[]{:S(2)}) async-start(), calls=%async_computation.11 | async-start | bytes 5971968 | tf_op jit(solution)/shard_map/psum | solution.py:234
  349.1 73.6 %copy-start.29 = (f32[1152]{0:T(1024)S(1)}, f32[1152]{0:T(1024)}, u32[]{:S(2)}) copy-start(f32[1152]{0:T(1024)} %get-tuple-element.48) | copy-start | bytes 13828
  349.1 73.6 %copy-start.49 = (f32[128]{0:T(128)S(1)}, f32[128]{0:T(128)}, u32[]{:S(2)}) copy-start(f32[128]{0:T(128)} %copy-done.48) | copy-start | bytes 1540
  349.2 73.9 %copy-start.27 = (f32[1152]{0:T(1024)S(1)}, f32[1152]{0:T(1024)}, u32[]{:S(2)}) copy-start(f32[1152]{0:T(1024)} %get-tuple-element.49) | copy-start | bytes 13828
  349.2 73.9 %copy-start.45 = (f32[128]{0:T(128)S(1)}, f32[128]{0:T(128)}, u32[]{:S(2)}) copy-start(f32[128]{0:T(128)} %copy-done.44) | copy-start | bytes 1540
  429.8 27.3 %all-to-all-start.3 = ((bf16[8,128,512]{2,1,0:T(8,128)(2,1)}), bf16[8,128,512]{2,1,0:T(8,128)(2,1)S(1)}, u32[]{:S(2)}, u32[]{:S(2)}) async-start(bf16[8,128,512]{2,1,0:T(8,128)(2,1)} %pad_maximum_fusion), calls=%async_computation.3 | async-start | bytes 2097152 | tf_op jit(solution)/shard_map/all_to_all | solution.py:77
  440.0 97.6 %copy-start.51 = (f32[128]{0:T(128)S(1)}, f32[128]{0:T(128)}, u32[]{:S(2)}) copy-start(f32[128]{0:T(128)} %copy-done.50) | copy-start | bytes 1540
  440.0 97.6 %copy-start.53 = (f32[128]{0:T(128)S(1)}, f32[128]{0:T(128)}, u32[]{:S(2)}) copy-start(f32[128]{0:T(128)} %copy-done.52) | copy-start | bytes 1540
  440.0 97.9 %copy-start.10 = (f32[128,256]{1,0:T(8,128)S(1)}, f32[128,256]{1,0:T(8,128)}, u32[]{:S(2)}) copy-start(f32[128,256]{1,0:T(8,128)} %copy-done.9) | copy-start | bytes 393220
  440.0 97.9 %copy-start.35 = (f32[256]{0:T(256)S(1)}, f32[256]{0:T(256)}, u32[]{:S(2)}) copy-start(f32[256]{0:T(256)} %copy-done.34) | copy-start | bytes 3076
  440.0 97.9 %copy-start.47 = (f32[128]{0:T(128)S(1)}, f32[128]{0:T(128)}, u32[]{:S(2)}) copy-start(f32[128]{0:T(128)} %copy-done.46) | copy-start | bytes 1540
  445.9 95.3 %copy-start.41 = (f32[128]{0:T(128)S(1)}, f32[128]{0:T(128)}, u32[]{:S(2)}) copy-start(f32[128]{0:T(128)} %copy-done.39) | copy-start | bytes 1540
  632.6 12.4 %all-to-all-start.5 = ((bf16[8,321,72]{1,2,0:T(8,128)(2,1)}), bf16[8,321,72]{1,2,0:T(8,128)(2,1)S(1)}, u32[]{:S(2)}, u32[]{:S(2)}) async-start(bf16[8,321,72]{1,2,0:T(8,128)(2,1)} %copy.124), calls=%async_computation.5 | async-start | bytes 884736 | tf_op jit(solution)/shard_map/all_to_all | solution.py:273
  645.0 16.2 %copy-start.1 = (bf16[432,1152]{1,0:T(8,128)(2,1)S(1)}, bf16[432,1152]{1,0:T(8,128)(2,1)}, u32[]{:S(2)}) copy-start(bf16[432,1152]{1,0:T(8,128)(2,1)} %param.27) | copy-start | bytes 2985988
  645.8 12.1 %all-to-all-start.6 = ((bf16[8,321,72]{1,2,0:T(8,128)(2,1)}), bf16[8,321,72]{1,2,0:T(8,128)(2,1)S(1)}, u32[]{:S(2)}, u32[]{:S(2)}) async-start(bf16[8,321,72]{1,2,0:T(8,128)(2,1)} %broadcast_in_dim.100), calls=%async_computation.6 | async-start | bytes 884736 | tf_op jit(solution)/shard_map/all_to_all | solution.py:274
  (46 other events, 269.3 us)
Sparse Core Ops, SparseCore 0:
  11.1 57.3 all-gather.4
  70.8 48.2 all-gather.6
  123.1 57.3 all-gather.8
  257.8 55.1 all-gather.10
  349.3 188.2 all-reduce.8

commit v7 on v5

--- a/solution.py
+++ b/solution.py
@@ -125,8 +125,9 @@
         axis=1,
     )
     gain_cols = jnp.pad(gain_cols, ((0, 0), (0, 128 - gain_cols.shape[1])))
-    packed = jnp.concatenate([w_query, w_key, w_value, w_output.T, gain_cols], axis=1)
+    packed = jnp.concatenate([w_query, w_key, w_value, gain_cols], axis=1)
     packed_all = lax.all_gather(packed, "fsdp", axis=0, tiled=True)
+    full_output_t = lax.all_gather(w_output.T, "fsdp", axis=0, tiled=True)
     o1 = qw
     o2 = o1 + kw
     o3 = o2 + kw
@@ -134,8 +135,7 @@
     full_query = packed_all[:, :o1]
     full_key = packed_all[:, o1:o2]
     full_value = packed_all[:, o2:o3]
-    full_output_t = packed_all[:, o3:o4]
-    gains_all = packed_all[:, o4:].astype(f32)
+    gains_all = packed_all[:, o3:].astype(f32)
     head_shard = gain_query.shape[0]
 
     def head_gain(col):
@@ -239,6 +239,10 @@
     grad_k_full, grad_gain_key = norm_backward(grad_k_normed, key_unit, key_inv, norm_key)
     grad_q_in = grad_q_full.reshape(local, H * HD).astype(low)
     grad_k_in = grad_k_full.astype(low)
+    output_shard = lax.psum_scatter(term_output.astype(low), "fsdp", scatter_dimension=1, tiled=True)
+    output_shard, grad_q_in, grad_k_in, grad_values = lax.optimization_barrier(
+        (output_shard, grad_q_in, grad_k_in, grad_values)
+    )
     term_query = jnp.einsum("tc,td->cd", grad_q_in, normed_in, preferred_element_type=f32)
     term_key = jnp.einsum("tc,td->cd", grad_k_in, normed_in, preferred_element_type=f32)
     term_value = jnp.einsum("tc,td->cd", grad_values, normed_in, preferred_element_type=f32)
@@ -277,10 +281,11 @@
     ffn_sums = ctx_sum(
         jnp.concatenate([shard_gate, shard_up, shard_down], axis=0).astype(low)
     ).astype(f32)
-    grad_packed = jnp.concatenate([term_query, term_key, term_value, term_output], axis=0).astype(low)
+    grad_packed = jnp.concatenate([term_query, term_key, term_value], axis=0).astype(low)
     grad_shard = jnp.concatenate(
         [
             lax.psum_scatter(grad_packed, "fsdp", scatter_dimension=1, tiled=True),
+            output_shard,
             gain_shard.astype(low),
         ],
         axis=0,

time: 619 us -> 648 us (1.047)
  waiting for transfers between devices: 304 us -> 342 us
  local copies, waits for them, and re-layouts: 54.4 us -> 46.9 us
    reduce_scatter x0 -> x1, waiting for transfers between devices: none -> 41.6 us  [body(): lax.psum_scatter(term_output.astype(low), 'fsdp', scatter_dimension=1, ti...]
    all_gather x0 -> x1, waiting for transfers between devices: none -> 11.8 us  [body(): full_output_t = lax.all_gather(w_output.T, 'fsdp', axis=0, tiled=True)]
    all_gather x1, waiting for transfers between devices: 63.4 us -> 54.1 us  [body(): packed_all = lax.all_gather(packed, 'fsdp', axis=0, tiled=True)]
    all_to_all x2, waiting for transfers between devices: 67.7 us -> 59.5 us  [a2a_sum(): pieces = lax.all_to_all(x.reshape(count, -1, *x.shape[1:]), axis_name, 0, 0)]
    unnamed x108 -> x92, local copies, waits for them, and re-layouts: 18 us -> 11.4 us
  transfers between devices with their start and end apart: 11 -> 13, of which waited for: 10 -> 12; matrix products, arithmetic and copies ran while one was open for 9% -> 13% of each run, Pallas kernels for 0% -> 0%
where the time goes in v7:
time: 648 us; the launch traced here: 641 us
  waiting for transfers between devices  342 us (53%)
  blocking collectives  102 us (16%)
  matrix products  68.6 us (11%)
  local copies, waits for them, and re-layouts  46.9 us (7%)
  other arithmetic  33.7 us (5%)
  starting transfers between devices  32.2 us (5%)
  between operations  15.5 us (2%)
    all_to_all x1, blocking collectives, a2a_sum(): pieces = lax.all_to_all(x.reshape(count, -1, *x.shape[1:]), axis_name, 0, 0)  61.1 us
    all_to_all x2, waiting for transfers between devices, a2a_sum(): pieces = lax.all_to_all(x.reshape(count, -1, *x.shape[1:]), axis_name, 0, 0)  59.5 us
    all_gather x1, waiting for transfers between devices, body(): rows_all = lax.all_gather(normed_pre, 'fsdp', axis=0, tiled=True)  56.2 us
    all_gather x1, waiting for transfers between devices, body(): grad_all = lax.all_gather(grad_ffn, 'fsdp', axis=0, tiled=True)  55.3 us
    all_gather x1, waiting for transfers between devices, body(): packed_all = lax.all_gather(packed, 'fsdp', axis=0, tiled=True)  54.1 us
    all_to_all x2, waiting for transfers between devices, ctx_sum(): lax.all_to_all(jnp.broadcast_to(mine[None], chunks.shape), 'ctx', 0, 0)  42.6 us
    reduce_scatter x1, waiting for transfers between devices, body(): lax.psum_scatter(term_output.astype(low), 'fsdp', scatter_dimension=1, ti...  41.6 us
    all_to_all x1, blocking collectives, ctx_sum(): lax.all_to_all(chunks, 'ctx', 0, 0).astype(f32)  40.9 us
  transfers between devices with their start and end apart: 13, of which 12 were waited for; matrix products, arithmetic and copies ran while one was open for 13% of the time, Pallas kernels for 0%

profile of v7, /device:TPU:0, one launch (start us, length us, event | category | flops | bytes accessed | tf_op | source)
XLA Modules:
  0.0 640.6 jit_solution(16960250128443830481)
XLA Ops:
  14.4 54.1 %all-gather.5.cloned.1.call-done = bf16[1152,1664]{1,0:T(8,128)(2,1)} async-done(((bf16[72,1664]{1,0:T(8,128)(2,1)}), bf16[1152,1664]{1,0:T(8,128)(2,1)}) %all-gather.5.cloned.1.call-update) | async-done | bytes 3833872 | tf_op jit(solution)/shard_map/all_gather | solution.py:129
  74.7 4.4 copy.94
  83.7 4.4 all-to-all-start
  91.8 13.0 %all-to-all-done = bf16[8,128,512]{2,1,0:T(8,128)(2,1)S(1)} async-done(((bf16[8,128,512]{2,1,0:T(8,128)(2,1)}), bf16[8,128,512]{2,1,0:T(8,128)(2,1)S(1)}, u32[]{:S(2)}, u32[]{:S(2)}) %all-to-all-start) | async-done | bytes 1048608 | tf_op jit(solution)/shard_map/all_to_all | solution.py:83
  107.3 11.8 %all-gather.7.cloned.1.call-done = bf16[1152,1024]{1,0:T(8,128)(2,1)} async-done(((bf16[72,1024]{1,0:T(8,128)(2,1)}), bf16[1152,1024]{1,0:T(8,128)(2,1)}) %all-gather.7.cloned.1.call-update) | async-done | bytes 2359312 | tf_op jit(solution)/shard_map/all_gather | solution.py:130
  123.5 56.2 %all-gather.9.cloned.1.call-done = bf16[2048,1152]{1,0:T(8,128)(2,1)} async-done(((bf16[128,1152]{1,0:T(8,128)(2,1)}), bf16[2048,1152]{1,0:T(8,128)(2,1)}) %all-gather.9.cloned.1.call-update) | async-done | bytes 4718608 | tf_op jit(solution)/shard_map/all_gather | solution.py:186
  179.8 5.2 fusion.99
  185.1 4.6 multiply_convert_fusion.1
  192.9 61.1 %all_to_all.45 = bf16[16,128,1152]{2,1,0:T(8,128)(2,1)S(1)} all-to-all(bf16[16,128,1152]{2,1,0:T(8,128)(2,1)S(1)} %bitcast.187), channel_id=1, replica_groups=mesh['ctx'=8,'fsdp'=16] {'fsdp'}, dimensions={0} | all-to-all | bytes 9437184 | tf_op jit(solution)/shard_map/all_to_all | solution.py:77
  256.4 55.3 %all-gather.11.cloned.1.call-done = bf16[2048,1152]{1,0:T(8,128)(2,1)} async-done(((bf16[128,1152]{1,0:T(8,128)(2,1)}), bf16[2048,1152]{1,0:T(8,128)(2,1)}) %all-gather.11.cloned.1.call-update) | async-done | bytes 4718608 | tf_op jit(solution)/shard_map/all_gather | solution.py:199
  311.7 8.5 %multiply_convert_fusion = (bf16[2048,432]{0,1:T(8,128)(2,1)S(1)}, bf16[2048,432]{0,1:T(8,128)(2,1)S(1)}) fusion(f32[2048,432]{0,1:T(8,128)} %copy-done.40, f32[2048,432]{0,1:T(8,128)} %get-tuple-element.82, bf16[2048,1152]{1,0:T(8,128)(2,1)} %all-gather.11.cloned.1.call-done, bf16[432,1152]{1,0:T(8,128)(2,1)S(1)} %copy-done), kind=kOutput, calls=%fused_computation.16 | convolution fusion | flops 2058780672 | bytes 16330752 | tf_op jit(solution)/shard_map/td,fd->tf/dot_general | solution.py:200
  323.2 4.6 add_convert_fusion
  327.8 4.6 all-to-all-start.2
  336.0 6.5 %convolution_convert_fusion.3 = bf16[432,1152]{1,0:T(8,128)(2,1)} fusion(bf16[2048,432]{0,1:T(8,128)(2,1)} %copy-done.41, bf16[2048,1152]{1,0:T(8,128)(2,1)} %all-gather.11.cloned.1.call-done), kind=kOutput, calls=%fused_computation.20 | convolution fusion | flops 2038929408 | bytes 7483392 | tf_op jit(solution)/shard_map/tf,td->fd/dot_general | solution.py:205
  342.5 3.4 convolution_convert_fusion.4
  349.3 46.4 %all-to-all-done.2 = bf16[16,128,1152]{2,1,0:T(8,128)(2,1)} async-done(((bf16[16,128,1152]{2,1,0:T(8,128)(2,1)}), bf16[16,128,1152]{2,1,0:T(8,128)(2,1)}, u32[]{:S(2)}, u32[]{:S(2)}) %all-to-all-start.2) | async-done | bytes 4718624 | tf_op jit(solution)/shard_map/all_to_all | solution.py:77
  411.2 4.5 all-to-all-start.3
  418.6 13.1 %all-to-all-done.3 = bf16[8,128,512]{2,1,0:T(8,128)(2,1)S(1)} async-done(((bf16[8,128,512]{2,1,0:T(8,128)(2,1)}), bf16[8,128,512]{2,1,0:T(8,128)(2,1)S(1)}, u32[]{:S(2)}, u32[]{:S(2)}) %all-to-all-start.3) | async-done | bytes 1048608 | tf_op jit(solution)/shard_map/all_to_all | solution.py:77
  433.3 41.6 %reduce-scatter.5.cloned.1.call-done = bf16[1024,72]{0,1:T(8,128)(2,1)} async-done(((bf16[1024,1152]{0,1:T(8,128)(2,1)}), bf16[1024,72]{0,1:T(8,128)(2,1)}) %reduce-scatter.5.cloned.1.call-update) | async-done | bytes 147472 | tf_op jit(solution)/shard_map/reduce_scatter | solution.py:242
  476.5 6.4 %pad_maximum_fusion = bf16[1536,1152]{1,0:T(8,128)(2,1)} fusion(bf16[256,1152]{1,0:T(8,128)(2,1)S(1)} %convolution_convert_fusion.6, bf16[256,1152]{1,0:T(8,128)(2,1)S(1)} %convolution_convert_fusion.7, bf16[1024,1152]{1,0:T(8,128)(2,1)S(1)} %convolution_convert_fusion.1), kind=kLoop, calls=%fused_computation.15 | loop fusion | flops 10616832 | bytes 7077888 | tf_op jit(solution)/shard_map/concatenate | solution.py:284
  482.9 5.8 copy.122
  493.2 3.4 convert_element_type.203
  496.6 40.9 %all_to_all.46 = bf16[8,162,1152]{2,1,0:T(8,128)(2,1)} all-to-all(bf16[8,162,1152]{2,1,0:T(8,128)(2,1)} %convert_element_type.203), channel_id=1, replica_groups=mesh['ctx'=8,'fsdp'=16] {'ctx'}, dimensions={0} | all-to-all | bytes 5971968 | tf_op jit(solution)/shard_map/all_to_all | solution.py:277
  541.8 5.7 all-to-all-start.8
  554.3 35.2 %all-to-all-done.8 = bf16[8,162,1152]{2,1,0:T(8,128)(2,1)} async-done(((bf16[8,162,1152]{2,1,0:T(8,128)(2,1)}), bf16[8,162,1152]{2,1,0:T(8,128)(2,1)}, u32[]{:S(2)}, u32[]{:S(2)}) %all-to-all-start.8) | async-done | bytes 2986016 | tf_op jit(solution)/shard_map/all_to_all | solution.py:278
  589.6 4.9 all-to-all-start.4
  594.5 4.3 reshape.345
  604.6 3.5 all-to-all-start.5
  608.1 5.5 fusion.97
  613.7 3.5 all-to-all-done.5
  618.1 3.5 all-to-all-start.6
  622.5 7.4 %all-to-all-done.6 = bf16[8,321,72]{1,2,0:T(8,128)(2,1)S(1)} async-done(((bf16[8,321,72]{1,2,0:T(8,128)(2,1)}), bf16[8,321,72]{1,2,0:T(8,128)(2,1)S(1)}, u32[]{:S(2)}, u32[]{:S(2)}) %all-to-all-start.6) | async-done | bytes 369824 | tf_op jit(solution)/shard_map/all_to_all | solution.py:278
  (223 shorter events, 91.6 us)
Async XLA Ops:
  7.2 182.5 %copy-start = (bf16[432,1152]{1,0:T(8,128)(2,1)S(1)}, bf16[432,1152]{1,0:T(8,128)(2,1)}, u32[]{:S(2)}) copy-start(bf16[432,1152]{1,0:T(8,128)(2,1)} %param.27) | copy-start | bytes 2985988
  7.2 61.2 %all-gather.5.cloned.1.call-start = ((), (), s32[]{:S(2)}) async-start(), calls=%async_computation.11 | async-start | bytes 4073472 | tf_op jit(solution)/shard_map/all_gather | solution.py:129
  10.5 108.6 %all-gather.7.cloned.1.call-start = ((), (), s32[]{:S(2)}) async-start(), calls=%async_computation.12 | async-start | bytes 2506752 | tf_op jit(solution)/shard_map/all_gather | solution.py:130
  11.3 69.5 %copy-start.28 = (f32[128]{0:T(128)}, f32[128]{0:T(128)S(1)}, u32[]{:S(2)}) copy-start(f32[128]{0:T(128)S(1)} %multiply_power_fusion) | copy-start | bytes 1540
  13.1 67.7 %copy-start.30 = (f32[128]{0:T(128)}, f32[128]{0:T(128)S(1)}, u32[]{:S(2)}) copy-start(f32[128]{0:T(128)S(1)} %convert_bitcast_fusion.1) | copy-start | bytes 1540
  14.4 91.3 %copy-start.22 = (pred[128,1024]{0,1:T(8,128)(4,1)}, pred[128,1024]{0,1:T(8,128)(4,1)S(1)}, u32[]{:S(2)}) copy-start(pred[128,1024]{0,1:T(8,128)(4,1)S(1)} %broadcast_compare_fusion.1) | copy-start | bytes 393220
  81.1 10.5 %copy-start.16 = (f32[128,128]{1,0:T(8,128)}, f32[128,128]{1,0:T(8,128)S(1)}, u32[]{:S(2)}) copy-start(f32[128,128]{1,0:T(8,128)S(1)} %get-tuple-element.69) | copy-start | bytes 196612
  81.2 10.5 %copy-start.18 = (f32[128,128]{1,0:T(8,128)}, f32[128,128]{1,0:T(8,128)S(1)}, u32[]{:S(2)}) copy-start(f32[128,128]{1,0:T(8,128)S(1)} %get-tuple-element.70) | copy-start | bytes 196612
  83.7 21.1 %all-to-all-start = ((bf16[8,128,512]{2,1,0:T(8,128)(2,1)}), bf16[8,128,512]{2,1,0:T(8,128)(2,1)S(1)}, u32[]{:S(2)}, u32[]{:S(2)}) async-start(bf16[8,128,512]{2,1,0:T(8,128)(2,1)} %broadcast_in_dim.52), calls=%async_computation | async-start | bytes 2097152 | tf_op jit(solution)/shard_map/all_to_all | solution.py:83
  88.0 91.8 %all-gather.9.cloned.1.call-start = ((), (), s32[]{:S(2)}) async-start(), calls=%async_computation.13 | async-start | bytes 5013504 | tf_op jit(solution)/shard_map/all_gather | solution.py:186
  91.7 13.9 %copy-start.23 = (f32[128,4,128]{2,0,1:T(8,128)}, f32[128,4,128]{2,0,1:T(8,128)S(1)}, u32[]{:S(2)}) copy-start(f32[128,4,128]{2,0,1:T(8,128)S(1)} %get-tuple-element.61) | copy-start | bytes 786436
  91.8 13.9 %copy-start.25 = (f32[128,4,128]{2,0,1:T(8,128)}, f32[128,4,128]{2,0,1:T(8,128)S(1)}, u32[]{:S(2)}) copy-start(f32[128,4,128]{2,0,1:T(8,128)S(1)} %get-tuple-element.62) | copy-start | bytes 786436
  107.3 292.4 %copy-start.11 = (bf16[256,4,128]{2,0,1:T(8,128)(2,1)}, bf16[256,4,128]{2,0,1:T(8,128)(2,1)S(1)}, u32[]{:S(2)}) copy-start(bf16[256,4,128]{2,0,1:T(8,128)(2,1)S(1)} %convolution_convert_fusion.9) | copy-start | bytes 786436
  123.0 188.7 %all-gather.11.cloned.1.call-start = ((), (), s32[]{:S(2)}) async-start(), calls=%async_computation.14 | async-start | bytes 5013504 | tf_op jit(solution)/shard_map/all_gather | solution.py:199
  311.7 8.6 %copy-start.32 = (bf16[432,1152]{1,0:T(8,128)(2,1)S(1)}, bf16[432,1152]{1,0:T(8,128)(2,1)}, u32[]{:S(2)}) copy-start(bf16[432,1152]{1,0:T(8,128)(2,1)} %param.25) | copy-start | bytes 2985988
  327.8 67.9 %all-to-all-start.2 = ((bf16[16,128,1152]{2,1,0:T(8,128)(2,1)}), bf16[16,128,1152]{2,1,0:T(8,128)(2,1)}, u32[]{:S(2)}, u32[]{:S(2)}) async-start(bf16[16,128,1152]{2,1,0:T(8,128)(2,1)} %bitcast.186), calls=%async_computation.2 | async-start | bytes 9437184 | tf_op jit(solution)/shard_map/all_to_all | solution.py:77
  332.4 142.5 %reduce-scatter.5.cloned.1.call-start = ((), (), s32[]{:S(2)}) async-start(), calls=%async_computation.15 | async-start | bytes 2506752 | tf_op jit(solution)/shard_map/reduce_scatter | solution.py:242
  332.9 9.6 %slice-start = ((s8[4718592]{0:T(1024)(128)(4,1)}), s8[4194304]{0:T(1024)(128)(4,1)S(1)}, s32[]{:S(2)}) async-start(s8[4718592]{0:T(1024)(128)(4,1)} %bitcast.210), calls=%async_computation.17 | async-start | bytes 8388608
  336.0 6.5 %copy-start.39 = (bf16[2048,432]{0,1:T(8,128)(2,1)S(1)}, bf16[2048,432]{0,1:T(8,128)(2,1)}, u32[]{:S(2)}) copy-start(bf16[2048,432]{0,1:T(8,128)(2,1)} %copy-done.38) | copy-start | bytes 5308420
  410.1 7.7 %copy-start.17 = (f32[128,128]{1,0:T(8,128)S(1)}, f32[128,128]{1,0:T(8,128)}, u32[]{:S(2)}) copy-start(f32[128,128]{1,0:T(8,128)} %copy-done.16) | copy-start | bytes 196612
  410.1 7.8 %copy-start.19 = (f32[128,128]{1,0:T(8,128)S(1)}, f32[128,128]{1,0:T(8,128)}, u32[]{:S(2)}) copy-start(f32[128,128]{1,0:T(8,128)} %copy-done.18) | copy-start | bytes 196612
  410.1 7.8 %copy-start.6 = (f32[128,4,256]{2,0,1:T(8,128)S(1)}, f32[128,4,256]{2,0,1:T(8,128)}, u32[]{:S(2)}) copy-start(f32[128,4,256]{2,0,1:T(8,128)} %copy-done.5) | copy-start | bytes 1572868
  411.2 20.6 %all-to-all-start.3 = ((bf16[8,128,512]{2,1,0:T(8,128)(2,1)}), bf16[8,128,512]{2,1,0:T(8,128)(2,1)S(1)}, u32[]{:S(2)}, u32[]{:S(2)}) async-start(bf16[8,128,512]{2,1,0:T(8,128)(2,1)} %pad_maximum_fusion.2), calls=%async_computation.4 | async-start | bytes 2097152 | tf_op jit(solution)/shard_map/all_to_all | solution.py:77
  415.7 16.2 %copy-start.29 = (f32[128]{0:T(128)S(1)}, f32[128]{0:T(128)}, u32[]{:S(2)}) copy-start(f32[128]{0:T(128)} %copy-done.28) | copy-start | bytes 1540
  415.7 186.4 %reduce-scatter.7.cloned.1.call-start = ((), (), s32[]{:S(2)}) async-start(), calls=%async_computation.16 | async-start | bytes 3760128
  431.9 51.0 %copy-start.20 = (bf16[128,256]{1,0:T(8,128)(2,1)}, bf16[128,256]{1,0:T(8,128)(2,1)S(1)}, u32[]{:S(2)}) copy-start(bf16[128,256]{1,0:T(8,128)(2,1)S(1)} %slice.241) | copy-start | bytes 196612
  541.8 47.7 %all-to-all-start.8 = ((bf16[8,162,1152]{2,1,0:T(8,128)(2,1)}), bf16[8,162,1152]{2,1,0:T(8,128)(2,1)}, u32[]{:S(2)}, u32[]{:S(2)}) async-start(bf16[8,162,1152]{2,1,0:T(8,128)(2,1)} %broadcast_in_dim.65), calls=%async_computation.9 | async-start | bytes 6193152 | tf_op jit(solution)/shard_map/all_to_all | solution.py:278
  589.6 12.6 %all-to-all-start.4 = ((bf16[16,8,72]{2,1,0:T(8,128)(2,1)}), bf16[16,8,72]{2,1,0:T(8,128)(2,1)S(1)}, u32[]{:S(2)}, u32[]{:S(2)}) async-start(bf16[16,8,72]{2,1,0:T(8,128)(2,1)} %copy.104), calls=%async_computation.5 | async-start | bytes 65536 | tf_op jit(solution)/shard_map/all_to_all | solution.py:273
  604.6 12.5 %all-to-all-start.5 = ((bf16[8,321,72]{1,2,0:T(8,128)(2,1)}), bf16[8,321,72]{1,2,0:T(8,128)(2,1)S(1)}, u32[]{:S(2)}, u32[]{:S(2)}) async-start(bf16[8,321,72]{1,2,0:T(8,128)(2,1)} %copy.107), calls=%async_computation.6 | async-start | bytes 884736 | tf_op jit(solution)/shard_map/all_to_all | solution.py:277
  608.1 13.4 %copy-start.8 = (f32[128,1152]{1,0:T(8,128)S(1)}, f32[128,1152]{1,0:T(8,128)}, u32[]{:S(2)}) copy-start(f32[128,1152]{1,0:T(8,128)} %copy-done.7) | copy-start | bytes 1769476
  617.3 16.0 %copy-start.1 = (bf16[432,1152]{1,0:T(8,128)(2,1)S(1)}, bf16[432,1152]{1,0:T(8,128)(2,1)}, u32[]{:S(2)}) copy-start(bf16[432,1152]{1,0:T(8,128)(2,1)} %param.27) | copy-start | bytes 2985988
  618.1 11.9 %all-to-all-start.6 = ((bf16[8,321,72]{1,2,0:T(8,128)(2,1)}), bf16[8,321,72]{1,2,0:T(8,128)(2,1)S(1)}, u32[]{:S(2)}, u32[]{:S(2)}) async-start(bf16[8,321,72]{1,2,0:T(8,128)(2,1)} %broadcast_in_dim.64), calls=%async_computation.7 | async-start | bytes 884736 | tf_op jit(solution)/shard_map/all_to_all | solution.py:278
  (25 other events, 85.5 us)
Sparse Core Ops, SparseCore 0:
  11.1 57.3 all-gather.4
  70.9 48.2 all-gather.6
  123.1 56.6 all-gather.8
  256.5 55.1 all-gather.10
  402.1 72.6 reduce-scatter.4
  488.8 90.9 reduce-scatter.6

commit v8 on v5

--- a/solution.py
+++ b/solution.py
@@ -125,8 +125,9 @@
         axis=1,
     )
     gain_cols = jnp.pad(gain_cols, ((0, 0), (0, 128 - gain_cols.shape[1])))
-    packed = jnp.concatenate([w_query, w_key, w_value, w_output.T, gain_cols], axis=1)
+    packed = jnp.concatenate([w_query, w_key, w_value, gain_cols], axis=1)
     packed_all = lax.all_gather(packed, "fsdp", axis=0, tiled=True)
+    full_output_t = lax.all_gather(w_output.T, "fsdp", axis=0, tiled=True)
     o1 = qw
     o2 = o1 + kw
     o3 = o2 + kw
@@ -134,8 +135,7 @@
     full_query = packed_all[:, :o1]
     full_key = packed_all[:, o1:o2]
     full_value = packed_all[:, o2:o3]
-    full_output_t = packed_all[:, o3:o4]
-    gains_all = packed_all[:, o4:].astype(f32)
+    gains_all = packed_all[:, o3:].astype(f32)
     head_shard = gain_query.shape[0]
 
     def head_gain(col):
@@ -203,14 +203,17 @@
     shard_gate = jnp.einsum("tf,td->fd", grad_gate, rows_all, preferred_element_type=f32)
     shard_up = jnp.einsum("tf,td->fd", grad_up, rows_all, preferred_element_type=f32)
     shard_down = jnp.einsum("tf,td->fd", hidden, grad_all, preferred_element_type=f32)
-    grad_pre = a2a_sum(
-        (
-            jnp.dot(grad_gate, w_gate, preferred_element_type=f32)
-            + jnp.dot(grad_up, w_up, preferred_element_type=f32)
-        ).astype(jnp.bfloat16),
-        "fsdp",
-        groups,
-    )
+    pre_partial = (
+        jnp.dot(grad_gate, w_gate, preferred_element_type=f32)
+        + jnp.dot(grad_up, w_up, preferred_element_type=f32)
+    ).astype(jnp.bfloat16)
+    ffn_packed = jnp.concatenate([shard_gate, shard_up, shard_down], axis=0).astype(low)
+    ffn_rows = ffn_packed.shape[0]
+    ffn_step = 8 * parts
+    ffn_packed = jnp.pad(ffn_packed, ((0, -ffn_rows % ffn_step), (0, 0)))
+    ffn_packed, pre_partial = lax.optimization_barrier((ffn_packed, pre_partial))
+    ffn_mine = lax.psum_scatter(ffn_packed, "ctx", scatter_dimension=0, tiled=True)
+    grad_pre = a2a_sum(pre_partial, "fsdp", groups)
     grad_from_pre, grad_gain_pre = norm_backward(grad_pre, pre_unit, pre_inv, norm_pre)
     grad_residual = grad_out + grad_from_pre
     grad_branch_full, grad_gain_attn = norm_backward(grad_residual, attn_unit, attn_inv, norm_attn)
@@ -231,6 +234,7 @@
     key_value_terms = jnp.concatenate([key_term, value_term], axis=1)
     grad_query_rot = jnp.einsum("hqk,kd->qhd", grad_scores, key_all, preferred_element_type=f32)
     summed_kv = a2a_sum(key_value_terms.astype(jnp.bfloat16), "ctx", parts)
+    ffn_mine, summed_kv = lax.optimization_barrier((ffn_mine, summed_kv))
     grad_key_rot = summed_kv[:, :HD]
     grad_values = summed_kv[:, HD:].astype(low)
     grad_q_normed = rotate_back(grad_query_rot * scale, cosine[:, None, :], sine[:, None, :])
@@ -274,9 +278,7 @@
         return lax.all_to_all(jnp.broadcast_to(mine[None], chunks.shape), "ctx", 0, 0).reshape(x.shape)
 
     ffn_units = shard_gate.shape[0]
-    ffn_sums = ctx_sum(
-        jnp.concatenate([shard_gate, shard_up, shard_down], axis=0).astype(low)
-    ).astype(f32)
+    ffn_sums = a2a_gather(ffn_mine, "ctx", parts)[:ffn_rows].astype(f32)
     grad_packed = jnp.concatenate([term_query, term_key, term_value, term_output], axis=0).astype(low)
     grad_shard = jnp.concatenate(
         [

time: 619 us -> 645 us (1.042)
  waiting for transfers between devices: 304 us -> 376 us
  blocking collectives: 105 us -> 75.2 us
  local copies, waits for them, and re-layouts: 54.4 us -> 41.1 us
  starting transfers between devices: 34.9 us -> 28.1 us
  other arithmetic: 31.3 us -> 38 us
    unnamed x5 -> x7, waiting for transfers between devices: 0.08 us -> 85.4 us
    all_to_all x2 -> x1, waiting for transfers between devices: 43 us -> 2.03 us  [ctx_sum(): lax.all_to_all(jnp.broadcast_to(mine[None], chunks.shape), 'ctx', 0, 0)]
    all_to_all x1, blocking collectives: 44.3 us -> 14.1 us  [body(): lax.all_to_all(gain_block, 'fsdp', 0, 0).astype(f32)]
    all_to_all x2, waiting for transfers between devices: 67.7 us -> 86 us  [a2a_sum(): pieces = lax.all_to_all(x.reshape(count, -1, *x.shape[1:]), axis_name, 0, 0)]
    optimization_barrier x0 -> x1, waiting for transfers between devices: none -> 11.5 us  [body(): ffn_mine, summed_kv = lax.optimization_barrier((ffn_mine, summed_kv))]
    all_gather x0 -> x1, waiting for transfers between devices: none -> 9.7 us  [body(): full_output_t = lax.all_gather(w_output.T, 'fsdp', axis=0, tiled=True)]
    all_gather x1, waiting for transfers between devices: 63.4 us -> 54 us  [body(): packed_all = lax.all_gather(packed, 'fsdp', axis=0, tiled=True)]
    all_to_all x1 -> x0, starting transfers between devices: 8.21 us -> none  [body(): lax.all_to_all(gain_block, 'fsdp', 0, 0).astype(f32)]
  transfers between devices with their start and end apart: 11 -> 12, of which waited for: 10 -> 11; matrix products, arithmetic and copies ran while one was open for 9% -> 10% of each run, Pallas kernels for 0% -> 0%
where the time goes in v8:
time: 645 us; the launch traced here: 638 us
  waiting for transfers between devices  376 us (58%)
  blocking collectives  75.2 us (12%)
  matrix products  63.6 us (10%)
  local copies, waits for them, and re-layouts  41.1 us (6%)
  other arithmetic  38 us (6%)
  starting transfers between devices  28.1 us (4%)
  between operations  15.7 us (2%)
    all_to_all x2, waiting for transfers between devices, a2a_sum(): pieces = lax.all_to_all(x.reshape(count, -1, *x.shape[1:]), axis_name, 0, 0)  86 us
    unnamed x7, waiting for transfers between devices  85.4 us
    all_to_all x1, blocking collectives, a2a_sum(): pieces = lax.all_to_all(x.reshape(count, -1, *x.shape[1:]), axis_name, 0, 0)  61.1 us
    all_gather x1, waiting for transfers between devices, body(): rows_all = lax.all_gather(normed_pre, 'fsdp', axis=0, tiled=True)  56.9 us
    all_gather x1, waiting for transfers between devices, body(): grad_all = lax.all_gather(grad_ffn, 'fsdp', axis=0, tiled=True)  55.3 us
    all_gather x1, waiting for transfers between devices, body(): packed_all = lax.all_gather(packed, 'fsdp', axis=0, tiled=True)  54 us
    unnamed x132, local copies, waits for them, and re-layouts  14.7 us
    all_to_all x1, blocking collectives, body(): lax.all_to_all(gain_block, 'fsdp', 0, 0).astype(f32)  14.1 us
  transfers between devices with their start and end apart: 12, of which 11 were waited for; matrix products, arithmetic and copies ran while one was open for 10% of the time, Pallas kernels for 0%

profile of v8, /device:TPU:0, one launch (start us, length us, event | category | flops | bytes accessed | tf_op | source)
XLA Modules:
  0.0 638.2 jit_solution(6045403539281522225)
XLA Ops:
  14.4 54.0 %all-gather.5.cloned.1.call-done = bf16[1152,1664]{1,0:T(8,128)(2,1)} async-done(((bf16[72,1664]{1,0:T(8,128)(2,1)}), bf16[1152,1664]{1,0:T(8,128)(2,1)}) %all-gather.5.cloned.1.call-update) | async-done | bytes 3833872 | tf_op jit(solution)/shard_map/all_gather | solution.py:129
  68.4 3.3 slice_bitcast_fusion
  71.7 4.4 copy.90
  84.7 4.3 all-to-all-start
  93.2 12.6 %all-to-all-done = bf16[8,128,512]{2,1,0:T(8,128)(2,1)S(1)} async-done(((bf16[8,128,512]{2,1,0:T(8,128)(2,1)}), bf16[8,128,512]{2,1,0:T(8,128)(2,1)S(1)}, u32[]{:S(2)}, u32[]{:S(2)}) %all-to-all-start) | async-done | bytes 1048608 | tf_op jit(solution)/shard_map/all_to_all | solution.py:83
  109.5 9.7 %all-gather.7.cloned.1.call-done = bf16[1152,1024]{1,0:T(8,128)(2,1)} async-done(((bf16[72,1024]{1,0:T(8,128)(2,1)}), bf16[1152,1024]{1,0:T(8,128)(2,1)}) %all-gather.7.cloned.1.call-update) | async-done | bytes 2359312 | tf_op jit(solution)/shard_map/all_gather | solution.py:130
  123.6 56.9 %all-gather.9.cloned.1.call-done = bf16[2048,1152]{1,0:T(8,128)(2,1)} async-done(((bf16[128,1152]{1,0:T(8,128)(2,1)}), bf16[2048,1152]{1,0:T(8,128)(2,1)}) %all-gather.9.cloned.1.call-update) | async-done | bytes 4718608 | tf_op jit(solution)/shard_map/all_gather | solution.py:186
  180.5 5.2 fusion.103
  185.8 4.6 multiply_convert_fusion.1
  190.5 3.2 convolution_convert_fusion
  193.7 61.1 %all_to_all.40 = bf16[16,128,1152]{2,1,0:T(8,128)(2,1)S(1)} all-to-all(bf16[16,128,1152]{2,1,0:T(8,128)(2,1)S(1)} %bitcast.188), channel_id=1, replica_groups=mesh['ctx'=8,'fsdp'=16] {'fsdp'}, dimensions={0} | all-to-all | bytes 9437184 | tf_op jit(solution)/shard_map/all_to_all | solution.py:77
  257.6 55.3 %all-gather.11.cloned.1.call-done = bf16[2048,1152]{1,0:T(8,128)(2,1)} async-done(((bf16[128,1152]{1,0:T(8,128)(2,1)}), bf16[2048,1152]{1,0:T(8,128)(2,1)}) %all-gather.11.cloned.1.call-update) | async-done | bytes 4718608 | tf_op jit(solution)/shard_map/all_gather | solution.py:199
  312.9 8.5 %fusion.9 = (bf16[2048,432]{0,1:T(8,128)(2,1)S(1)}, bf16[2048,432]{0,1:T(8,128)(2,1)S(1)}) fusion(f32[2048,432]{0,1:T(8,128)} %copy-done.57, f32[2048,432]{0,1:T(8,128)} %get-tuple-element.82, bf16[2048,1152]{1,0:T(8,128)(2,1)} %all-gather.11.cloned.1.call-done, bf16[432,1152]{1,0:T(8,128)(2,1)S(1)} %copy-done), kind=kOutput, calls=%fused_computation.19 | convolution fusion | flops 2058780672 | bytes 16330752 | tf_op jit(solution)/shard_map/td,fd->tf/dot_general | solution.py:200
  321.5 2.9 fusion.104
  324.5 4.8 add_convert_fusion
  336.7 6.9 %fusion.11 = bf16[1344,1152]{1,0:T(8,128)(2,1)} fusion(bf16[432,1152]{1,0:T(8,128)(2,1)S(1)} %convolution_convert_fusion.3, bf16[432,1152]{1,0:T(8,128)(2,1)S(1)} %convolution_convert_fusion.4, bf16[432,1152]{1,0:T(8,128)(2,1)S(1)} %convolution_convert_fusion.5), kind=kLoop, calls=%fused_computation.24 | loop fusion | flops 15482880 | bytes 6082560 | tf_op jit(solution)/shard_map/concatenate | solution.py:210
  343.6 4.7 all-to-all-start.2
  349.2 2.9 fusion.13
  352.1 71.5 %all-to-all-done.2 = bf16[16,128,1152]{2,1,0:T(8,128)(2,1)} async-done(((bf16[16,128,1152]{2,1,0:T(8,128)(2,1)}), bf16[16,128,1152]{2,1,0:T(8,128)(2,1)}, u32[]{:S(2)}, u32[]{:S(2)}) %all-to-all-start.2) | async-done | bytes 4718624 | tf_op jit(solution)/shard_map/all_to_all | solution.py:77
  423.6 3.1 convert_reduce_fusion
  433.8 5.8 all-to-all-start.3
  446.9 14.6 %all-to-all-done.3 = bf16[8,128,512]{2,1,0:T(8,128)(2,1)S(1)} async-done(((bf16[8,128,512]{2,1,0:T(8,128)(2,1)}), bf16[8,128,512]{2,1,0:T(8,128)(2,1)S(1)}, u32[]{:S(2)}, u32[]{:S(2)}) %all-to-all-start.3) | async-done | bytes 1048608 | tf_op jit(solution)/shard_map/all_to_all | solution.py:77
  461.6 11.5 %reduce-scatter.10.cloned.1.call-done = bf16[168,1152]{1,0:T(8,128)(2,1)} async-done(((bf16[1344,1152]{1,0:T(8,128)(2,1)}), bf16[168,1152]{1,0:T(8,128)(2,1)}) %reduce-scatter.10.cloned.1.call-update) | async-done | bytes 387088 | tf_op jit(solution)/shard_map/optimization_barrier | solution.py:237
  474.8 4.6 pad_maximum_fusion
  479.5 8.9 %copy.117 = bf16[2560,1152]{0,1:T(8,128)(2,1)} copy(bf16[2560,1152]{1,0:T(8,128)(2,1)} %pad_maximum_fusion) | data formatting | bytes 11796480
  495.3 14.1 %all_to_all.41 = bf16[16,8,72]{2,1,0:T(8,128)(2,1)S(1)} all-to-all(bf16[16,8,72]{2,1,0:T(8,128)(2,1)S(1)} %copy.100), channel_id=1, replica_groups=mesh['ctx'=8,'fsdp'=16] {'fsdp'}, dimensions={0} | all-to-all | bytes 36864 | tf_op jit(solution)/shard_map/all_to_all | solution.py:273
  511.3 4.4 all-to-all-start.7
  516.7 84.3 %reduce-scatter.8.cloned.1.call-done = bf16[72,2560]{1,0:T(8,128)(2,1)} async-done(((bf16[1152,2560]{1,0:T(8,128)(2,1)}), bf16[72,2560]{1,0:T(8,128)(2,1)}) %reduce-scatter.8.cloned.1.call-update) | async-done | bytes 368656
  603.7 4.3 all-to-all-start.5
  608.0 4.8 slice_convert_fusion
  616.6 3.5 all-to-all-start.6
  620.0 5.6 fusion.101
  (258 shorter events, 75.9 us)
Async XLA Ops:
  7.2 183.3 %copy-start = (bf16[432,1152]{1,0:T(8,128)(2,1)S(1)}, bf16[432,1152]{1,0:T(8,128)(2,1)}, u32[]{:S(2)}) copy-start(bf16[432,1152]{1,0:T(8,128)(2,1)} %param.27) | copy-start | bytes 2985988
  7.2 61.2 %all-gather.5.cloned.1.call-start = ((), (), s32[]{:S(2)}) async-start(), calls=%async_computation.10 | async-start | bytes 4073472 | tf_op jit(solution)/shard_map/all_gather | solution.py:129
  10.5 108.6 %all-gather.7.cloned.1.call-start = ((), (), s32[]{:S(2)}) async-start(), calls=%async_computation.11 | async-start | bytes 2506752 | tf_op jit(solution)/shard_map/all_gather | solution.py:130
  11.3 70.5 %copy-start.46 = (f32[128]{0:T(128)}, f32[128]{0:T(128)S(1)}, u32[]{:S(2)}) copy-start(f32[128]{0:T(128)S(1)} %multiply_power_fusion) | copy-start | bytes 1540
  12.3 63.8 %copy-start.50 = (s32[128]{0:T(128)}, s32[128]{0:T(128)S(1)}, u32[]{:S(2)}) copy-start(s32[128]{0:T(128)S(1)} %fusion.90) | copy-start | bytes 1540
  13.5 75.6 %copy-start.30 = (f32[128]{0:T(128)}, f32[128]{0:T(128)S(1)}, u32[]{:S(2)}) copy-start(f32[128]{0:T(128)S(1)} %add_rsqrt_fusion.5) | copy-start | bytes 1540
  14.2 67.7 %copy-start.48 = (f32[128]{0:T(128)}, f32[128]{0:T(128)S(1)}, u32[]{:S(2)}) copy-start(f32[128]{0:T(128)S(1)} %convert_bitcast_fusion.1) | copy-start | bytes 1540
  14.4 93.5 %copy-start.15 = (pred[128,1024]{0,1:T(8,128)(4,1)}, pred[128,1024]{0,1:T(8,128)(4,1)S(1)}, u32[]{:S(2)}) copy-start(pred[128,1024]{0,1:T(8,128)(4,1)S(1)} %broadcast_compare_fusion.1) | copy-start | bytes 393220
  84.7 21.1 %all-to-all-start = ((bf16[8,128,512]{2,1,0:T(8,128)(2,1)}), bf16[8,128,512]{2,1,0:T(8,128)(2,1)S(1)}, u32[]{:S(2)}, u32[]{:S(2)}) async-start(bf16[8,128,512]{2,1,0:T(8,128)(2,1)} %broadcast_in_dim.52), calls=%async_computation | async-start | bytes 2097152 | tf_op jit(solution)/shard_map/all_to_all | solution.py:83
  89.0 91.5 %all-gather.9.cloned.1.call-start = ((), (), s32[]{:S(2)}) async-start(), calls=%async_computation.12 | async-start | bytes 5013504 | tf_op jit(solution)/shard_map/all_gather | solution.py:186
  93.2 14.7 %copy-start.20 = (f32[128,4,128]{2,0,1:T(8,128)}, f32[128,4,128]{2,0,1:T(8,128)S(1)}, u32[]{:S(2)}) copy-start(f32[128,4,128]{2,0,1:T(8,128)S(1)} %get-tuple-element.61) | copy-start | bytes 786436
  108.8 13.3 %copy-start.25 = (f32[1152]{0:T(1024)S(1)}, f32[1152]{0:T(1024)}, u32[]{:S(2)}) copy-start(f32[1152]{0:T(1024)} %get-tuple-element.40) | copy-start | bytes 13828
  121.8 63.9 %copy-start.40 = (f32[128]{0:T(128)}, f32[128]{0:T(128)S(1)}, u32[]{:S(2)}) copy-start(f32[128]{0:T(128)S(1)} %add_rsqrt_fusion.3) | copy-start | bytes 1540
  122.1 63.7 %copy-start.44 = (f32[128]{0:T(128)}, f32[128]{0:T(128)S(1)}, u32[]{:S(2)}) copy-start(f32[128]{0:T(128)S(1)} %add_rsqrt_fusion.2) | copy-start | bytes 1540
  123.0 189.9 %all-gather.11.cloned.1.call-start = ((), (), s32[]{:S(2)}) async-start(), calls=%async_computation.13 | async-start | bytes 5013504 | tf_op jit(solution)/shard_map/all_gather | solution.py:199
  343.6 79.9 %all-to-all-start.2 = ((bf16[16,128,1152]{2,1,0:T(8,128)(2,1)}), bf16[16,128,1152]{2,1,0:T(8,128)(2,1)}, u32[]{:S(2)}, u32[]{:S(2)}) async-start(bf16[16,128,1152]{2,1,0:T(8,128)(2,1)} %bitcast.187), calls=%async_computation.2 | async-start | bytes 9437184 | tf_op jit(solution)/shard_map/all_to_all | solution.py:77
  348.3 124.8 %reduce-scatter.10.cloned.1.call-start = ((), (), s32[]{:S(2)}) async-start(), calls=%async_computation.15 | async-start | bytes 3483648
  349.2 77.6 %copy-start.26 = (f32[1152]{0:T(1024)S(1)}, f32[1152]{0:T(1024)}, u32[]{:S(2)}) copy-start(f32[1152]{0:T(1024)} %get-tuple-element.40) | copy-start | bytes 13828
  349.2 77.6 %copy-start.45 = (f32[128]{0:T(128)S(1)}, f32[128]{0:T(128)}, u32[]{:S(2)}) copy-start(f32[128]{0:T(128)} %copy-done.44) | copy-start | bytes 1540
  352.1 74.9 %copy-start.24 = (f32[1152]{0:T(1024)S(1)}, f32[1152]{0:T(1024)}, u32[]{:S(2)}) copy-start(f32[1152]{0:T(1024)} %get-tuple-element.41) | copy-start | bytes 13828
  352.1 74.9 %copy-start.41 = (f32[128]{0:T(128)S(1)}, f32[128]{0:T(128)}, u32[]{:S(2)}) copy-start(f32[128]{0:T(128)} %copy-done.40) | copy-start | bytes 1540
  433.8 27.7 %all-to-all-start.3 = ((bf16[8,128,512]{2,1,0:T(8,128)(2,1)}), bf16[8,128,512]{2,1,0:T(8,128)(2,1)S(1)}, u32[]{:S(2)}, u32[]{:S(2)}) async-start(bf16[8,128,512]{2,1,0:T(8,128)(2,1)} %pad_maximum_fusion.1), calls=%async_computation.3 | async-start | bytes 2097152 | tf_op jit(solution)/shard_map/all_to_all | solution.py:77
  439.6 161.4 %reduce-scatter.8.cloned.1.call-start = ((), (), s32[]{:S(2)}) async-start(), calls=%async_computation.14 | async-start | bytes 6266880
  442.4 30.7 %copy-start.47 = (f32[128]{0:T(128)S(1)}, f32[128]{0:T(128)}, u32[]{:S(2)}) copy-start(f32[128]{0:T(128)} %copy-done.46) | copy-start | bytes 1540
  442.4 30.7 %copy-start.49 = (f32[128]{0:T(128)S(1)}, f32[128]{0:T(128)}, u32[]{:S(2)}) copy-start(f32[128]{0:T(128)} %copy-done.48) | copy-start | bytes 1540
  442.4 31.4 %copy-start.9 = (f32[128,256]{1,0:T(8,128)S(1)}, f32[128,256]{1,0:T(8,128)}, u32[]{:S(2)}) copy-start(f32[128,256]{1,0:T(8,128)} %copy-done.8) | copy-start | bytes 393220
  442.5 31.4 %copy-start.33 = (f32[256]{0:T(256)S(1)}, f32[256]{0:T(256)}, u32[]{:S(2)}) copy-start(f32[256]{0:T(256)} %copy-done.32) | copy-start | bytes 3076
  442.5 31.4 %copy-start.43 = (f32[128]{0:T(128)S(1)}, f32[128]{0:T(128)}, u32[]{:S(2)}) copy-start(f32[128]{0:T(128)} %copy-done.42) | copy-start | bytes 1540
  489.3 20.1 %copy-start.19 = (bf16[168,1152]{1,0:T(8,128)(2,1)S(1)}, bf16[168,1152]{1,0:T(8,128)(2,1)}, u32[]{:S(2)}) copy-start(bf16[168,1152]{1,0:T(8,128)(2,1)} %reduce-scatter.10.cloned.1.call-done) | copy-start | bytes 1161220
  511.3 92.4 %all-to-all-start.7 = ((bf16[8,168,1152]{2,1,0:T(8,128)(2,1)}), bf16[8,168,1152]{2,1,0:T(8,128)(2,1)}, u32[]{:S(2)}, u32[]{:S(2)}) async-start(bf16[8,168,1152]{2,1,0:T(8,128)(2,1)} %broadcast_in_dim.65), calls=%async_computation.7 | async-start | bytes 6193152 | tf_op jit(solution)/shard_map/all_to_all | solution.py:83
  603.7 12.0 %all-to-all-start.5 = ((bf16[8,321,72]{1,2,0:T(8,128)(2,1)}), bf16[8,321,72]{1,2,0:T(8,128)(2,1)S(1)}, u32[]{:S(2)}, u32[]{:S(2)}) async-start(bf16[8,321,72]{1,2,0:T(8,128)(2,1)} %copy.102), calls=%async_computation.5 | async-start | bytes 884736 | tf_op jit(solution)/shard_map/all_to_all | solution.py:277
  616.6 11.1 %all-to-all-start.6 = ((bf16[8,321,72]{1,2,0:T(8,128)(2,1)}), bf16[8,321,72]{1,2,0:T(8,128)(2,1)S(1)}, u32[]{:S(2)}, u32[]{:S(2)}) async-start(bf16[8,321,72]{1,2,0:T(8,128)(2,1)} %broadcast_in_dim.64), calls=%async_computation.6 | async-start | bytes 884736 | tf_op jit(solution)/shard_map/all_to_all | solution.py:278
  (44 other events, 249.1 us)
Sparse Core Ops, SparseCore 0:
  11.1 57.3 all-gather.4
  70.8 48.2 all-gather.6
  123.1 57.3 all-gather.8
  257.7 55.1 all-gather.10
  351.3 121.8 reduce-scatter.9
  488.5 112.4 reduce-scatter.7

commit v9 on v8

--- a/solution.py
+++ b/solution.py
@@ -125,9 +125,8 @@
         axis=1,
     )
     gain_cols = jnp.pad(gain_cols, ((0, 0), (0, 128 - gain_cols.shape[1])))
-    packed = jnp.concatenate([w_query, w_key, w_value, gain_cols], axis=1)
+    packed = jnp.concatenate([w_query, w_key, w_value, w_output.T, gain_cols], axis=1)
     packed_all = lax.all_gather(packed, "fsdp", axis=0, tiled=True)
-    full_output_t = lax.all_gather(w_output.T, "fsdp", axis=0, tiled=True)
     o1 = qw
     o2 = o1 + kw
     o3 = o2 + kw
@@ -135,7 +134,8 @@
     full_query = packed_all[:, :o1]
     full_key = packed_all[:, o1:o2]
     full_value = packed_all[:, o2:o3]
-    gains_all = packed_all[:, o3:].astype(f32)
+    full_output_t = packed_all[:, o3:o4]
+    gains_all = packed_all[:, o4:].astype(f32)
     head_shard = gain_query.shape[0]
 
     def head_gain(col):
@@ -208,12 +208,9 @@
         + jnp.dot(grad_up, w_up, preferred_element_type=f32)
     ).astype(jnp.bfloat16)
     ffn_packed = jnp.concatenate([shard_gate, shard_up, shard_down], axis=0).astype(low)
-    ffn_rows = ffn_packed.shape[0]
-    ffn_step = 8 * parts
-    ffn_packed = jnp.pad(ffn_packed, ((0, -ffn_rows % ffn_step), (0, 0)))
     ffn_packed, pre_partial = lax.optimization_barrier((ffn_packed, pre_partial))
-    ffn_mine = lax.psum_scatter(ffn_packed, "ctx", scatter_dimension=0, tiled=True)
     grad_pre = a2a_sum(pre_partial, "fsdp", groups)
+    ffn_mine = a2a_sum(ffn_packed, "ctx", parts).astype(low)
     grad_from_pre, grad_gain_pre = norm_backward(grad_pre, pre_unit, pre_inv, norm_pre)
     grad_residual = grad_out + grad_from_pre
     grad_branch_full, grad_gain_attn = norm_backward(grad_residual, attn_unit, attn_inv, norm_attn)
@@ -234,7 +231,8 @@
     key_value_terms = jnp.concatenate([key_term, value_term], axis=1)
     grad_query_rot = jnp.einsum("hqk,kd->qhd", grad_scores, key_all, preferred_element_type=f32)
     summed_kv = a2a_sum(key_value_terms.astype(jnp.bfloat16), "ctx", parts)
-    ffn_mine, summed_kv = lax.optimization_barrier((ffn_mine, summed_kv))
+    ffn_sums = a2a_gather(ffn_mine, "ctx", parts)
+    ffn_sums, summed_kv = lax.optimization_barrier((ffn_sums, summed_kv))
     grad_key_rot = summed_kv[:, :HD]
     grad_values = summed_kv[:, HD:].astype(low)
     grad_q_normed = rotate_back(grad_query_rot * scale, cosine[:, None, :], sine[:, None, :])
@@ -278,7 +276,7 @@
         return lax.all_to_all(jnp.broadcast_to(mine[None], chunks.shape), "ctx", 0, 0).reshape(x.shape)
 
     ffn_units = shard_gate.shape[0]
-    ffn_sums = a2a_gather(ffn_mine, "ctx", parts)[:ffn_rows].astype(f32)
+    ffn_sums = ffn_sums.astype(f32)
     grad_packed = jnp.concatenate([term_query, term_key, term_value, term_output], axis=0).astype(low)
     grad_shard = jnp.concatenate(
         [

time: 645 us -> 681 us (1.056)
  blocking collectives: 75.2 us -> 117 us
  waiting for transfers between devices: 376 us -> 347 us
  local copies, waits for them, and re-layouts: 41.1 us -> 62 us
    all_to_all x1 -> x2, blocking collectives: 61.1 us -> 104 us  [a2a_sum(): pieces = lax.all_to_all(x.reshape(count, -1, *x.shape[1:]), axis_name, 0, 0)]
    unnamed x7 -> x5, waiting for transfers between devices: 85.4 us -> 55.9 us
    all_to_all x2, waiting for transfers between devices: 12.6 us -> 41.8 us  [a2a_gather(): lax.all_to_all(copies, axis_name, 0, 0)]
    all_to_all x2, waiting for transfers between devices: 86 us -> 65.7 us  [a2a_sum(): pieces = lax.all_to_all(x.reshape(count, -1, *x.shape[1:]), axis_name, 0, 0)]
    optimization_barrier x1 -> x0, waiting for transfers between devices: 11.5 us -> none  [body(): ffn_mine, summed_kv = lax.optimization_barrier((ffn_mine, summed_kv))]
    all_gather x1 -> x0, waiting for transfers between devices: 9.7 us -> none  [body(): full_output_t = lax.all_gather(w_output.T, 'fsdp', axis=0, tiled=True)]
    all_gather x1, waiting for transfers between devices: 54 us -> 63.4 us  [body(): packed_all = lax.all_gather(packed, 'fsdp', axis=0, tiled=True)]
    unnamed x132 -> x114, local copies, waits for them, and re-layouts: 14.7 us -> 20 us
  transfers between devices with their start and end apart: 12 -> 10, of which waited for: 11 -> 10; matrix products, arithmetic and copies ran while one was open for 10% -> 8% of each run, Pallas kernels for 0% -> 0%
where the time goes in v9:
time: 681 us; the launch traced here: 673 us
  waiting for transfers between devices  347 us (51%)
  blocking collectives  117 us (17%)
  matrix products  67.9 us (10%)
  local copies, waits for them, and re-layouts  62 us (9%)
  other arithmetic  37.7 us (6%)
  starting transfers between devices  26.8 us (4%)
  between operations  15.1 us (2%)
    all_to_all x2, blocking collectives, a2a_sum(): pieces = lax.all_to_all(x.reshape(count, -1, *x.shape[1:]), axis_name, 0, 0)  104 us
    all_to_all x2, waiting for transfers between devices, a2a_sum(): pieces = lax.all_to_all(x.reshape(count, -1, *x.shape[1:]), axis_name, 0, 0)  65.7 us
    all_gather x1, waiting for transfers between devices, body(): packed_all = lax.all_gather(packed, 'fsdp', axis=0, tiled=True)  63.4 us
    unnamed x5, waiting for transfers between devices  55.9 us
    all_gather x1, waiting for transfers between devices, body(): grad_all = lax.all_gather(grad_ffn, 'fsdp', axis=0, tiled=True)  55.3 us
    all_gather x1, waiting for transfers between devices, body(): rows_all = lax.all_gather(normed_pre, 'fsdp', axis=0, tiled=True)  54 us
    all_to_all x2, waiting for transfers between devices, a2a_gather(): lax.all_to_all(copies, axis_name, 0, 0)  41.8 us
    unnamed x114, local copies, waits for them, and re-layouts  20 us
  transfers between devices with their start and end apart: 10, of which 10 were waited for; matrix products, arithmetic and copies ran while one was open for 8% of the time, Pallas kernels for 0%

profile of v9, /device:TPU:0, one launch (start us, length us, event | category | flops | bytes accessed | tf_op | source)
XLA Modules:
  0.0 673.5 jit_solution(11208782572845947055)
XLA Ops:
  16.1 63.4 %all-gather.4.cloned.1.call-done = bf16[1152,2688]{1,0:T(8,128)(2,1)} async-done(((bf16[72,2688]{1,0:T(8,128)(2,1)}), bf16[1152,2688]{1,0:T(8,128)(2,1)}) %all-gather.4.cloned.1.call-update) | async-done | bytes 6193168 | tf_op jit(solution)/shard_map/all_gather | solution.py:129
  82.3 3.4 slice_bitcast_fusion
  85.7 4.4 copy.90
  94.9 4.3 all-to-all-start
  102.6 13.6 %all-to-all-done = bf16[8,128,512]{2,1,0:T(8,128)(2,1)} async-done(((bf16[8,128,512]{2,1,0:T(8,128)(2,1)}), bf16[8,128,512]{2,1,0:T(8,128)(2,1)}, u32[]{:S(2)}, u32[]{:S(2)}) %all-to-all-start) | async-done | bytes 1048608 | tf_op jit(solution)/shard_map/all_to_all | solution.py:83
  125.3 54.0 %all-gather.6.cloned.1.call-done = bf16[2048,1152]{1,0:T(8,128)(2,1)} async-done(((bf16[128,1152]{1,0:T(8,128)(2,1)}), bf16[2048,1152]{1,0:T(8,128)(2,1)}) %all-gather.6.cloned.1.call-update) | async-done | bytes 4718608 | tf_op jit(solution)/shard_map/all_gather | solution.py:186
  179.3 5.2 fusion.103
  184.6 4.7 multiply_convert_fusion.1
  189.3 3.2 convolution_convert_fusion
  192.5 61.1 %all_to_all.45 = bf16[16,128,1152]{2,1,0:T(8,128)(2,1)S(1)} all-to-all(bf16[16,128,1152]{2,1,0:T(8,128)(2,1)S(1)} %bitcast.185), channel_id=1, replica_groups=mesh['ctx'=8,'fsdp'=16] {'fsdp'}, dimensions={0} | all-to-all | bytes 9437184 | tf_op jit(solution)/shard_map/all_to_all | solution.py:77
  256.4 55.3 %all-gather.8.cloned.1.call-done = bf16[2048,1152]{1,0:T(8,128)(2,1)} async-done(((bf16[128,1152]{1,0:T(8,128)(2,1)}), bf16[2048,1152]{1,0:T(8,128)(2,1)}) %all-gather.8.cloned.1.call-update) | async-done | bytes 4718608 | tf_op jit(solution)/shard_map/all_gather | solution.py:199
  311.7 8.5 %fusion.6 = (bf16[2048,432]{0,1:T(8,128)(2,1)S(1)}, bf16[2048,432]{0,1:T(8,128)(2,1)S(1)}) fusion(f32[2048,432]{0,1:T(8,128)} %copy-done.46, f32[2048,432]{0,1:T(8,128)} %get-tuple-element.82, bf16[2048,1152]{1,0:T(8,128)(2,1)} %all-gather.8.cloned.1.call-done, bf16[432,1152]{1,0:T(8,128)(2,1)S(1)} %copy-done), kind=kOutput, calls=%fused_computation.15 | convolution fusion | flops 2058780672 | bytes 16330752 | tf_op jit(solution)/shard_map/td,fd->tf/dot_general | solution.py:200
  320.3 2.9 fusion.104
  323.3 4.9 add_convert_fusion
  337.5 3.5 reshape.353
  341.1 42.5 %all_to_all.46 = bf16[8,162,1152]{2,1,0:T(8,128)(2,1)} all-to-all(bf16[8,162,1152]{2,1,0:T(8,128)(2,1)} %reshape.353), channel_id=1, replica_groups=mesh['ctx'=8,'fsdp'=16] {'ctx'}, dimensions={0} | all-to-all | bytes 5971968 | tf_op jit(solution)/shard_map/all_to_all | solution.py:77
  383.5 5.0 all-to-all-start.2
  388.8 2.9 fusion.8
  394.2 57.9 %all-to-all-done.2 = bf16[16,128,1152]{2,1,0:T(8,128)(2,1)} async-done(((bf16[16,128,1152]{2,1,0:T(8,128)(2,1)}), bf16[16,128,1152]{2,1,0:T(8,128)(2,1)}, u32[]{:S(2)}, u32[]{:S(2)}) %all-to-all-start.2) | async-done | bytes 4718624 | tf_op jit(solution)/shard_map/all_to_all | solution.py:77
  453.9 4.7 all-to-all-start.4
  458.7 3.1 convert_reduce_fusion
  475.7 28.2 %all-to-all-done.4 = bf16[8,162,1152]{2,1,0:T(8,128)(2,1)} async-done(((bf16[8,162,1152]{2,1,0:T(8,128)(2,1)}), bf16[8,162,1152]{2,1,0:T(8,128)(2,1)}, u32[]{:S(2)}, u32[]{:S(2)}) %all-to-all-start.4) | async-done | bytes 2986016 | tf_op jit(solution)/shard_map/all_to_all | solution.py:83
  503.8 4.2 all-to-all-start.5
  515.4 7.8 %all-to-all-done.5 = bf16[8,128,512]{2,1,0:T(8,128)(2,1)} async-done(((bf16[8,128,512]{2,1,0:T(8,128)(2,1)}), bf16[8,128,512]{2,1,0:T(8,128)(2,1)}, u32[]{:S(2)}, u32[]{:S(2)}) %all-to-all-start.5) | async-done | bytes 1048608 | tf_op jit(solution)/shard_map/all_to_all | solution.py:77
  529.8 4.6 pad_maximum_fusion
  534.5 8.9 %copy.117 = bf16[2560,1152]{0,1:T(8,128)(2,1)} copy(bf16[2560,1152]{1,0:T(8,128)(2,1)} %pad_maximum_fusion) | data formatting | bytes 11796480
  560.2 13.9 %all_to_all.47 = bf16[16,8,72]{2,1,0:T(8,128)(2,1)S(1)} all-to-all(bf16[16,8,72]{2,1,0:T(8,128)(2,1)S(1)} %copy.100), channel_id=1, replica_groups=mesh['ctx'=8,'fsdp'=16] {'fsdp'}, dimensions={0} | all-to-all | bytes 36864 | tf_op jit(solution)/shard_map/all_to_all | solution.py:271
  574.1 55.8 %reduce-scatter.4.cloned.1.call-done = bf16[72,2560]{1,0:T(8,128)(2,1)} async-done(((bf16[1152,2560]{1,0:T(8,128)(2,1)}), bf16[72,2560]{1,0:T(8,128)(2,1)}) %reduce-scatter.4.cloned.1.call-update) | async-done | bytes 368656
  638.2 4.4 all-to-all-start.7
  645.3 5.0 all-to-all-done.7
  652.3 3.5 all-to-all-start.8
  657.9 5.4 all-to-all-done.8
  (237 shorter events, 108.0 us)
Async XLA Ops:
  7.2 182.1 %copy-start = (bf16[432,1152]{1,0:T(8,128)(2,1)S(1)}, bf16[432,1152]{1,0:T(8,128)(2,1)}, u32[]{:S(2)}) copy-start(bf16[432,1152]{1,0:T(8,128)(2,1)} %param.27) | copy-start | bytes 2985988
  7.2 72.4 %all-gather.4.cloned.1.call-start = ((), (), s32[]{:S(2)}) async-start(), calls=%async_computation.10 | async-start | bytes 6580224 | tf_op jit(solution)/shard_map/all_gather | solution.py:129
  13.9 78.1 %copy-start.37 = (f32[128]{0:T(128)}, f32[128]{0:T(128)S(1)}, u32[]{:S(2)}) copy-start(f32[128]{0:T(128)S(1)} %multiply_power_fusion) | copy-start | bytes 1540
  15.2 70.5 %copy-start.39 = (s32[128]{0:T(128)}, s32[128]{0:T(128)S(1)}, u32[]{:S(2)}) copy-start(s32[128]{0:T(128)S(1)} %fusion.90) | copy-start | bytes 1540
  15.2 84.0 %copy-start.29 = (f32[128]{0:T(128)}, f32[128]{0:T(128)S(1)}, u32[]{:S(2)}) copy-start(f32[128]{0:T(128)S(1)} %add_rsqrt_fusion.5) | copy-start | bytes 1540
  15.9 76.1 %copy-start.38 = (f32[128]{0:T(128)}, f32[128]{0:T(128)S(1)}, u32[]{:S(2)}) copy-start(f32[128]{0:T(128)S(1)} %convert_bitcast_fusion.1) | copy-start | bytes 1540
  16.1 102.1 %copy-start.22 = (pred[128,1024]{0,1:T(8,128)(4,1)}, pred[128,1024]{0,1:T(8,128)(4,1)S(1)}, u32[]{:S(2)}) copy-start(pred[128,1024]{0,1:T(8,128)(4,1)S(1)} %broadcast_compare_fusion.1) | copy-start | bytes 393220
  90.2 11.7 %copy-start.32 = (f32[256]{0:T(256)}, f32[256]{0:T(256)S(1)}, u32[]{:S(2)}) copy-start(f32[256]{0:T(256)S(1)} %mul.514) | copy-start | bytes 3076
  91.9 10.1 %copy-start.14 = (f32[128,256]{1,0:T(8,128)}, f32[128,256]{1,0:T(8,128)S(1)}, u32[]{:S(2)}) copy-start(f32[128,256]{1,0:T(8,128)S(1)} %get-tuple-element.74) | copy-start | bytes 393220
  91.9 7.4 %copy-start.36 = (f32[128]{0:T(128)}, f32[128]{0:T(128)S(1)}, u32[]{:S(2)}) copy-start(f32[128]{0:T(128)S(1)} %add_rsqrt_fusion.4) | copy-start | bytes 1540
  92.3 10.2 %copy-start.17 = (f32[128,128]{1,0:T(8,128)}, f32[128,128]{1,0:T(8,128)S(1)}, u32[]{:S(2)}) copy-start(f32[128,128]{1,0:T(8,128)S(1)} %get-tuple-element.69) | copy-start | bytes 196612
  92.4 10.2 %copy-start.19 = (f32[128,128]{1,0:T(8,128)}, f32[128,128]{1,0:T(8,128)S(1)}, u32[]{:S(2)}) copy-start(f32[128,128]{1,0:T(8,128)S(1)} %get-tuple-element.70) | copy-start | bytes 196612
  94.9 21.4 %all-to-all-start = ((bf16[8,128,512]{2,1,0:T(8,128)(2,1)}), bf16[8,128,512]{2,1,0:T(8,128)(2,1)}, u32[]{:S(2)}, u32[]{:S(2)}) async-start(bf16[8,128,512]{2,1,0:T(8,128)(2,1)} %broadcast_in_dim.52), calls=%async_computation | async-start | bytes 2097152 | tf_op jit(solution)/shard_map/all_to_all | solution.py:83
  99.2 80.1 %all-gather.6.cloned.1.call-start = ((), (), s32[]{:S(2)}) async-start(), calls=%async_computation.11 | async-start | bytes 5013504 | tf_op jit(solution)/shard_map/all_gather | solution.py:186
  102.6 15.6 %copy-start.23 = (f32[128,4,128]{2,0,1:T(8,128)}, f32[128,4,128]{2,0,1:T(8,128)S(1)}, u32[]{:S(2)}) copy-start(f32[128,4,128]{2,0,1:T(8,128)S(1)} %get-tuple-element.61) | copy-start | bytes 786436
  102.6 18.3 %copy-start.25 = (f32[128,4,128]{2,0,1:T(8,128)}, f32[128,4,128]{2,0,1:T(8,128)S(1)}, u32[]{:S(2)}) copy-start(f32[128,4,128]{2,0,1:T(8,128)S(1)} %get-tuple-element.62) | copy-start | bytes 786436
  123.6 61.0 %copy-start.7 = (f32[128,1152]{1,0:T(8,128)}, f32[128,1152]{1,0:T(8,128)S(1)}, u32[]{:S(2)}) copy-start(f32[128,1152]{1,0:T(8,128)S(1)} %get-tuple-element.80) | copy-start | bytes 1769476
  124.8 187.0 %all-gather.8.cloned.1.call-start = ((), (), s32[]{:S(2)}) async-start(), calls=%async_computation.12 | async-start | bytes 5013504 | tf_op jit(solution)/shard_map/all_gather | solution.py:199
  311.7 8.5 %copy-start.43 = (bf16[432,1152]{1,0:T(8,128)(2,1)S(1)}, bf16[432,1152]{1,0:T(8,128)(2,1)}, u32[]{:S(2)}) copy-start(bf16[432,1152]{1,0:T(8,128)(2,1)} %param.25) | copy-start | bytes 2985988
  320.3 7.9 %slice-start.2 = ((s8[4718592]{0:T(1024)(128)(4,1)}), s8[4194304]{0:T(1024)(128)(4,1)S(1)}, s32[]{:S(2)}) async-start(s8[4718592]{0:T(1024)(128)(4,1)} %bitcast.205), calls=%async_computation.16 | async-start | bytes 8388608
  320.3 10.4 %slice-start = ((s8[4718592]{0:T(1024)(128)(4,1)}), s8[4194304]{0:T(1024)(128)(4,1)S(1)}, s32[]{:S(2)}) async-start(s8[4718592]{0:T(1024)(128)(4,1)} %bitcast.203), calls=%async_computation.14 | async-start | bytes 8388608
  323.3 7.4 %slice-start.1 = ((s8[4718592]{0:T(1024)(128)(4,1)}), s8[524288]{0:T(1024)(128)(4,1)S(1)}, s32[]{:S(2)}) async-start(s8[4718592]{0:T(1024)(128)(4,1)} %bitcast.203), calls=%async_computation.15 | async-start | bytes 1048576
  383.5 68.5 %all-to-all-start.2 = ((bf16[16,128,1152]{2,1,0:T(8,128)(2,1)}), bf16[16,128,1152]{2,1,0:T(8,128)(2,1)}, u32[]{:S(2)}, u32[]{:S(2)}) async-start(bf16[16,128,1152]{2,1,0:T(8,128)(2,1)} %bitcast.184), calls=%async_computation.2 | async-start | bytes 9437184 | tf_op jit(solution)/shard_map/all_to_all | solution.py:77
  453.9 49.9 %all-to-all-start.4 = ((bf16[8,162,1152]{2,1,0:T(8,128)(2,1)}), bf16[8,162,1152]{2,1,0:T(8,128)(2,1)}, u32[]{:S(2)}, u32[]{:S(2)}) async-start(bf16[8,162,1152]{2,1,0:T(8,128)(2,1)} %broadcast_in_dim.61), calls=%async_computation.4 | async-start | bytes 6193152 | tf_op jit(solution)/shard_map/all_to_all | solution.py:83
  474.8 33.7 %copy-start.13 = (bf16[128,1152]{1,0:T(8,128)(2,1)S(1)}, bf16[128,1152]{1,0:T(8,128)(2,1)}, u32[]{:S(2)}) copy-start(bf16[128,1152]{1,0:T(8,128)(2,1)} %copy-done.12) | copy-start | bytes 884740
  475.7 35.2 %copy-start.30 = (f32[128]{0:T(128)S(1)}, f32[128]{0:T(128)}, u32[]{:S(2)}) copy-start(f32[128]{0:T(128)} %copy-done.29) | copy-start | bytes 1540
  503.8 19.4 %all-to-all-start.5 = ((bf16[8,128,512]{2,1,0:T(8,128)(2,1)}), bf16[8,128,512]{2,1,0:T(8,128)(2,1)}, u32[]{:S(2)}, u32[]{:S(2)}) async-start(bf16[8,128,512]{2,1,0:T(8,128)(2,1)} %pad_maximum_fusion.2), calls=%async_computation.5 | async-start | bytes 2097152 | tf_op jit(solution)/shard_map/all_to_all | solution.py:77
  508.1 121.8 %reduce-scatter.4.cloned.1.call-start = ((), (), s32[]{:S(2)}) async-start(), calls=%async_computation.13 | async-start | bytes 6266880
  523.2 6.6 copy-start.3
  638.2 12.1 %all-to-all-start.7 = ((bf16[8,321,72]{1,2,0:T(8,128)(2,1)}), bf16[8,321,72]{1,2,0:T(8,128)(2,1)}, u32[]{:S(2)}, u32[]{:S(2)}) async-start(bf16[8,321,72]{1,2,0:T(8,128)(2,1)} %copy.102), calls=%async_computation.7 | async-start | bytes 884736 | tf_op jit(solution)/shard_map/all_to_all | solution.py:275
  651.4 15.2 %copy-start.1 = (bf16[432,1152]{1,0:T(8,128)(2,1)S(1)}, bf16[432,1152]{1,0:T(8,128)(2,1)}, u32[]{:S(2)}) copy-start(bf16[432,1152]{1,0:T(8,128)(2,1)} %param.27) | copy-start | bytes 2985988
  652.3 11.1 %all-to-all-start.8 = ((bf16[8,321,72]{1,2,0:T(8,128)(2,1)}), bf16[8,321,72]{1,2,0:T(8,128)(2,1)S(1)}, u32[]{:S(2)}, u32[]{:S(2)}) async-start(bf16[8,321,72]{1,2,0:T(8,128)(2,1)} %broadcast_in_dim.65), calls=%async_computation.8 | async-start | bytes 884736 | tf_op jit(solution)/shard_map/all_to_all | solution.py:276
  (31 other events, 95.7 us)
Sparse Core Ops, SparseCore 0:
  13.1 66.3 all-gather.3
  124.9 54.3 all-gather.5
  256.5 55.1 all-gather.7
  543.5 86.3 reduce-scatter.3

commit v10 on v5

--- a/solution.py
+++ b/solution.py
@@ -125,8 +125,9 @@
         axis=1,
     )
     gain_cols = jnp.pad(gain_cols, ((0, 0), (0, 128 - gain_cols.shape[1])))
-    packed = jnp.concatenate([w_query, w_key, w_value, w_output.T, gain_cols], axis=1)
+    packed = jnp.concatenate([w_query, w_key, w_value, gain_cols], axis=1)
     packed_all = lax.all_gather(packed, "fsdp", axis=0, tiled=True)
+    full_output_t = a2a_gather(w_output.T, "fsdp", groups)
     o1 = qw
     o2 = o1 + kw
     o3 = o2 + kw
@@ -134,8 +135,7 @@
     full_query = packed_all[:, :o1]
     full_key = packed_all[:, o1:o2]
     full_value = packed_all[:, o2:o3]
-    full_output_t = packed_all[:, o3:o4]
-    gains_all = packed_all[:, o4:].astype(f32)
+    gains_all = packed_all[:, o3:].astype(f32)
     head_shard = gain_query.shape[0]
 
     def head_gain(col):

time: 619 us -> 638 us (1.031)
  waiting for transfers between devices: 304 us -> 316 us
    all_to_all x1 -> x2, waiting for transfers between devices: 13 us -> 29 us  [a2a_gather(): lax.all_to_all(copies, axis_name, 0, 0)]
    all_gather x1, waiting for transfers between devices: 63.4 us -> 56 us  [body(): packed_all = lax.all_gather(packed, 'fsdp', axis=0, tiled=True)]
    unnamed x108 -> x150, local copies, waits for them, and re-layouts: 18 us -> 15.7 us
  transfers between devices with their start and end apart: 11 -> 12, of which waited for: 10 -> 11; matrix products, arithmetic and copies ran while one was open for 9% -> 11% of each run, Pallas kernels for 0% -> 0%
where the time goes in v10:
time: 638 us; the launch traced here: 631 us
  waiting for transfers between devices  316 us (50%)
  blocking collectives  106 us (17%)
  matrix products  67 us (11%)
  local copies, waits for them, and re-layouts  54.8 us (9%)
  starting transfers between devices  38.7 us (6%)
  other arithmetic  32.4 us (5%)
  between operations  15.3 us (2%)
    all_to_all x2, waiting for transfers between devices, a2a_sum(): pieces = lax.all_to_all(x.reshape(count, -1, *x.shape[1:]), axis_name, 0, 0)  70.5 us
    all_to_all x1, blocking collectives, a2a_sum(): pieces = lax.all_to_all(x.reshape(count, -1, *x.shape[1:]), axis_name, 0, 0)  61.2 us
    all_gather x1, waiting for transfers between devices, body(): packed_all = lax.all_gather(packed, 'fsdp', axis=0, tiled=True)  56 us
    all_gather x1, waiting for transfers between devices, body(): rows_all = lax.all_gather(normed_pre, 'fsdp', axis=0, tiled=True)  55.3 us
    all_gather x1, waiting for transfers between devices, body(): grad_all = lax.all_gather(grad_ffn, 'fsdp', axis=0, tiled=True)  55.3 us
    all_to_all x1, blocking collectives, ctx_sum(): lax.all_to_all(chunks, 'ctx', 0, 0).astype(f32)  45 us
    all_to_all x2, waiting for transfers between devices, ctx_sum(): lax.all_to_all(jnp.broadcast_to(mine[None], chunks.shape), 'ctx', 0, 0)  43.2 us
    all_to_all x2, waiting for transfers between devices, a2a_gather(): lax.all_to_all(copies, axis_name, 0, 0)  29 us
  transfers between devices with their start and end apart: 12, of which 11 were waited for; matrix products, arithmetic and copies ran while one was open for 11% of the time, Pallas kernels for 0%

profile of v10, /device:TPU:0, one launch (start us, length us, event | category | flops | bytes accessed | tf_op | source)
XLA Modules:
  0.0 630.6 jit_solution(15005362404209505857)
XLA Ops:
  12.4 56.0 %all-gather.4.cloned.1.call-done = bf16[1152,1664]{1,0:T(8,128)(2,1)} async-done(((bf16[72,1664]{1,0:T(8,128)(2,1)}), bf16[1152,1664]{1,0:T(8,128)(2,1)}) %all-gather.4.cloned.1.call-update) | async-done | bytes 3833872 | tf_op jit(solution)/shard_map/all_gather | solution.py:129
  77.2 4.3 all-to-all-start
  82.8 15.5 %all-to-all-done = bf16[8,128,512]{2,1,0:T(8,128)(2,1)S(1)} async-done(((bf16[8,128,512]{2,1,0:T(8,128)(2,1)}), bf16[8,128,512]{2,1,0:T(8,128)(2,1)S(1)}, u32[]{:S(2)}, u32[]{:S(2)}) %all-to-all-start) | async-done | bytes 1048608 | tf_op jit(solution)/shard_map/all_to_all | solution.py:83
  100.1 5.0 all-to-all-start.1
  108.5 4.3 copy.90
  123.6 13.5 %all-to-all-done.1 = bf16[16,72,1024]{2,1,0:T(8,128)(2,1)S(1)} async-done(((bf16[16,72,1024]{2,1,0:T(8,128)(2,1)}), bf16[16,72,1024]{2,1,0:T(8,128)(2,1)S(1)}, u32[]{:S(2)}, u32[]{:S(2)}) %all-to-all-start.1) | async-done | bytes 2359328 | tf_op jit(solution)/shard_map/all_to_all | solution.py:83
  143.1 55.3 %all-gather.6.cloned.1.call-done = bf16[2048,1152]{1,0:T(8,128)(2,1)} async-done(((bf16[128,1152]{1,0:T(8,128)(2,1)}), bf16[2048,1152]{1,0:T(8,128)(2,1)}) %all-gather.6.cloned.1.call-update) | async-done | bytes 4718608 | tf_op jit(solution)/shard_map/all_gather | solution.py:186
  198.5 5.3 fusion.98
  203.8 4.6 multiply_convert_fusion.1
  211.6 61.2 %all_to_all.50 = bf16[16,128,1152]{2,1,0:T(8,128)(2,1)S(1)} all-to-all(bf16[16,128,1152]{2,1,0:T(8,128)(2,1)S(1)} %bitcast.189), channel_id=1, replica_groups=mesh['ctx'=8,'fsdp'=16] {'fsdp'}, dimensions={0} | all-to-all | bytes 9437184 | tf_op jit(solution)/shard_map/all_to_all | solution.py:77
  275.6 55.3 %all-gather.8.cloned.1.call-done = bf16[2048,1152]{1,0:T(8,128)(2,1)} async-done(((bf16[128,1152]{1,0:T(8,128)(2,1)}), bf16[2048,1152]{1,0:T(8,128)(2,1)}) %all-gather.8.cloned.1.call-update) | async-done | bytes 4718608 | tf_op jit(solution)/shard_map/all_gather | solution.py:199
  330.9 8.5 %multiply_convert_fusion = (bf16[2048,432]{0,1:T(8,128)(2,1)S(1)}, bf16[2048,432]{0,1:T(8,128)(2,1)S(1)}) fusion(f32[2048,432]{0,1:T(8,128)} %copy-done.69, f32[2048,432]{0,1:T(8,128)} %get-tuple-element.74, bf16[2048,1152]{1,0:T(8,128)(2,1)} %all-gather.8.cloned.1.call-done, bf16[432,1152]{1,0:T(8,128)(2,1)S(1)} %copy-done), kind=kOutput, calls=%fused_computation.16 | convolution fusion | flops 2058780672 | bytes 16330752 | tf_op jit(solution)/shard_map/td,fd->tf/dot_general | solution.py:200
  342.5 4.6 add_convert_fusion
  347.1 5.1 all-to-all-start.3
  355.6 60.0 %all-to-all-done.3 = bf16[16,128,1152]{2,1,0:T(8,128)(2,1)} async-done(((bf16[16,128,1152]{2,1,0:T(8,128)(2,1)}), bf16[16,128,1152]{2,1,0:T(8,128)(2,1)}, u32[]{:S(2)}, u32[]{:S(2)}) %all-to-all-start.3) | async-done | bytes 4718624 | tf_op jit(solution)/shard_map/all_to_all | solution.py:77
  426.3 4.7 all-to-all-start.4
  436.6 10.4 %all-to-all-done.4 = bf16[8,128,512]{2,1,0:T(8,128)(2,1)S(1)} async-done(((bf16[8,128,512]{2,1,0:T(8,128)(2,1)}), bf16[8,128,512]{2,1,0:T(8,128)(2,1)S(1)}, u32[]{:S(2)}, u32[]{:S(2)}) %all-to-all-start.4) | async-done | bytes 1048608 | tf_op jit(solution)/shard_map/all_to_all | solution.py:77
  448.7 4.6 pad_maximum_fusion
  453.4 8.8 %copy.117 = bf16[2560,1152]{0,1:T(8,128)(2,1)} copy(bf16[2560,1152]{1,0:T(8,128)(2,1)} %pad_maximum_fusion) | data formatting | bytes 11796480
  462.3 5.5 convolution_convert_fusion.3
  467.8 5.2 convolution_convert_fusion.4
  477.4 3.6 convert_element_type.202
  480.9 45.0 %all_to_all.51 = bf16[8,162,1152]{2,1,0:T(8,128)(2,1)} all-to-all(bf16[8,162,1152]{2,1,0:T(8,128)(2,1)} %convert_element_type.202), channel_id=1, replica_groups=mesh['ctx'=8,'fsdp'=16] {'ctx'}, dimensions={0} | all-to-all | bytes 5971968 | tf_op jit(solution)/shard_map/all_to_all | solution.py:273
  530.2 4.9 all-to-all-start.9
  542.0 35.8 %all-to-all-done.9 = bf16[8,162,1152]{2,1,0:T(8,128)(2,1)} async-done(((bf16[8,162,1152]{2,1,0:T(8,128)(2,1)}), bf16[8,162,1152]{2,1,0:T(8,128)(2,1)}, u32[]{:S(2)}, u32[]{:S(2)}) %all-to-all-start.9) | async-done | bytes 2986016 | tf_op jit(solution)/shard_map/all_to_all | solution.py:274
  577.8 7.1 %all-to-all-start.5 = ((bf16[16,8,72]{2,1,0:T(8,128)(2,1)}), bf16[16,8,72]{2,1,0:T(8,128)(2,1)S(1)}, u32[]{:S(2)}, u32[]{:S(2)}) async-start(bf16[16,8,72]{2,1,0:T(8,128)(2,1)} %copy.100), calls=%async_computation.5 | async-start | bytes 65536 | tf_op jit(solution)/shard_map/all_to_all | solution.py:269
  584.9 4.3 reshape.366
  595.2 3.5 all-to-all-start.6
  598.7 5.5 fusion.96
  604.3 3.5 all-to-all-done.6
  608.7 3.5 all-to-all-start.7
  613.1 7.4 %all-to-all-done.7 = bf16[8,321,72]{1,2,0:T(8,128)(2,1)S(1)} async-done(((bf16[8,321,72]{1,2,0:T(8,128)(2,1)}), bf16[8,321,72]{1,2,0:T(8,128)(2,1)S(1)}, u32[]{:S(2)}, u32[]{:S(2)}) %all-to-all-start.7) | async-done | bytes 369824 | tf_op jit(solution)/shard_map/all_to_all | solution.py:274
  (276 shorter events, 93.2 us)
Async XLA Ops:
  7.2 201.2 %copy-start = (bf16[432,1152]{1,0:T(8,128)(2,1)S(1)}, bf16[432,1152]{1,0:T(8,128)(2,1)}, u32[]{:S(2)}) copy-start(bf16[432,1152]{1,0:T(8,128)(2,1)} %param.27) | copy-start | bytes 2985988
  7.2 64.3 %copy-start.2 = (bf16[1,128,1152]{2,1,0:T(8,128)(2,1)S(1)}, bf16[1,128,1152]{2,1,0:T(8,128)(2,1)}, u32[]{:S(2)}) copy-start(bf16[1,128,1152]{2,1,0:T(8,128)(2,1)} %param.17) | copy-start | bytes 884740
  7.2 61.2 %all-gather.4.cloned.1.call-start = ((), (), s32[]{:S(2)}) async-start(), calls=%async_computation.11 | async-start | bytes 4073472 | tf_op jit(solution)/shard_map/all_gather | solution.py:129
  10.6 65.5 %copy-start.54 = (f32[128]{0:T(128)}, f32[128]{0:T(128)S(1)}, u32[]{:S(2)}) copy-start(f32[128]{0:T(128)S(1)} %multiply_power_fusion) | copy-start | bytes 1540
  11.7 64.4 %copy-start.40 = (f32[128]{0:T(128)}, f32[128]{0:T(128)S(1)}, u32[]{:S(2)}) copy-start(f32[128]{0:T(128)S(1)} %add_rsqrt_fusion.5) | copy-start | bytes 1540
  12.4 63.7 %copy-start.56 = (f32[128]{0:T(128)}, f32[128]{0:T(128)S(1)}, u32[]{:S(2)}) copy-start(f32[128]{0:T(128)S(1)} %convert_bitcast_fusion.1) | copy-start | bytes 1540
  71.5 26.8 %copy-start.33 = (bf16[1024,72]{0,1:T(8,128)(2,1)S(1)}, bf16[1024,72]{0,1:T(8,128)(2,1)}, u32[]{:S(2)}) copy-start(bf16[1024,72]{0,1:T(8,128)(2,1)} %param.24) | copy-start | bytes 442372
  77.2 21.1 %all-to-all-start = ((bf16[8,128,512]{2,1,0:T(8,128)(2,1)}), bf16[8,128,512]{2,1,0:T(8,128)(2,1)S(1)}, u32[]{:S(2)}, u32[]{:S(2)}) async-start(bf16[8,128,512]{2,1,0:T(8,128)(2,1)} %broadcast_in_dim.54), calls=%async_computation | async-start | bytes 2097152 | tf_op jit(solution)/shard_map/all_to_all | solution.py:83
  82.0 18.1 %copy-start.58 = (s32[128]{0:T(128)}, s32[128]{0:T(128)S(1)}, u32[]{:S(2)}) copy-start(s32[128]{0:T(128)S(1)} %fusion.85) | copy-start | bytes 1540
  100.1 37.1 %all-to-all-start.1 = ((bf16[16,72,1024]{2,1,0:T(8,128)(2,1)}), bf16[16,72,1024]{2,1,0:T(8,128)(2,1)S(1)}, u32[]{:S(2)}, u32[]{:S(2)}) async-start(bf16[16,72,1024]{2,1,0:T(8,128)(2,1)} %broadcast_in_dim.62), calls=%async_computation.1 | async-start | bytes 4718592 | tf_op jit(solution)/shard_map/all_to_all | solution.py:83
  105.1 93.3 %all-gather.6.cloned.1.call-start = ((), (), s32[]{:S(2)}) async-start(), calls=%async_computation.12 | async-start | bytes 5013504 | tf_op jit(solution)/shard_map/all_gather | solution.py:186
  142.9 188.0 %all-gather.8.cloned.1.call-start = ((), (), s32[]{:S(2)}) async-start(), calls=%async_computation.13 | async-start | bytes 5013504 | tf_op jit(solution)/shard_map/all_gather | solution.py:199
  347.1 68.4 %all-to-all-start.3 = ((bf16[16,128,1152]{2,1,0:T(8,128)(2,1)}), bf16[16,128,1152]{2,1,0:T(8,128)(2,1)}, u32[]{:S(2)}, u32[]{:S(2)}) async-start(bf16[16,128,1152]{2,1,0:T(8,128)(2,1)} %bitcast.188), calls=%async_computation.3 | async-start | bytes 9437184 | tf_op jit(solution)/shard_map/all_to_all | solution.py:77
  352.5 66.2 %copy-start.6 = (f32[128,1152]{1,0:T(8,128)S(1)}, f32[128,1152]{1,0:T(8,128)}, u32[]{:S(2)}) copy-start(f32[128,1152]{1,0:T(8,128)} %copy-done.4) | copy-start | bytes 1769476
  352.5 66.2 %copy-start.36 = (f32[1152]{0:T(1024)S(1)}, f32[1152]{0:T(1024)}, u32[]{:S(2)}) copy-start(f32[1152]{0:T(1024)} %get-tuple-element.32) | copy-start | bytes 13828
  352.5 66.2 %copy-start.53 = (f32[128]{0:T(128)S(1)}, f32[128]{0:T(128)}, u32[]{:S(2)}) copy-start(f32[128]{0:T(128)} %copy-done.52) | copy-start | bytes 1540
  355.5 63.5 %copy-start.17 = (bf16[1,128,1152]{2,1,0:T(8,128)(2,1)S(1)}, bf16[1,128,1152]{2,1,0:T(8,128)(2,1)}, u32[]{:S(2)}) copy-start(bf16[1,128,1152]{2,1,0:T(8,128)(2,1)} %param.18) | copy-start | bytes 884740
  355.5 63.5 %copy-start.34 = (f32[1152]{0:T(1024)S(1)}, f32[1152]{0:T(1024)}, u32[]{:S(2)}) copy-start(f32[1152]{0:T(1024)} %get-tuple-element.33) | copy-start | bytes 13828
  355.6 63.5 %copy-start.49 = (f32[128]{0:T(128)S(1)}, f32[128]{0:T(128)}, u32[]{:S(2)}) copy-start(f32[128]{0:T(128)} %copy-done.48) | copy-start | bytes 1540
  426.3 20.7 %all-to-all-start.4 = ((bf16[8,128,512]{2,1,0:T(8,128)(2,1)}), bf16[8,128,512]{2,1,0:T(8,128)(2,1)S(1)}, u32[]{:S(2)}, u32[]{:S(2)}) async-start(bf16[8,128,512]{2,1,0:T(8,128)(2,1)} %pad_maximum_fusion.2), calls=%async_computation.4 | async-start | bytes 2097152 | tf_op jit(solution)/shard_map/all_to_all | solution.py:77
  431.1 161.5 %reduce-scatter.4.cloned.1.call-start = ((), (), s32[]{:S(2)}) async-start(), calls=%async_computation.14 | async-start | bytes 6266880
  432.1 15.1 %copy-start.55 = (f32[128]{0:T(128)S(1)}, f32[128]{0:T(128)}, u32[]{:S(2)}) copy-start(f32[128]{0:T(128)} %copy-done.54) | copy-start | bytes 1540
  432.1 15.1 %copy-start.57 = (f32[128]{0:T(128)S(1)}, f32[128]{0:T(128)}, u32[]{:S(2)}) copy-start(f32[128]{0:T(128)} %copy-done.56) | copy-start | bytes 1540
  432.1 15.9 %copy-start.43 = (f32[256]{0:T(256)S(1)}, f32[256]{0:T(256)}, u32[]{:S(2)}) copy-start(f32[256]{0:T(256)} %copy-done.42) | copy-start | bytes 3076
  432.1 15.9 %copy-start.51 = (f32[128]{0:T(128)S(1)}, f32[128]{0:T(128)}, u32[]{:S(2)}) copy-start(f32[128]{0:T(128)} %copy-done.50) | copy-start | bytes 1540
  462.3 10.7 %slice-start = ((s8[4718592]{0:T(1024)(128)(4,1)}), s8[4194304]{0:T(1024)(128)(4,1)S(1)}, s32[]{:S(2)}) async-start(s8[4718592]{0:T(1024)(128)(4,1)} %bitcast.212), calls=%async_computation.15 | async-start | bytes 8388608
  530.2 47.6 %all-to-all-start.9 = ((bf16[8,162,1152]{2,1,0:T(8,128)(2,1)}), bf16[8,162,1152]{2,1,0:T(8,128)(2,1)}, u32[]{:S(2)}, u32[]{:S(2)}) async-start(bf16[8,162,1152]{2,1,0:T(8,128)(2,1)} %broadcast_in_dim.68), calls=%async_computation.9 | async-start | bytes 6193152 | tf_op jit(solution)/shard_map/all_to_all | solution.py:274
  577.8 14.7 %all-to-all-start.5 = ((bf16[16,8,72]{2,1,0:T(8,128)(2,1)}), bf16[16,8,72]{2,1,0:T(8,128)(2,1)S(1)}, u32[]{:S(2)}, u32[]{:S(2)}) async-start(bf16[16,8,72]{2,1,0:T(8,128)(2,1)} %copy.100), calls=%async_computation.5 | async-start | bytes 65536 | tf_op jit(solution)/shard_map/all_to_all | solution.py:269
  595.2 12.5 %all-to-all-start.6 = ((bf16[8,321,72]{1,2,0:T(8,128)(2,1)}), bf16[8,321,72]{1,2,0:T(8,128)(2,1)S(1)}, u32[]{:S(2)}, u32[]{:S(2)}) async-start(bf16[8,321,72]{1,2,0:T(8,128)(2,1)} %copy.102), calls=%async_computation.6 | async-start | bytes 884736 | tf_op jit(solution)/shard_map/all_to_all | solution.py:273
  598.7 13.4 %copy-start.14 = (f32[128,1152]{1,0:T(8,128)S(1)}, f32[128,1152]{1,0:T(8,128)}, u32[]{:S(2)}) copy-start(f32[128,1152]{1,0:T(8,128)} %copy-done.13) | copy-start | bytes 1769476
  607.9 16.0 %copy-start.1 = (bf16[432,1152]{1,0:T(8,128)(2,1)S(1)}, bf16[432,1152]{1,0:T(8,128)(2,1)}, u32[]{:S(2)}) copy-start(bf16[432,1152]{1,0:T(8,128)(2,1)} %param.27) | copy-start | bytes 2985988
  608.7 11.9 %all-to-all-start.7 = ((bf16[8,321,72]{1,2,0:T(8,128)(2,1)}), bf16[8,321,72]{1,2,0:T(8,128)(2,1)S(1)}, u32[]{:S(2)}, u32[]{:S(2)}) async-start(bf16[8,321,72]{1,2,0:T(8,128)(2,1)} %broadcast_in_dim.67), calls=%async_computation.7 | async-start | bytes 884736 | tf_op jit(solution)/shard_map/all_to_all | solution.py:274
  (53 other events, 188.8 us)
Sparse Core Ops, SparseCore 0:
  11.1 57.3 all-gather.3
  143.0 55.4 all-gather.5
  275.7 55.1 all-gather.7
  462.4 123.5 reduce-scatter.3

commit v11 on v5

--- a/solution.py
+++ b/solution.py
@@ -183,7 +183,7 @@
     residual = flat_in + attn_normed
     pre_full, pre_unit, pre_inv = norm_forward(residual, norm_pre)
     normed_pre = pre_full.astype(low)
-    rows_all = lax.all_gather(normed_pre, "fsdp", axis=0, tiled=True)
+    rows_all = a2a_gather(normed_pre, "fsdp", groups)
     gate = jnp.einsum("td,fd->tf", rows_all, w_gate, preferred_element_type=f32)
     upper = jnp.einsum("td,fd->tf", rows_all, w_up, preferred_element_type=f32)
     gelu_value, gelu_slope = gelu_pair(gate)
@@ -196,7 +196,7 @@
     grad_out = out_grad[0].astype(f32)
     grad_ffn_full, grad_gain_post = norm_backward(grad_out, post_unit, post_inv, norm_post)
     grad_ffn = grad_ffn_full.astype(low)
-    grad_all = lax.all_gather(grad_ffn, "fsdp", axis=0, tiled=True)
+    grad_all = a2a_gather(grad_ffn, "fsdp", groups)
     grad_hidden = jnp.einsum("td,fd->tf", grad_all, w_down, preferred_element_type=f32)
     grad_gate = (grad_hidden * upper * gelu_slope).astype(low)
     grad_up = (grad_hidden * gelu_value).astype(low)

time: 619 us -> 623 us (level)
  blocking collectives: 105 us -> 227 us
  waiting for transfers between devices: 304 us -> 195 us
  matrix products: 66.8 us -> 58.3 us
    all_to_all x0 -> x2, blocking collectives: none -> 122 us  [a2a_gather(): lax.all_to_all(copies, axis_name, 0, 0)]
    all_gather x2 -> x0, waiting for transfers between devices: 110 us -> none  [the longest x1 55.3 us: body(): grad_all = lax.all_gather(grad_ffn, 'fsdp', axis=0, tiled=True)]
    unnamed x108 -> x106, local copies, waits for them, and re-layouts: 18 us -> 18 us
  transfers between devices with their start and end apart: 11 -> 9, of which waited for: 10 -> 8; matrix products, arithmetic and copies ran while one was open for 9% -> 9% of each run, Pallas kernels for 0% -> 0%
where the time goes in v11:
time: 623 us; the launch traced here: 615 us
  blocking collectives  227 us (36%)
  waiting for transfers between devices  195 us (31%)
  matrix products  58.3 us (9%)
  local copies, waits for them, and re-layouts  55.7 us (9%)
  starting transfers between devices  33.1 us (5%)
  other arithmetic  30.4 us (5%)
  between operations  15.7 us (3%)
    all_to_all x2, blocking collectives, a2a_gather(): lax.all_to_all(copies, axis_name, 0, 0)  122 us
    all_to_all x2, waiting for transfers between devices, a2a_sum(): pieces = lax.all_to_all(x.reshape(count, -1, *x.shape[1:]), axis_name, 0, 0)  68.1 us
    all_gather x1, waiting for transfers between devices, body(): packed_all = lax.all_gather(packed, 'fsdp', axis=0, tiled=True)  63.4 us
    all_to_all x1, blocking collectives, a2a_sum(): pieces = lax.all_to_all(x.reshape(count, -1, *x.shape[1:]), axis_name, 0, 0)  60 us
    all_to_all x1, blocking collectives, ctx_sum(): lax.all_to_all(chunks, 'ctx', 0, 0).astype(f32)  44.6 us
    all_to_all x2, waiting for transfers between devices, ctx_sum(): lax.all_to_all(jnp.broadcast_to(mine[None], chunks.shape), 'ctx', 0, 0)  43.4 us
    unnamed x106, local copies, waits for them, and re-layouts  18 us
    all_to_all x1, waiting for transfers between devices, a2a_gather(): lax.all_to_all(copies, axis_name, 0, 0)  13 us
  transfers between devices with their start and end apart: 9, of which 8 were waited for; matrix products, arithmetic and copies ran while one was open for 9% of the time, Pallas kernels for 0%

profile of v11, /device:TPU:0, one launch (start us, length us, event | category | flops | bytes accessed | tf_op | source)
XLA Modules:
  0.0 614.9 jit_solution(15901634646975172630)
XLA Ops:
  16.2 63.4 %all-gather.2.cloned.1.call-done = bf16[1152,2688]{1,0:T(8,128)(2,1)} async-done(((bf16[72,2688]{1,0:T(8,128)(2,1)}), bf16[1152,2688]{1,0:T(8,128)(2,1)}) %all-gather.2.cloned.1.call-update) | async-done | bytes 6193168 | tf_op jit(solution)/shard_map/all_gather | solution.py:129
  84.0 3.3 slice_bitcast_fusion
  87.3 4.3 copy.90
  94.8 4.3 all-to-all-start
  102.9 13.0 %all-to-all-done = bf16[8,128,512]{2,1,0:T(8,128)(2,1)S(1)} async-done(((bf16[8,128,512]{2,1,0:T(8,128)(2,1)}), bf16[8,128,512]{2,1,0:T(8,128)(2,1)S(1)}, u32[]{:S(2)}, u32[]{:S(2)}) %all-to-all-start) | async-done | bytes 1048608 | tf_op jit(solution)/shard_map/all_to_all | solution.py:83
  122.2 62.2 %all_to_all.55 = bf16[16,128,1152]{2,1,0:T(8,128)(2,1)S(1)} all-to-all(bf16[16,128,1152]{2,1,0:T(8,128)(2,1)S(1)} %broadcast_in_dim.66), channel_id=1, replica_groups=mesh['ctx'=8,'fsdp'=16] {'fsdp'}, dimensions={0} | all-to-all | bytes 9437184 | tf_op jit(solution)/shard_map/all_to_all | solution.py:83
  189.8 3.2 convolution_convert_fusion
  193.0 60.0 %all_to_all.56 = bf16[16,128,1152]{2,1,0:T(8,128)(2,1)S(1)} all-to-all(bf16[16,128,1152]{2,1,0:T(8,128)(2,1)S(1)} %bitcast.213), channel_id=1, replica_groups=mesh['ctx'=8,'fsdp'=16] {'fsdp'}, dimensions={0} | all-to-all | bytes 9437184 | tf_op jit(solution)/shard_map/all_to_all | solution.py:77
  255.8 60.2 %all_to_all.57 = bf16[16,128,1152]{2,1,0:T(8,128)(2,1)S(1)} all-to-all(bf16[16,128,1152]{2,1,0:T(8,128)(2,1)S(1)} %broadcast_in_dim.69), channel_id=1, replica_groups=mesh['ctx'=8,'fsdp'=16] {'fsdp'}, dimensions={0} | all-to-all | bytes 9437184 | tf_op jit(solution)/shard_map/all_to_all | solution.py:83
  316.0 4.5 multiply_convert_fusion
  323.6 4.6 add_convert_fusion
  328.2 4.6 all-to-all-start.4
  333.0 3.0 fusion.8
  335.9 60.1 %all-to-all-done.4 = bf16[16,128,1152]{2,1,0:T(8,128)(2,1)} async-done(((bf16[16,128,1152]{2,1,0:T(8,128)(2,1)}), bf16[16,128,1152]{2,1,0:T(8,128)(2,1)}, u32[]{:S(2)}, u32[]{:S(2)}) %all-to-all-start.4) | async-done | bytes 4718624 | tf_op jit(solution)/shard_map/all_to_all | solution.py:77
  396.1 3.1 convert_reduce_fusion
  412.5 3.7 all-to-all-start.5
  424.6 8.0 %all-to-all-done.5 = bf16[8,128,512]{2,1,0:T(8,128)(2,1)S(1)} async-done(((bf16[8,128,512]{2,1,0:T(8,128)(2,1)}), bf16[8,128,512]{2,1,0:T(8,128)(2,1)S(1)}, u32[]{:S(2)}, u32[]{:S(2)}) %all-to-all-start.5) | async-done | bytes 1048608 | tf_op jit(solution)/shard_map/all_to_all | solution.py:77
  434.3 4.6 pad_maximum_fusion
  438.9 8.9 %copy.117 = bf16[2560,1152]{0,1:T(8,128)(2,1)} copy(bf16[2560,1152]{1,0:T(8,128)(2,1)} %pad_maximum_fusion) | data formatting | bytes 11796480
  447.8 5.5 convolution_convert_fusion.3
  460.1 3.6 convert_element_type.207
  463.7 44.6 %all_to_all.58 = bf16[8,162,1152]{2,1,0:T(8,128)(2,1)} all-to-all(bf16[8,162,1152]{2,1,0:T(8,128)(2,1)} %convert_element_type.207), channel_id=1, replica_groups=mesh['ctx'=8,'fsdp'=16] {'ctx'}, dimensions={0} | all-to-all | bytes 5971968 | tf_op jit(solution)/shard_map/all_to_all | solution.py:273
  512.6 5.0 all-to-all-start.10
  524.5 36.0 %all-to-all-done.10 = bf16[8,162,1152]{2,1,0:T(8,128)(2,1)} async-done(((bf16[8,162,1152]{2,1,0:T(8,128)(2,1)}), bf16[8,162,1152]{2,1,0:T(8,128)(2,1)}, u32[]{:S(2)}, u32[]{:S(2)}) %all-to-all-start.10) | async-done | bytes 2986016 | tf_op jit(solution)/shard_map/all_to_all | solution.py:274
  560.5 8.2 %all-to-all-start.6 = ((bf16[16,8,72]{2,1,0:T(8,128)(2,1)}), bf16[16,8,72]{2,1,0:T(8,128)(2,1)S(1)}, u32[]{:S(2)}, u32[]{:S(2)}) async-start(bf16[16,8,72]{2,1,0:T(8,128)(2,1)} %copy.100), calls=%async_computation.6 | async-start | bytes 65536 | tf_op jit(solution)/shard_map/all_to_all | solution.py:269
  568.7 4.3 reshape.430
  573.0 3.3 all-to-all-done.6
  579.0 3.5 all-to-all-start.7
  582.4 5.5 fusion.107
  588.0 3.5 all-to-all-done.7
  592.4 3.5 all-to-all-start.8
  596.9 7.4 %all-to-all-done.8 = bf16[8,321,72]{1,2,0:T(8,128)(2,1)S(1)} async-done(((bf16[8,321,72]{1,2,0:T(8,128)(2,1)}), bf16[8,321,72]{1,2,0:T(8,128)(2,1)S(1)}, u32[]{:S(2)}, u32[]{:S(2)}) %all-to-all-start.8) | async-done | bytes 369824 | tf_op jit(solution)/shard_map/all_to_all | solution.py:274
  (227 shorter events, 86.3 us)
Async XLA Ops:
  7.2 182.6 %copy-start = (bf16[432,1152]{1,0:T(8,128)(2,1)S(1)}, bf16[432,1152]{1,0:T(8,128)(2,1)}, u32[]{:S(2)}) copy-start(bf16[432,1152]{1,0:T(8,128)(2,1)} %param.27) | copy-start | bytes 2985988
  7.2 75.2 %copy-start.2 = (bf16[1,128,1152]{2,1,0:T(8,128)(2,1)S(1)}, bf16[1,128,1152]{2,1,0:T(8,128)(2,1)}, u32[]{:S(2)}) copy-start(bf16[1,128,1152]{2,1,0:T(8,128)(2,1)} %param.17) | copy-start | bytes 884740
  7.2 72.4 %all-gather.2.cloned.1.call-start = ((), (), s32[]{:S(2)}) async-start(), calls=%async_computation.12 | async-start | bytes 6580224 | tf_op jit(solution)/shard_map/all_gather | solution.py:129
  13.9 78.0 %copy-start.36 = (f32[128]{0:T(128)}, f32[128]{0:T(128)S(1)}, u32[]{:S(2)}) copy-start(f32[128]{0:T(128)S(1)} %multiply_power_fusion) | copy-start | bytes 1540
  15.9 76.0 %copy-start.38 = (f32[128]{0:T(128)}, f32[128]{0:T(128)S(1)}, u32[]{:S(2)}) copy-start(f32[128]{0:T(128)S(1)} %convert_bitcast_fusion.2) | copy-start | bytes 1540
  16.2 100.6 %copy-start.26 = (pred[128,1024]{0,1:T(8,128)(4,1)}, pred[128,1024]{0,1:T(8,128)(4,1)S(1)}, u32[]{:S(2)}) copy-start(pred[128,1024]{0,1:T(8,128)(4,1)S(1)} %broadcast_compare_fusion.1) | copy-start | bytes 393220
  83.9 8.0 %copy-start.34 = (f32[128]{0:T(128)}, f32[128]{0:T(128)S(1)}, u32[]{:S(2)}) copy-start(f32[128]{0:T(128)S(1)} %add_rsqrt_fusion.4) | copy-start | bytes 1540
  92.3 10.5 %copy-start.22 = (f32[128,128]{1,0:T(8,128)}, f32[128,128]{1,0:T(8,128)S(1)}, u32[]{:S(2)}) copy-start(f32[128,128]{1,0:T(8,128)S(1)} %get-tuple-element.60) | copy-start | bytes 196612
  92.3 10.5 %copy-start.24 = (f32[128,128]{1,0:T(8,128)}, f32[128,128]{1,0:T(8,128)S(1)}, u32[]{:S(2)}) copy-start(f32[128,128]{1,0:T(8,128)S(1)} %get-tuple-element.61) | copy-start | bytes 196612
  94.8 21.1 %all-to-all-start = ((bf16[8,128,512]{2,1,0:T(8,128)(2,1)}), bf16[8,128,512]{2,1,0:T(8,128)(2,1)S(1)}, u32[]{:S(2)}, u32[]{:S(2)}) async-start(bf16[8,128,512]{2,1,0:T(8,128)(2,1)} %broadcast_in_dim.58), calls=%async_computation | async-start | bytes 2097152 | tf_op jit(solution)/shard_map/all_to_all | solution.py:83
  102.8 13.9 %copy-start.27 = (f32[128,4,128]{2,0,1:T(8,128)}, f32[128,4,128]{2,0,1:T(8,128)S(1)}, u32[]{:S(2)}) copy-start(f32[128,4,128]{2,0,1:T(8,128)S(1)} %get-tuple-element.53) | copy-start | bytes 786436
  102.9 15.5 %copy-start.29 = (f32[128,4,128]{2,0,1:T(8,128)}, f32[128,4,128]{2,0,1:T(8,128)S(1)}, u32[]{:S(2)}) copy-start(f32[128,4,128]{2,0,1:T(8,128)S(1)} %get-tuple-element.54) | copy-start | bytes 786436
  117.7 215.3 %copy-start.31 = (f32[4,128]{1,0:T(4,128)}, f32[4,128]{1,0:T(4,128)S(1)}, u32[]{:S(2)}) copy-start(f32[4,128]{1,0:T(4,128)S(1)} %log_add_fusion) | copy-start | bytes 6148
  121.1 278.3 %copy-start.10 = (f32[128,1152]{1,0:T(8,128)}, f32[128,1152]{1,0:T(8,128)S(1)}, u32[]{:S(2)}) copy-start(f32[128,1152]{1,0:T(8,128)S(1)} %get-tuple-element.71) | copy-start | bytes 1769476
  121.1 278.3 %copy-start.33 = (f32[128]{0:T(128)}, f32[128]{0:T(128)S(1)}, u32[]{:S(2)}) copy-start(f32[128]{0:T(128)S(1)} %add_rsqrt_fusion.3) | copy-start | bytes 1540
  122.2 62.2 %copy-start.40 = (bf16[432,1152]{1,0:T(8,128)(2,1)S(1)}, bf16[432,1152]{1,0:T(8,128)(2,1)}, u32[]{:S(2)}) copy-start(bf16[432,1152]{1,0:T(8,128)(2,1)} %param.25) | copy-start | bytes 2985988
  328.2 67.9 %all-to-all-start.4 = ((bf16[16,128,1152]{2,1,0:T(8,128)(2,1)}), bf16[16,128,1152]{2,1,0:T(8,128)(2,1)}, u32[]{:S(2)}, u32[]{:S(2)}) async-start(bf16[16,128,1152]{2,1,0:T(8,128)(2,1)} %bitcast.212), calls=%async_computation.4 | async-start | bytes 9437184 | tf_op jit(solution)/shard_map/all_to_all | solution.py:77
  399.9 9.3 %copy-start.8 = (f32[128,1152]{1,0:T(8,128)}, f32[128,1152]{1,0:T(8,128)S(1)}, u32[]{:S(2)}) copy-start(f32[128,1152]{1,0:T(8,128)S(1)} %get-tuple-element.39) | copy-start | bytes 1769476
  399.9 7.4 %copy-start.5 = (f32[1024,128,4]{1,0,2:T(8,128)S(1)}, f32[1024,128,4]{1,0,2:T(8,128)}, u32[]{:S(2)}) copy-start(f32[1024,128,4]{1,0,2:T(8,128)} %copy-done.4) | copy-start | bytes 6291460
  412.5 7.5 %copy-start.16 = (bf16[128,1152]{1,0:T(8,128)(2,1)S(1)}, bf16[128,1152]{1,0:T(8,128)(2,1)}, u32[]{:S(2)}) copy-start(bf16[128,1152]{1,0:T(8,128)(2,1)} %copy-done.15) | copy-start | bytes 884740
  412.5 7.5 %copy-start.18 = (bf16[256,4,128]{2,0,1:T(8,128)(2,1)S(1)}, bf16[256,4,128]{2,0,1:T(8,128)(2,1)}, u32[]{:S(2)}) copy-start(bf16[256,4,128]{2,0,1:T(8,128)(2,1)} %copy-done.17) | copy-start | bytes 786436
  412.5 20.1 %all-to-all-start.5 = ((bf16[8,128,512]{2,1,0:T(8,128)(2,1)}), bf16[8,128,512]{2,1,0:T(8,128)(2,1)S(1)}, u32[]{:S(2)}, u32[]{:S(2)}) async-start(bf16[8,128,512]{2,1,0:T(8,128)(2,1)} %pad_maximum_fusion.2), calls=%async_computation.5 | async-start | bytes 2097152 | tf_op jit(solution)/shard_map/all_to_all | solution.py:77
  416.2 160.1 %reduce-scatter.4.cloned.1.call-start = ((), (), s32[]{:S(2)}) async-start(), calls=%async_computation.13 | async-start | bytes 6266880
  420.0 12.7 %copy-start.37 = (f32[128]{0:T(128)S(1)}, f32[128]{0:T(128)}, u32[]{:S(2)}) copy-start(f32[128]{0:T(128)} %copy-done.36) | copy-start | bytes 1540
  420.0 12.7 %copy-start.39 = (f32[128]{0:T(128)S(1)}, f32[128]{0:T(128)}, u32[]{:S(2)}) copy-start(f32[128]{0:T(128)} %copy-done.38) | copy-start | bytes 1540
  420.0 13.5 %copy-start.35 = (f32[128]{0:T(128)S(1)}, f32[128]{0:T(128)}, u32[]{:S(2)}) copy-start(f32[128]{0:T(128)} %copy-done.34) | copy-start | bytes 1540
  512.6 47.9 %all-to-all-start.10 = ((bf16[8,162,1152]{2,1,0:T(8,128)(2,1)}), bf16[8,162,1152]{2,1,0:T(8,128)(2,1)}, u32[]{:S(2)}, u32[]{:S(2)}) async-start(bf16[8,162,1152]{2,1,0:T(8,128)(2,1)} %broadcast_in_dim.124), calls=%async_computation.10 | async-start | bytes 6193152 | tf_op jit(solution)/shard_map/all_to_all | solution.py:274
  560.5 15.8 %all-to-all-start.6 = ((bf16[16,8,72]{2,1,0:T(8,128)(2,1)}), bf16[16,8,72]{2,1,0:T(8,128)(2,1)S(1)}, u32[]{:S(2)}, u32[]{:S(2)}) async-start(bf16[16,8,72]{2,1,0:T(8,128)(2,1)} %copy.100), calls=%async_computation.6 | async-start | bytes 65536 | tf_op jit(solution)/shard_map/all_to_all | solution.py:269
  579.0 12.5 %all-to-all-start.7 = ((bf16[8,321,72]{1,2,0:T(8,128)(2,1)}), bf16[8,321,72]{1,2,0:T(8,128)(2,1)S(1)}, u32[]{:S(2)}, u32[]{:S(2)}) async-start(bf16[8,321,72]{1,2,0:T(8,128)(2,1)} %copy.102), calls=%async_computation.7 | async-start | bytes 884736 | tf_op jit(solution)/shard_map/all_to_all | solution.py:273
  582.4 13.4 %copy-start.9 = (f32[128,1152]{1,0:T(8,128)S(1)}, f32[128,1152]{1,0:T(8,128)}, u32[]{:S(2)}) copy-start(f32[128,1152]{1,0:T(8,128)} %copy-done.8) | copy-start | bytes 1769476
  591.6 16.0 %copy-start.1 = (bf16[432,1152]{1,0:T(8,128)(2,1)S(1)}, bf16[432,1152]{1,0:T(8,128)(2,1)}, u32[]{:S(2)}) copy-start(bf16[432,1152]{1,0:T(8,128)(2,1)} %param.27) | copy-start | bytes 2985988
  592.4 11.9 %all-to-all-start.8 = ((bf16[8,321,72]{1,2,0:T(8,128)(2,1)}), bf16[8,321,72]{1,2,0:T(8,128)(2,1)S(1)}, u32[]{:S(2)}, u32[]{:S(2)}) async-start(bf16[8,321,72]{1,2,0:T(8,128)(2,1)} %broadcast_in_dim.73), calls=%async_computation.8 | async-start | bytes 884736 | tf_op jit(solution)/shard_map/all_to_all | solution.py:274
  (26 other events, 87.6 us)
Sparse Core Ops, SparseCore 0:
  13.2 66.3 all-gather.1
  447.9 122.3 reduce-scatter.3

commit v12 on v5

--- a/solution.py
+++ b/solution.py
@@ -239,9 +239,12 @@
     grad_k_full, grad_gain_key = norm_backward(grad_k_normed, key_unit, key_inv, norm_key)
     grad_q_in = grad_q_full.reshape(local, H * HD).astype(low)
     grad_k_in = grad_k_full.astype(low)
-    term_query = jnp.einsum("tc,td->cd", grad_q_in, normed_in, preferred_element_type=f32)
-    term_key = jnp.einsum("tc,td->cd", grad_k_in, normed_in, preferred_element_type=f32)
-    term_value = jnp.einsum("tc,td->cd", grad_values, normed_in, preferred_element_type=f32)
+    term_qkv = jnp.einsum(
+        "tc,td->cd",
+        jnp.concatenate([grad_q_in, grad_k_in, grad_values], axis=1),
+        normed_in,
+        preferred_element_type=f32,
+    )
     grad_normed = (
         jnp.einsum("tc,dc->td", grad_q_in, full_query, preferred_element_type=f32)
         + jnp.einsum("tc,dc->td", grad_k_in, full_key, preferred_element_type=f32)
@@ -277,7 +280,7 @@
     ffn_sums = ctx_sum(
         jnp.concatenate([shard_gate, shard_up, shard_down], axis=0).astype(low)
     ).astype(f32)
-    grad_packed = jnp.concatenate([term_query, term_key, term_value, term_output], axis=0).astype(low)
+    grad_packed = jnp.concatenate([term_qkv, term_output], axis=0).astype(low)
     grad_shard = jnp.concatenate(
         [
             lax.psum_scatter(grad_packed, "fsdp", scatter_dimension=1, tiled=True),

time: 619 us -> 626 us (1.011)
    unnamed x108 -> x118, local copies, waits for them, and re-layouts: 18 us -> 17.8 us
where the time goes in v12:
time: 626 us; the launch traced here: 619 us
  waiting for transfers between devices  309 us (49%)
  blocking collectives  106 us (17%)
  matrix products  70.5 us (11%)
  local copies, waits for them, and re-layouts  53.6 us (9%)
  starting transfers between devices  33.4 us (5%)
  other arithmetic  30.4 us (5%)
  between operations  15.5 us (2%)
    all_to_all x2, waiting for transfers between devices, a2a_sum(): pieces = lax.all_to_all(x.reshape(count, -1, *x.shape[1:]), axis_name, 0, 0)  71.8 us
    all_gather x1, waiting for transfers between devices, body(): packed_all = lax.all_gather(packed, 'fsdp', axis=0, tiled=True)  63.4 us
    all_to_all x1, blocking collectives, a2a_sum(): pieces = lax.all_to_all(x.reshape(count, -1, *x.shape[1:]), axis_name, 0, 0)  61.1 us
    all_gather x1, waiting for transfers between devices, body(): grad_all = lax.all_gather(grad_ffn, 'fsdp', axis=0, tiled=True)  55.3 us
    all_gather x1, waiting for transfers between devices, body(): rows_all = lax.all_gather(normed_pre, 'fsdp', axis=0, tiled=True)  54.3 us
    all_to_all x1, blocking collectives, ctx_sum(): lax.all_to_all(chunks, 'ctx', 0, 0).astype(f32)  45 us
    all_to_all x2, waiting for transfers between devices, ctx_sum(): lax.all_to_all(jnp.broadcast_to(mine[None], chunks.shape), 'ctx', 0, 0)  43.2 us
    unnamed x118, local copies, waits for them, and re-layouts  17.8 us
  transfers between devices with their start and end apart: 11, of which 10 were waited for; matrix products, arithmetic and copies ran while one was open for 9% of the time, Pallas kernels for 0%

profile of v12, /device:TPU:0, one launch (start us, length us, event | category | flops | bytes accessed | tf_op | source)
XLA Modules:
  0.0 618.8 jit_solution(10206907587957472870)
XLA Ops:
  16.2 63.4 %all-gather.4.cloned.1.call-done = bf16[1152,2688]{1,0:T(8,128)(2,1)} async-done(((bf16[72,2688]{1,0:T(8,128)(2,1)}), bf16[1152,2688]{1,0:T(8,128)(2,1)}) %all-gather.4.cloned.1.call-update) | async-done | bytes 6193168 | tf_op jit(solution)/shard_map/all_gather | solution.py:129
  84.1 3.4 slice_bitcast_fusion
  87.4 4.3 copy.96
  94.8 4.3 all-to-all-start
  102.2 14.1 %all-to-all-done = bf16[8,128,512]{2,1,0:T(8,128)(2,1)} async-done(((bf16[8,128,512]{2,1,0:T(8,128)(2,1)}), bf16[8,128,512]{2,1,0:T(8,128)(2,1)}, u32[]{:S(2)}, u32[]{:S(2)}) %all-to-all-start) | async-done | bytes 1048608 | tf_op jit(solution)/shard_map/all_to_all | solution.py:83
  125.8 54.3 %all-gather.6.cloned.1.call-done = bf16[2048,1152]{1,0:T(8,128)(2,1)} async-done(((bf16[128,1152]{1,0:T(8,128)(2,1)}), bf16[2048,1152]{1,0:T(8,128)(2,1)}) %all-gather.6.cloned.1.call-update) | async-done | bytes 4718608 | tf_op jit(solution)/shard_map/all_gather | solution.py:186
  180.1 5.2 fusion.109
  185.4 4.7 multiply_convert_fusion.1
  190.1 3.2 convolution_convert_fusion
  193.3 61.1 %all_to_all.45 = bf16[16,128,1152]{2,1,0:T(8,128)(2,1)S(1)} all-to-all(bf16[16,128,1152]{2,1,0:T(8,128)(2,1)S(1)} %bitcast.180), channel_id=1, replica_groups=mesh['ctx'=8,'fsdp'=16] {'fsdp'}, dimensions={0} | all-to-all | bytes 9437184 | tf_op jit(solution)/shard_map/all_to_all | solution.py:77
  257.3 55.3 %all-gather.8.cloned.1.call-done = bf16[2048,1152]{1,0:T(8,128)(2,1)} async-done(((bf16[128,1152]{1,0:T(8,128)(2,1)}), bf16[2048,1152]{1,0:T(8,128)(2,1)}) %all-gather.8.cloned.1.call-update) | async-done | bytes 4718608 | tf_op jit(solution)/shard_map/all_gather | solution.py:199
  312.6 8.5 %multiply_convert_fusion = (bf16[2048,432]{0,1:T(8,128)(2,1)S(1)}, bf16[2048,432]{0,1:T(8,128)(2,1)S(1)}) fusion(f32[2048,432]{0,1:T(8,128)} %copy-done.51, f32[2048,432]{0,1:T(8,128)} %get-tuple-element.74, bf16[2048,1152]{1,0:T(8,128)(2,1)} %all-gather.8.cloned.1.call-done, bf16[432,1152]{1,0:T(8,128)(2,1)S(1)} %copy-done), kind=kOutput, calls=%fused_computation.16 | convolution fusion | flops 2058780672 | bytes 16330752 | tf_op jit(solution)/shard_map/td,fd->tf/dot_general | solution.py:200
  324.2 4.6 add_convert_fusion
  328.7 4.8 all-to-all-start.2
  336.8 60.1 %all-to-all-done.2 = bf16[16,128,1152]{2,1,0:T(8,128)(2,1)} async-done(((bf16[16,128,1152]{2,1,0:T(8,128)(2,1)}), bf16[16,128,1152]{2,1,0:T(8,128)(2,1)}, u32[]{:S(2)}, u32[]{:S(2)}) %all-to-all-start.2) | async-done | bytes 4718624 | tf_op jit(solution)/shard_map/all_to_all | solution.py:77
  411.6 4.6 all-to-all-start.3
  420.6 11.7 %all-to-all-done.3 = bf16[8,128,512]{2,1,0:T(8,128)(2,1)} async-done(((bf16[8,128,512]{2,1,0:T(8,128)(2,1)}), bf16[8,128,512]{2,1,0:T(8,128)(2,1)}, u32[]{:S(2)}, u32[]{:S(2)}) %all-to-all-start.3) | async-done | bytes 1048608 | tf_op jit(solution)/shard_map/all_to_all | solution.py:77
  439.2 8.9 %copy.125 = bf16[2560,1152]{0,1:T(8,128)(2,1)} copy(bf16[2560,1152]{1,0:T(8,128)(2,1)} %pad_maximum_fusion) | data formatting | bytes 11796480
  448.2 5.5 convolution_convert_fusion.3
  453.7 5.2 convolution_convert_fusion.4
  463.2 3.6 convert_element_type.199
  466.8 45.0 %all_to_all.46 = bf16[8,162,1152]{2,1,0:T(8,128)(2,1)} all-to-all(bf16[8,162,1152]{2,1,0:T(8,128)(2,1)} %convert_element_type.199), channel_id=1, replica_groups=mesh['ctx'=8,'fsdp'=16] {'ctx'}, dimensions={0} | all-to-all | bytes 5971968 | tf_op jit(solution)/shard_map/all_to_all | solution.py:276
  516.1 5.0 all-to-all-start.8
  528.0 35.8 %all-to-all-done.8 = bf16[8,162,1152]{2,1,0:T(8,128)(2,1)} async-done(((bf16[8,162,1152]{2,1,0:T(8,128)(2,1)}), bf16[8,162,1152]{2,1,0:T(8,128)(2,1)}, u32[]{:S(2)}, u32[]{:S(2)}) %all-to-all-start.8) | async-done | bytes 2986016 | tf_op jit(solution)/shard_map/all_to_all | solution.py:277
  563.8 7.1 %all-to-all-start.4 = ((bf16[16,8,72]{2,1,0:T(8,128)(2,1)}), bf16[16,8,72]{2,1,0:T(8,128)(2,1)S(1)}, u32[]{:S(2)}, u32[]{:S(2)}) async-start(bf16[16,8,72]{2,1,0:T(8,128)(2,1)} %copy.108), calls=%async_computation.4 | async-start | bytes 65536 | tf_op jit(solution)/shard_map/all_to_all | solution.py:272
  570.9 4.3 reshape.345
  575.2 3.3 all-to-all-done.4
  583.1 3.5 all-to-all-start.5
  586.6 5.5 fusion.106
  592.1 3.6 all-to-all-done.5
  596.5 3.5 all-to-all-start.6
  601.0 7.4 %all-to-all-done.6 = bf16[8,321,72]{1,2,0:T(8,128)(2,1)S(1)} async-done(((bf16[8,321,72]{1,2,0:T(8,128)(2,1)}), bf16[8,321,72]{1,2,0:T(8,128)(2,1)S(1)}, u32[]{:S(2)}, u32[]{:S(2)}) %all-to-all-start.6) | async-done | bytes 369824 | tf_op jit(solution)/shard_map/all_to_all | solution.py:277
  (242 shorter events, 88.5 us)
Async XLA Ops:
  7.2 182.9 %copy-start = (bf16[432,1152]{1,0:T(8,128)(2,1)S(1)}, bf16[432,1152]{1,0:T(8,128)(2,1)}, u32[]{:S(2)}) copy-start(bf16[432,1152]{1,0:T(8,128)(2,1)} %param.27) | copy-start | bytes 2985988
  7.2 75.2 %copy-start.2 = (bf16[1,128,1152]{2,1,0:T(8,128)(2,1)S(1)}, bf16[1,128,1152]{2,1,0:T(8,128)(2,1)}, u32[]{:S(2)}) copy-start(bf16[1,128,1152]{2,1,0:T(8,128)(2,1)} %param.17) | copy-start | bytes 884740
  7.2 72.4 %all-gather.4.cloned.1.call-start = ((), (), s32[]{:S(2)}) async-start(), calls=%async_computation.10 | async-start | bytes 6580224 | tf_op jit(solution)/shard_map/all_gather | solution.py:129
  13.9 78.1 %copy-start.39 = (f32[128]{0:T(128)}, f32[128]{0:T(128)S(1)}, u32[]{:S(2)}) copy-start(f32[128]{0:T(128)S(1)} %multiply_power_fusion) | copy-start | bytes 1540
  15.3 84.0 %copy-start.31 = (f32[128]{0:T(128)}, f32[128]{0:T(128)S(1)}, u32[]{:S(2)}) copy-start(f32[128]{0:T(128)S(1)} %add_rsqrt_fusion.5) | copy-start | bytes 1540
  15.9 76.1 %copy-start.41 = (f32[128]{0:T(128)}, f32[128]{0:T(128)S(1)}, u32[]{:S(2)}) copy-start(f32[128]{0:T(128)S(1)} %convert_bitcast_fusion.1) | copy-start | bytes 1540
  16.2 102.1 %copy-start.12 = (pred[128,1024]{0,1:T(8,128)(4,1)}, pred[128,1024]{0,1:T(8,128)(4,1)S(1)}, u32[]{:S(2)}) copy-start(pred[128,1024]{0,1:T(8,128)(4,1)S(1)} %broadcast_compare_fusion.1) | copy-start | bytes 393220
  82.4 16.8 %copy-start.18 = (f32[1152]{0:T(1024)}, f32[1152]{0:T(1024)S(1)}, u32[]{:S(2)}) copy-start(f32[1152]{0:T(1024)S(1)} %get-tuple-element.36) | copy-start | bytes 13828
  82.4 41.2 %copy-start.20 = (f32[1152]{0:T(1024)}, f32[1152]{0:T(1024)S(1)}, u32[]{:S(2)}) copy-start(f32[1152]{0:T(1024)S(1)} %get-tuple-element.33) | copy-start | bytes 13828
  82.4 317.5 %copy-start.22 = (f32[1152]{0:T(1024)}, f32[1152]{0:T(1024)S(1)}, u32[]{:S(2)}) copy-start(f32[1152]{0:T(1024)S(1)} %get-tuple-element.32) | copy-start | bytes 13828
  94.8 21.4 %all-to-all-start = ((bf16[8,128,512]{2,1,0:T(8,128)(2,1)}), bf16[8,128,512]{2,1,0:T(8,128)(2,1)}, u32[]{:S(2)}, u32[]{:S(2)}) async-start(bf16[8,128,512]{2,1,0:T(8,128)(2,1)} %broadcast_in_dim.52), calls=%async_computation | async-start | bytes 2097152 | tf_op jit(solution)/shard_map/all_to_all | solution.py:83
  99.2 80.9 %all-gather.6.cloned.1.call-start = ((), (), s32[]{:S(2)}) async-start(), calls=%async_computation.11 | async-start | bytes 5013504 | tf_op jit(solution)/shard_map/all_gather | solution.py:186
  102.1 18.7 %copy-start.14 = (f32[128,4,128]{2,0,1:T(8,128)}, f32[128,4,128]{2,0,1:T(8,128)S(1)}, u32[]{:S(2)}) copy-start(f32[128,4,128]{2,0,1:T(8,128)S(1)} %get-tuple-element.53) | copy-start | bytes 786436
  119.1 214.7 %copy-start.29 = (f32[4,128]{1,0:T(4,128)}, f32[4,128]{1,0:T(4,128)S(1)}, u32[]{:S(2)}) copy-start(f32[4,128]{1,0:T(4,128)S(1)} %log_add_fusion) | copy-start | bytes 6148
  120.8 64.5 %copy-start.9 = (bf16[256,4,128]{2,0,1:T(8,128)(2,1)}, bf16[256,4,128]{2,0,1:T(8,128)(2,1)S(1)}, u32[]{:S(2)}) copy-start(bf16[256,4,128]{2,0,1:T(8,128)(2,1)S(1)} %convolution_convert_fusion.6) | copy-start | bytes 786436
  123.6 61.8 %copy-start.33 = (f32[128]{0:T(128)}, f32[128]{0:T(128)S(1)}, u32[]{:S(2)}) copy-start(f32[128]{0:T(128)S(1)} %add_rsqrt_fusion.3) | copy-start | bytes 1540
  124.7 275.2 %copy-start.38 = (f32[128]{0:T(128)}, f32[128]{0:T(128)S(1)}, u32[]{:S(2)}) copy-start(f32[128]{0:T(128)S(1)} %add_rsqrt_fusion.2) | copy-start | bytes 1540
  125.6 187.0 %all-gather.8.cloned.1.call-start = ((), (), s32[]{:S(2)}) async-start(), calls=%async_computation.12 | async-start | bytes 5013504 | tf_op jit(solution)/shard_map/all_gather | solution.py:199
  328.7 68.1 %all-to-all-start.2 = ((bf16[16,128,1152]{2,1,0:T(8,128)(2,1)}), bf16[16,128,1152]{2,1,0:T(8,128)(2,1)}, u32[]{:S(2)}, u32[]{:S(2)}) async-start(bf16[16,128,1152]{2,1,0:T(8,128)(2,1)} %bitcast.179), calls=%async_computation.2 | async-start | bytes 9437184 | tf_op jit(solution)/shard_map/all_to_all | solution.py:77
  336.8 63.5 %copy-start.6 = (f32[128,1152]{1,0:T(8,128)S(1)}, f32[128,1152]{1,0:T(8,128)}, u32[]{:S(2)}) copy-start(f32[128,1152]{1,0:T(8,128)} %copy-done.5) | copy-start | bytes 1769476
  336.8 63.5 %copy-start.21 = (f32[1152]{0:T(1024)S(1)}, f32[1152]{0:T(1024)}, u32[]{:S(2)}) copy-start(f32[1152]{0:T(1024)} %copy-done.20) | copy-start | bytes 13828
  336.8 63.5 %copy-start.34 = (f32[128]{0:T(128)S(1)}, f32[128]{0:T(128)}, u32[]{:S(2)}) copy-start(f32[128]{0:T(128)} %copy-done.33) | copy-start | bytes 1540
  411.6 20.7 %all-to-all-start.3 = ((bf16[8,128,512]{2,1,0:T(8,128)(2,1)}), bf16[8,128,512]{2,1,0:T(8,128)(2,1)}, u32[]{:S(2)}, u32[]{:S(2)}) async-start(bf16[8,128,512]{2,1,0:T(8,128)(2,1)} %pad_maximum_fusion.2), calls=%async_computation.3 | async-start | bytes 2097152 | tf_op jit(solution)/shard_map/all_to_all | solution.py:77
  416.2 162.4 %reduce-scatter.4.cloned.1.call-start = ((), (), s32[]{:S(2)}) async-start(), calls=%async_computation.13 | async-start | bytes 6266880
  417.6 16.4 %copy-start.24 = (f32[256]{0:T(256)S(1)}, f32[256]{0:T(256)}, u32[]{:S(2)}) copy-start(f32[256]{0:T(256)} %copy-done.23) | copy-start | bytes 3076
  417.6 16.4 %copy-start.37 = (f32[128]{0:T(128)S(1)}, f32[128]{0:T(128)}, u32[]{:S(2)}) copy-start(f32[128]{0:T(128)} %copy-done.36) | copy-start | bytes 1540
  418.0 16.7 %copy-start.19 = (f32[1152]{0:T(1024)S(1)}, f32[1152]{0:T(1024)}, u32[]{:S(2)}) copy-start(f32[1152]{0:T(1024)} %copy-done.18) | copy-start | bytes 13828
  418.0 16.7 %copy-start.32 = (f32[128]{0:T(128)S(1)}, f32[128]{0:T(128)}, u32[]{:S(2)}) copy-start(f32[128]{0:T(128)} %copy-done.31) | copy-start | bytes 1540
  516.1 47.7 %all-to-all-start.8 = ((bf16[8,162,1152]{2,1,0:T(8,128)(2,1)}), bf16[8,162,1152]{2,1,0:T(8,128)(2,1)}, u32[]{:S(2)}, u32[]{:S(2)}) async-start(bf16[8,162,1152]{2,1,0:T(8,128)(2,1)} %broadcast_in_dim.65), calls=%async_computation.8 | async-start | bytes 6193152 | tf_op jit(solution)/shard_map/all_to_all | solution.py:277
  563.8 14.7 %all-to-all-start.4 = ((bf16[16,8,72]{2,1,0:T(8,128)(2,1)}), bf16[16,8,72]{2,1,0:T(8,128)(2,1)S(1)}, u32[]{:S(2)}, u32[]{:S(2)}) async-start(bf16[16,8,72]{2,1,0:T(8,128)(2,1)} %copy.108), calls=%async_computation.4 | async-start | bytes 65536 | tf_op jit(solution)/shard_map/all_to_all | solution.py:272
  583.1 12.5 %all-to-all-start.5 = ((bf16[8,321,72]{1,2,0:T(8,128)(2,1)}), bf16[8,321,72]{1,2,0:T(8,128)(2,1)S(1)}, u32[]{:S(2)}, u32[]{:S(2)}) async-start(bf16[8,321,72]{1,2,0:T(8,128)(2,1)} %copy.110), calls=%async_computation.5 | async-start | bytes 884736 | tf_op jit(solution)/shard_map/all_to_all | solution.py:276
  596.5 11.9 %all-to-all-start.6 = ((bf16[8,321,72]{1,2,0:T(8,128)(2,1)}), bf16[8,321,72]{1,2,0:T(8,128)(2,1)S(1)}, u32[]{:S(2)}, u32[]{:S(2)}) async-start(bf16[8,321,72]{1,2,0:T(8,128)(2,1)} %broadcast_in_dim.64), calls=%async_computation.6 | async-start | bytes 884736 | tf_op jit(solution)/shard_map/all_to_all | solution.py:277
  (34 other events, 202.2 us)
Sparse Core Ops, SparseCore 0:
  13.2 66.3 all-gather.3
  125.7 54.3 all-gather.5
  257.4 55.1 all-gather.7
  448.3 123.4 reduce-scatter.3

commit v13 on v5

--- a/solution.py
+++ b/solution.py
@@ -274,9 +274,11 @@
         return lax.all_to_all(jnp.broadcast_to(mine[None], chunks.shape), "ctx", 0, 0).reshape(x.shape)
 
     ffn_units = shard_gate.shape[0]
-    ffn_sums = ctx_sum(
-        jnp.concatenate([shard_gate, shard_up, shard_down], axis=0).astype(low)
-    ).astype(f32)
+    ffn_packed = jnp.concatenate([shard_gate, shard_up, shard_down], axis=0).astype(low)
+    ffn_rows = ffn_packed.shape[0]
+    ffn_packed = jnp.pad(ffn_packed, ((0, -ffn_rows % (8 * parts)), (0, 0)))
+    ffn_mine = a2a_sum(ffn_packed, "ctx", parts).astype(low)
+    ffn_sums = lax.all_gather(ffn_mine, "ctx", axis=0, tiled=True)[:ffn_rows].astype(f32)
     grad_packed = jnp.concatenate([term_query, term_key, term_value, term_output], axis=0).astype(low)
     grad_shard = jnp.concatenate(
         [

time: 619 us -> 663 us (1.071)
  waiting for transfers between devices: 304 us -> 351 us
  local copies, waits for them, and re-layouts: 54.4 us -> 44.7 us
  other arithmetic: 31.3 us -> 40.7 us
    all_gather x0 -> x1, waiting for transfers between devices: none -> 67.3 us  [body(): lax.all_gather(ffn_mine, 'ctx', axis=0, tiled=True)[:ffn_rows].astype(f32)]
    all_to_all x1 -> x0, blocking collectives: 44.3 us -> none  [ctx_sum(): lax.all_to_all(chunks, 'ctx', 0, 0).astype(f32)]
    all_to_all x1 -> x2, blocking collectives: 61.1 us -> 105 us  [a2a_sum(): pieces = lax.all_to_all(x.reshape(count, -1, *x.shape[1:]), axis_name, 0, 0)]
    all_to_all x2 -> x1, waiting for transfers between devices: 43 us -> 2.82 us  [ctx_sum(): lax.all_to_all(jnp.broadcast_to(mine[None], chunks.shape), 'ctx', 0, 0)]
    unnamed x5 -> x6, waiting for transfers between devices: 0.08 us -> 20.1 us
    convert_element_type x2 -> x0, local copies, waits for them, and re-layouts: 7.86 us -> none  [the longest x1 4.28 us: body(): ffn_sums = ctx_sum(jnp.concatenate([shard_gate, shard_up, shard_down], ax...]
where the time goes in v13:
time: 663 us; the launch traced here: 656 us
  waiting for transfers between devices  351 us (53%)
  blocking collectives  105 us (16%)
  matrix products  69.6 us (10%)
  local copies, waits for them, and re-layouts  44.7 us (7%)
  other arithmetic  40.7 us (6%)
  starting transfers between devices  29.8 us (4%)
  between operations  15.4 us (2%)
    all_to_all x2, blocking collectives, a2a_sum(): pieces = lax.all_to_all(x.reshape(count, -1, *x.shape[1:]), axis_name, 0, 0)  105 us
    all_to_all x2, waiting for transfers between devices, a2a_sum(): pieces = lax.all_to_all(x.reshape(count, -1, *x.shape[1:]), axis_name, 0, 0)  68 us
    all_gather x1, waiting for transfers between devices, body(): lax.all_gather(ffn_mine, 'ctx', axis=0, tiled=True)[:ffn_rows].astype(f32)  67.3 us
    all_gather x1, waiting for transfers between devices, body(): packed_all = lax.all_gather(packed, 'fsdp', axis=0, tiled=True)  63.4 us
    all_gather x1, waiting for transfers between devices, body(): grad_all = lax.all_gather(grad_ffn, 'fsdp', axis=0, tiled=True)  55.3 us
    all_gather x1, waiting for transfers between devices, body(): rows_all = lax.all_gather(normed_pre, 'fsdp', axis=0, tiled=True)  54.2 us
    unnamed x6, waiting for transfers between devices  20.1 us
    unnamed x108, local copies, waits for them, and re-layouts  18 us
  transfers between devices with their start and end apart: 11, of which 10 were waited for; matrix products, arithmetic and copies ran while one was open for 9% of the time, Pallas kernels for 0%

profile of v13, /device:TPU:0, one launch (start us, length us, event | category | flops | bytes accessed | tf_op | source)
XLA Modules:
  0.0 655.6 jit_solution(2675881509462732657)
XLA Ops:
  16.2 63.4 %all-gather.5.cloned.1.call-done = bf16[1152,2688]{1,0:T(8,128)(2,1)} async-done(((bf16[72,2688]{1,0:T(8,128)(2,1)}), bf16[1152,2688]{1,0:T(8,128)(2,1)}) %all-gather.5.cloned.1.call-update) | async-done | bytes 6193168 | tf_op jit(solution)/shard_map/all_gather | solution.py:129
  84.0 3.3 slice_bitcast_fusion
  87.3 4.3 copy.90
  94.8 4.3 all-to-all-start
  102.9 13.0 %all-to-all-done = bf16[8,128,512]{2,1,0:T(8,128)(2,1)S(1)} async-done(((bf16[8,128,512]{2,1,0:T(8,128)(2,1)}), bf16[8,128,512]{2,1,0:T(8,128)(2,1)S(1)}, u32[]{:S(2)}, u32[]{:S(2)}) %all-to-all-start) | async-done | bytes 1048608 | tf_op jit(solution)/shard_map/all_to_all | solution.py:83
  122.9 54.2 %all-gather.7.cloned.1.call-done = bf16[2048,1152]{1,0:T(8,128)(2,1)} async-done(((bf16[128,1152]{1,0:T(8,128)(2,1)}), bf16[2048,1152]{1,0:T(8,128)(2,1)}) %all-gather.7.cloned.1.call-update) | async-done | bytes 4718608 | tf_op jit(solution)/shard_map/all_gather | solution.py:186
  177.1 5.2 fusion.108
  182.4 4.7 multiply_convert_fusion.1
  187.1 3.2 convolution_convert_fusion
  190.3 61.1 %all_to_all.40 = bf16[16,128,1152]{2,1,0:T(8,128)(2,1)S(1)} all-to-all(bf16[16,128,1152]{2,1,0:T(8,128)(2,1)S(1)} %bitcast.187), channel_id=1, replica_groups=mesh['ctx'=8,'fsdp'=16] {'fsdp'}, dimensions={0} | all-to-all | bytes 9437184 | tf_op jit(solution)/shard_map/all_to_all | solution.py:77
  253.7 55.3 %all-gather.9.cloned.1.call-done = bf16[2048,1152]{1,0:T(8,128)(2,1)} async-done(((bf16[128,1152]{1,0:T(8,128)(2,1)}), bf16[2048,1152]{1,0:T(8,128)(2,1)}) %all-gather.9.cloned.1.call-update) | async-done | bytes 4718608 | tf_op jit(solution)/shard_map/all_gather | solution.py:199
  309.0 8.5 %multiply_convert_fusion = (bf16[2048,432]{0,1:T(8,128)(2,1)S(1)}, bf16[2048,432]{0,1:T(8,128)(2,1)S(1)}) fusion(f32[2048,432]{0,1:T(8,128)} %copy-done.46, f32[2048,432]{0,1:T(8,128)} %get-tuple-element.74, bf16[2048,1152]{1,0:T(8,128)(2,1)} %all-gather.9.cloned.1.call-done, bf16[432,1152]{1,0:T(8,128)(2,1)S(1)} %copy-done), kind=kOutput, calls=%fused_computation.20 | convolution fusion | flops 2058780672 | bytes 16330752 | tf_op jit(solution)/shard_map/td,fd->tf/dot_general | solution.py:200
  320.6 4.6 add_convert_fusion
  325.2 4.8 all-to-all-start.2
  333.1 60.1 %all-to-all-done.2 = bf16[16,128,1152]{2,1,0:T(8,128)(2,1)} async-done(((bf16[16,128,1152]{2,1,0:T(8,128)(2,1)}), bf16[16,128,1152]{2,1,0:T(8,128)(2,1)}, u32[]{:S(2)}, u32[]{:S(2)}) %all-to-all-start.2) | async-done | bytes 4718624 | tf_op jit(solution)/shard_map/all_to_all | solution.py:77
  409.7 4.7 all-to-all-start.3
  422.5 7.9 %all-to-all-done.3 = bf16[8,128,512]{2,1,0:T(8,128)(2,1)S(1)} async-done(((bf16[8,128,512]{2,1,0:T(8,128)(2,1)}), bf16[8,128,512]{2,1,0:T(8,128)(2,1)S(1)}, u32[]{:S(2)}, u32[]{:S(2)}) %all-to-all-start.3) | async-done | bytes 1048608 | tf_op jit(solution)/shard_map/all_to_all | solution.py:77
  432.1 4.6 pad_maximum_fusion
  436.7 8.9 %copy.117 = bf16[2560,1152]{0,1:T(8,128)(2,1)} copy(bf16[2560,1152]{1,0:T(8,128)(2,1)} %pad_maximum_fusion) | data formatting | bytes 11796480
  445.9 5.5 convolution_convert_fusion.3
  451.4 5.2 convolution_convert_fusion.4
  459.2 5.8 fusion.11
  465.0 43.7 %all_to_all.41 = bf16[8,168,1152]{2,1,0:T(8,128)(2,1)} all-to-all(bf16[8,168,1152]{2,1,0:T(8,128)(2,1)S(1)} %bitcast.184), channel_id=1, replica_groups=mesh['ctx'=8,'fsdp'=16] {'ctx'}, dimensions={0} | all-to-all | bytes 6193152 | tf_op jit(solution)/shard_map/all_to_all | solution.py:77
  508.7 3.1 reduce_sum.288
  518.8 7.2 %all-to-all-start.4 = ((bf16[16,8,72]{2,1,0:T(8,128)(2,1)}), bf16[16,8,72]{2,1,0:T(8,128)(2,1)S(1)}, u32[]{:S(2)}, u32[]{:S(2)}) async-start(bf16[16,8,72]{2,1,0:T(8,128)(2,1)} %copy.100), calls=%async_computation.4 | async-start | bytes 65536 | tf_op jit(solution)/shard_map/all_to_all | solution.py:269
  526.9 6.6 %all-to-all-done.4 = bf16[16,8,72]{2,1,0:T(8,128)(2,1)S(1)} async-done(((bf16[16,8,72]{2,1,0:T(8,128)(2,1)}), bf16[16,8,72]{2,1,0:T(8,128)(2,1)S(1)}, u32[]{:S(2)}, u32[]{:S(2)}) %all-to-all-start.4) | async-done | bytes 18464 | tf_op jit(solution)/shard_map/all_to_all | solution.py:269
  533.6 20.0 %reduce-scatter.4.cloned.1.call-done = bf16[72,2560]{1,0:T(8,128)(2,1)} async-done(((bf16[1152,2560]{1,0:T(8,128)(2,1)}), bf16[72,2560]{1,0:T(8,128)(2,1)}) %reduce-scatter.4.cloned.1.call-update) | async-done | bytes 368656
  556.2 4.3 all-to-all-start.5
  560.5 67.3 %all-gather.11.cloned.1.call-done = bf16[1344,1152]{1,0:T(8,128)(2,1)} async-done(((bf16[168,1152]{1,0:T(8,128)(2,1)}), bf16[1344,1152]{1,0:T(8,128)(2,1)}) %all-gather.11.cloned.1.call-update) | async-done | bytes 3096592 | tf_op jit(solution)/shard_map/all_gather | solution.py:281
  627.8 4.8 slice_convert_fusion
  633.4 3.5 all-to-all-start.6
  636.9 5.6 fusion.106
  (230 shorter events, 81.6 us)
Async XLA Ops:
  7.2 179.9 %copy-start = (bf16[432,1152]{1,0:T(8,128)(2,1)S(1)}, bf16[432,1152]{1,0:T(8,128)(2,1)}, u32[]{:S(2)}) copy-start(bf16[432,1152]{1,0:T(8,128)(2,1)} %param.27) | copy-start | bytes 2985988
  7.2 75.2 %copy-start.2 = (bf16[1,128,1152]{2,1,0:T(8,128)(2,1)S(1)}, bf16[1,128,1152]{2,1,0:T(8,128)(2,1)}, u32[]{:S(2)}) copy-start(bf16[1,128,1152]{2,1,0:T(8,128)(2,1)} %param.17) | copy-start | bytes 884740
  7.2 72.4 %all-gather.5.cloned.1.call-start = ((), (), s32[]{:S(2)}) async-start(), calls=%async_computation.9 | async-start | bytes 6580224 | tf_op jit(solution)/shard_map/all_gather | solution.py:129
  13.9 78.0 %copy-start.34 = (f32[128]{0:T(128)}, f32[128]{0:T(128)S(1)}, u32[]{:S(2)}) copy-start(f32[128]{0:T(128)S(1)} %multiply_power_fusion) | copy-start | bytes 1540
  15.9 76.0 %copy-start.36 = (f32[128]{0:T(128)}, f32[128]{0:T(128)S(1)}, u32[]{:S(2)}) copy-start(f32[128]{0:T(128)S(1)} %convert_bitcast_fusion.1) | copy-start | bytes 1540
  16.2 100.7 %copy-start.24 = (pred[128,1024]{0,1:T(8,128)(4,1)}, pred[128,1024]{0,1:T(8,128)(4,1)S(1)}, u32[]{:S(2)}) copy-start(pred[128,1024]{0,1:T(8,128)(4,1)S(1)} %broadcast_compare_fusion.1) | copy-start | bytes 393220
  92.3 10.5 %copy-start.20 = (f32[128,128]{1,0:T(8,128)}, f32[128,128]{1,0:T(8,128)S(1)}, u32[]{:S(2)}) copy-start(f32[128,128]{1,0:T(8,128)S(1)} %get-tuple-element.61) | copy-start | bytes 196612
  92.3 10.5 %copy-start.22 = (f32[128,128]{1,0:T(8,128)}, f32[128,128]{1,0:T(8,128)S(1)}, u32[]{:S(2)}) copy-start(f32[128,128]{1,0:T(8,128)S(1)} %get-tuple-element.62) | copy-start | bytes 196612
  94.8 21.1 %all-to-all-start = ((bf16[8,128,512]{2,1,0:T(8,128)(2,1)}), bf16[8,128,512]{2,1,0:T(8,128)(2,1)S(1)}, u32[]{:S(2)}, u32[]{:S(2)}) async-start(bf16[8,128,512]{2,1,0:T(8,128)(2,1)} %broadcast_in_dim.50), calls=%async_computation | async-start | bytes 2097152 | tf_op jit(solution)/shard_map/all_to_all | solution.py:83
  99.1 77.9 %all-gather.7.cloned.1.call-start = ((), (), s32[]{:S(2)}) async-start(), calls=%async_computation.10 | async-start | bytes 5013504 | tf_op jit(solution)/shard_map/all_gather | solution.py:186
  102.9 13.9 %copy-start.25 = (f32[128,4,128]{2,0,1:T(8,128)}, f32[128,4,128]{2,0,1:T(8,128)S(1)}, u32[]{:S(2)}) copy-start(f32[128,4,128]{2,0,1:T(8,128)S(1)} %get-tuple-element.53) | copy-start | bytes 786436
  102.9 15.4 %copy-start.27 = (f32[128,4,128]{2,0,1:T(8,128)}, f32[128,4,128]{2,0,1:T(8,128)S(1)}, u32[]{:S(2)}) copy-start(f32[128,4,128]{2,0,1:T(8,128)S(1)} %get-tuple-element.54) | copy-start | bytes 786436
  117.7 212.5 %copy-start.29 = (f32[4,128]{1,0:T(4,128)}, f32[4,128]{1,0:T(4,128)S(1)}, u32[]{:S(2)}) copy-start(f32[4,128]{1,0:T(4,128)S(1)} %log_add_fusion) | copy-start | bytes 6148
  118.3 64.0 %copy-start.15 = (bf16[256,4,128]{2,0,1:T(8,128)(2,1)}, bf16[256,4,128]{2,0,1:T(8,128)(2,1)S(1)}, u32[]{:S(2)}) copy-start(bf16[256,4,128]{2,0,1:T(8,128)(2,1)S(1)} %convolution_convert_fusion.8) | copy-start | bytes 786436
  121.1 275.5 %copy-start.10 = (f32[128,1152]{1,0:T(8,128)}, f32[128,1152]{1,0:T(8,128)S(1)}, u32[]{:S(2)}) copy-start(f32[128,1152]{1,0:T(8,128)S(1)} %get-tuple-element.72) | copy-start | bytes 1769476
  121.1 275.5 %copy-start.31 = (f32[128]{0:T(128)}, f32[128]{0:T(128)S(1)}, u32[]{:S(2)}) copy-start(f32[128]{0:T(128)S(1)} %add_rsqrt_fusion.3) | copy-start | bytes 1540
  122.3 186.7 %all-gather.9.cloned.1.call-start = ((), (), s32[]{:S(2)}) async-start(), calls=%async_computation.11 | async-start | bytes 5013504 | tf_op jit(solution)/shard_map/all_gather | solution.py:199
  309.0 8.6 %copy-start.39 = (bf16[432,1152]{1,0:T(8,128)(2,1)S(1)}, bf16[432,1152]{1,0:T(8,128)(2,1)}, u32[]{:S(2)}) copy-start(bf16[432,1152]{1,0:T(8,128)(2,1)} %param.25) | copy-start | bytes 2985988
  325.2 68.1 %all-to-all-start.2 = ((bf16[16,128,1152]{2,1,0:T(8,128)(2,1)}), bf16[16,128,1152]{2,1,0:T(8,128)(2,1)}, u32[]{:S(2)}, u32[]{:S(2)}) async-start(bf16[16,128,1152]{2,1,0:T(8,128)(2,1)} %bitcast.186), calls=%async_computation.2 | async-start | bytes 9437184 | tf_op jit(solution)/shard_map/all_to_all | solution.py:77
  397.0 9.3 %copy-start.8 = (f32[128,1152]{1,0:T(8,128)}, f32[128,1152]{1,0:T(8,128)S(1)}, u32[]{:S(2)}) copy-start(f32[128,1152]{1,0:T(8,128)S(1)} %get-tuple-element.39) | copy-start | bytes 1769476
  409.7 20.7 %all-to-all-start.3 = ((bf16[8,128,512]{2,1,0:T(8,128)(2,1)}), bf16[8,128,512]{2,1,0:T(8,128)(2,1)S(1)}, u32[]{:S(2)}, u32[]{:S(2)}) async-start(bf16[8,128,512]{2,1,0:T(8,128)(2,1)} %pad_maximum_fusion.1), calls=%async_computation.3 | async-start | bytes 2097152 | tf_op jit(solution)/shard_map/all_to_all | solution.py:77
  414.4 139.2 %reduce-scatter.4.cloned.1.call-start = ((), (), s32[]{:S(2)}) async-start(), calls=%async_computation.13 | async-start | bytes 6266880
  417.9 12.7 %copy-start.35 = (f32[128]{0:T(128)S(1)}, f32[128]{0:T(128)}, u32[]{:S(2)}) copy-start(f32[128]{0:T(128)} %copy-done.34) | copy-start | bytes 1540
  417.9 12.7 %copy-start.37 = (f32[128]{0:T(128)S(1)}, f32[128]{0:T(128)}, u32[]{:S(2)}) copy-start(f32[128]{0:T(128)} %copy-done.36) | copy-start | bytes 1540
  417.9 13.4 %copy-start.33 = (f32[128]{0:T(128)S(1)}, f32[128]{0:T(128)}, u32[]{:S(2)}) copy-start(f32[128]{0:T(128)} %copy-done.32) | copy-start | bytes 1540
  445.6 182.2 %all-gather.11.cloned.1.call-start = ((), (), s32[]{:S(2)}) async-start(), calls=%async_computation.12 | async-start | bytes 3483648 | tf_op jit(solution)/shard_map/all_gather | solution.py:281
  445.9 10.7 %slice-start = ((s8[4718592]{0:T(1024)(128)(4,1)}), s8[4194304]{0:T(1024)(128)(4,1)S(1)}, s32[]{:S(2)}) async-start(s8[4718592]{0:T(1024)(128)(4,1)} %bitcast.209), calls=%async_computation.14 | async-start | bytes 8388608
  512.1 13.8 %copy-start.9 = (f32[128,1152]{1,0:T(8,128)S(1)}, f32[128,1152]{1,0:T(8,128)}, u32[]{:S(2)}) copy-start(f32[128,1152]{1,0:T(8,128)} %copy-done.8) | copy-start | bytes 1769476
  518.8 14.8 %all-to-all-start.4 = ((bf16[16,8,72]{2,1,0:T(8,128)(2,1)}), bf16[16,8,72]{2,1,0:T(8,128)(2,1)S(1)}, u32[]{:S(2)}, u32[]{:S(2)}) async-start(bf16[16,8,72]{2,1,0:T(8,128)(2,1)} %copy.100), calls=%async_computation.4 | async-start | bytes 65536 | tf_op jit(solution)/shard_map/all_to_all | solution.py:269
  556.2 76.3 %all-to-all-start.5 = ((bf16[8,321,72]{1,2,0:T(8,128)(2,1)}), bf16[8,321,72]{1,2,0:T(8,128)(2,1)S(1)}, u32[]{:S(2)}, u32[]{:S(2)}) async-start(bf16[8,321,72]{1,2,0:T(8,128)(2,1)} %copy.102), calls=%async_computation.5 | async-start | bytes 884736 | tf_op jit(solution)/shard_map/all_to_all | solution.py:273
  633.4 11.9 %all-to-all-start.6 = ((bf16[8,321,72]{1,2,0:T(8,128)(2,1)}), bf16[8,321,72]{1,2,0:T(8,128)(2,1)S(1)}, u32[]{:S(2)}, u32[]{:S(2)}) async-start(bf16[8,321,72]{1,2,0:T(8,128)(2,1)} %broadcast_in_dim.100), calls=%async_computation.6 | async-start | bytes 884736 | tf_op jit(solution)/shard_map/all_to_all | solution.py:274
  636.9 11.7 %copy-start.1 = (bf16[432,1152]{1,0:T(8,128)(2,1)S(1)}, bf16[432,1152]{1,0:T(8,128)(2,1)}, u32[]{:S(2)}) copy-start(bf16[432,1152]{1,0:T(8,128)(2,1)} %param.27) | copy-start | bytes 2985988
  (29 other events, 123.5 us)
Sparse Core Ops, SparseCore 0:
  13.2 66.3 all-gather.4
  122.4 54.6 all-gather.6
  253.8 55.1 all-gather.8
  445.7 107.7 reduce-scatter.3
  555.8 71.9 all-gather.10

commit v14 on v11

--- a/solution.py
+++ b/solution.py
@@ -183,7 +183,7 @@
     residual = flat_in + attn_normed
     pre_full, pre_unit, pre_inv = norm_forward(residual, norm_pre)
     normed_pre = pre_full.astype(low)
-    rows_all = a2a_gather(normed_pre, "fsdp", groups)
+    rows_all = lax.all_gather(normed_pre, "fsdp", axis=0, tiled=True)
     gate = jnp.einsum("td,fd->tf", rows_all, w_gate, preferred_element_type=f32)
     upper = jnp.einsum("td,fd->tf", rows_all, w_up, preferred_element_type=f32)
     gelu_value, gelu_slope = gelu_pair(gate)

time: 623 us -> 617 us (level)
  blocking collectives: 227 us -> 165 us
  waiting for transfers between devices: 195 us -> 248 us
    all_to_all x2 -> x1, blocking collectives: 122 us -> 60.2 us  [a2a_gather(): lax.all_to_all(copies, axis_name, 0, 0)]
    all_gather x0 -> x1, waiting for transfers between devices: none -> 54.8 us  [body(): rows_all = lax.all_gather(normed_pre, 'fsdp', axis=0, tiled=True)]
  transfers between devices with their start and end apart: 9 -> 10, of which waited for: 8 -> 9; matrix products, arithmetic and copies ran while one was open for 9% -> 9% of each run, Pallas kernels for 0% -> 0%
where the time goes in v14:
time: 617 us; the launch traced here: 612 us
  waiting for transfers between devices  248 us (40%)
  blocking collectives  165 us (27%)
  matrix products  61.3 us (10%)
  local copies, waits for them, and re-layouts  55.1 us (9%)
  starting transfers between devices  35.5 us (6%)
  other arithmetic  31.1 us (5%)
  between operations  15 us (2%)
    all_to_all x2, waiting for transfers between devices, a2a_sum(): pieces = lax.all_to_all(x.reshape(count, -1, *x.shape[1:]), axis_name, 0, 0)  67.4 us
    all_gather x1, waiting for transfers between devices, body(): packed_all = lax.all_gather(packed, 'fsdp', axis=0, tiled=True)  63.4 us
    all_to_all x1, blocking collectives, a2a_sum(): pieces = lax.all_to_all(x.reshape(count, -1, *x.shape[1:]), axis_name, 0, 0)  60.9 us
    all_to_all x1, blocking collectives, a2a_gather(): lax.all_to_all(copies, axis_name, 0, 0)  60.2 us
    all_gather x1, waiting for transfers between devices, body(): rows_all = lax.all_gather(normed_pre, 'fsdp', axis=0, tiled=True)  54.8 us
    all_to_all x1, blocking collectives, ctx_sum(): lax.all_to_all(chunks, 'ctx', 0, 0).astype(f32)  44.3 us
    all_to_all x2, waiting for transfers between devices, ctx_sum(): lax.all_to_all(jnp.broadcast_to(mine[None], chunks.shape), 'ctx', 0, 0)  43 us
    unnamed x106, local copies, waits for them, and re-layouts  18 us
  transfers between devices with their start and end apart: 10, of which 9 were waited for; matrix products, arithmetic and copies ran while one was open for 9% of the time, Pallas kernels for 0%

profile of v14, /device:TPU:0, one launch (start us, length us, event | category | flops | bytes accessed | tf_op | source)
XLA Modules:
  0.0 611.8 jit_solution(8419735347400589756)
XLA Ops:
  16.2 63.4 %all-gather.3.cloned.1.call-done = bf16[1152,2688]{1,0:T(8,128)(2,1)} async-done(((bf16[72,2688]{1,0:T(8,128)(2,1)}), bf16[1152,2688]{1,0:T(8,128)(2,1)}) %all-gather.3.cloned.1.call-update) | async-done | bytes 6193168 | tf_op jit(solution)/shard_map/all_gather | solution.py:129
  84.0 3.3 slice_bitcast_fusion
  87.3 4.3 copy.90
  94.8 4.3 all-to-all-start
  103.1 12.8 %all-to-all-done = bf16[8,128,512]{2,1,0:T(8,128)(2,1)S(1)} async-done(((bf16[8,128,512]{2,1,0:T(8,128)(2,1)}), bf16[8,128,512]{2,1,0:T(8,128)(2,1)S(1)}, u32[]{:S(2)}, u32[]{:S(2)}) %all-to-all-start) | async-done | bytes 1048608 | tf_op jit(solution)/shard_map/all_to_all | solution.py:83
  122.3 54.8 %all-gather.5.cloned.1.call-done = bf16[2048,1152]{1,0:T(8,128)(2,1)} async-done(((bf16[128,1152]{1,0:T(8,128)(2,1)}), bf16[2048,1152]{1,0:T(8,128)(2,1)}) %all-gather.5.cloned.1.call-update) | async-done | bytes 4718608 | tf_op jit(solution)/shard_map/all_gather | solution.py:186
  177.1 5.3 fusion.109
  185.3 3.2 convolution_convert_fusion
  188.5 60.9 %all_to_all.50 = bf16[16,128,1152]{2,1,0:T(8,128)(2,1)S(1)} all-to-all(bf16[16,128,1152]{2,1,0:T(8,128)(2,1)S(1)} %bitcast.206), channel_id=1, replica_groups=mesh['ctx'=8,'fsdp'=16] {'fsdp'}, dimensions={0} | all-to-all | bytes 9437184 | tf_op jit(solution)/shard_map/all_to_all | solution.py:77
  252.2 60.2 %all_to_all.51 = bf16[16,128,1152]{2,1,0:T(8,128)(2,1)S(1)} all-to-all(bf16[16,128,1152]{2,1,0:T(8,128)(2,1)S(1)} %broadcast_in_dim.66), channel_id=1, replica_groups=mesh['ctx'=8,'fsdp'=16] {'fsdp'}, dimensions={0} | all-to-all | bytes 9437184 | tf_op jit(solution)/shard_map/all_to_all | solution.py:83
  312.4 4.6 multiply_convert_fusion
  320.1 4.8 add_convert_fusion
  324.8 4.6 all-to-all-start.3
  332.6 60.1 %all-to-all-done.3 = bf16[16,128,1152]{2,1,0:T(8,128)(2,1)} async-done(((bf16[16,128,1152]{2,1,0:T(8,128)(2,1)}), bf16[16,128,1152]{2,1,0:T(8,128)(2,1)}, u32[]{:S(2)}, u32[]{:S(2)}) %all-to-all-start.3) | async-done | bytes 4718624 | tf_op jit(solution)/shard_map/all_to_all | solution.py:77
  392.7 3.1 convert_reduce_fusion
  409.2 5.2 all-to-all-start.4
  422.9 7.3 %all-to-all-done.4 = bf16[8,128,512]{2,1,0:T(8,128)(2,1)S(1)} async-done(((bf16[8,128,512]{2,1,0:T(8,128)(2,1)}), bf16[8,128,512]{2,1,0:T(8,128)(2,1)S(1)}, u32[]{:S(2)}, u32[]{:S(2)}) %all-to-all-start.4) | async-done | bytes 1048608 | tf_op jit(solution)/shard_map/all_to_all | solution.py:77
  431.9 4.6 pad_maximum_fusion
  436.5 8.9 %copy.117 = bf16[2560,1152]{0,1:T(8,128)(2,1)} copy(bf16[2560,1152]{1,0:T(8,128)(2,1)} %pad_maximum_fusion) | data formatting | bytes 11796480
  445.4 5.5 convolution_convert_fusion.3
  457.7 3.6 convert_element_type.207
  461.4 44.3 %all_to_all.52 = bf16[8,162,1152]{2,1,0:T(8,128)(2,1)} all-to-all(bf16[8,162,1152]{2,1,0:T(8,128)(2,1)} %convert_element_type.207), channel_id=1, replica_groups=mesh['ctx'=8,'fsdp'=16] {'ctx'}, dimensions={0} | all-to-all | bytes 5971968 | tf_op jit(solution)/shard_map/all_to_all | solution.py:273
  509.9 5.1 all-to-all-start.9
  521.8 35.6 %all-to-all-done.9 = bf16[8,162,1152]{2,1,0:T(8,128)(2,1)} async-done(((bf16[8,162,1152]{2,1,0:T(8,128)(2,1)}), bf16[8,162,1152]{2,1,0:T(8,128)(2,1)}, u32[]{:S(2)}, u32[]{:S(2)}) %all-to-all-start.9) | async-done | bytes 2986016 | tf_op jit(solution)/shard_map/all_to_all | solution.py:274
  557.4 8.8 %all-to-all-start.5 = ((bf16[16,8,72]{2,1,0:T(8,128)(2,1)}), bf16[16,8,72]{2,1,0:T(8,128)(2,1)S(1)}, u32[]{:S(2)}, u32[]{:S(2)}) async-start(bf16[16,8,72]{2,1,0:T(8,128)(2,1)} %copy.100), calls=%async_computation.5 | async-start | bytes 65536 | tf_op jit(solution)/shard_map/all_to_all | solution.py:269
  566.1 4.3 reshape.425
  570.4 3.3 all-to-all-done.5
  576.4 3.5 all-to-all-start.6
  579.9 5.5 fusion.107
  585.4 3.5 all-to-all-done.6
  589.9 3.5 all-to-all-start.7
  594.3 7.4 %all-to-all-done.7 = bf16[8,321,72]{1,2,0:T(8,128)(2,1)S(1)} async-done(((bf16[8,321,72]{1,2,0:T(8,128)(2,1)}), bf16[8,321,72]{1,2,0:T(8,128)(2,1)S(1)}, u32[]{:S(2)}, u32[]{:S(2)}) %all-to-all-start.7) | async-done | bytes 369824 | tf_op jit(solution)/shard_map/all_to_all | solution.py:274
  (228 shorter events, 87.3 us)
Async XLA Ops:
  7.2 178.1 %copy-start = (bf16[432,1152]{1,0:T(8,128)(2,1)S(1)}, bf16[432,1152]{1,0:T(8,128)(2,1)}, u32[]{:S(2)}) copy-start(bf16[432,1152]{1,0:T(8,128)(2,1)} %param.27) | copy-start | bytes 2985988
  7.2 75.2 %copy-start.2 = (bf16[1,128,1152]{2,1,0:T(8,128)(2,1)S(1)}, bf16[1,128,1152]{2,1,0:T(8,128)(2,1)}, u32[]{:S(2)}) copy-start(bf16[1,128,1152]{2,1,0:T(8,128)(2,1)} %param.17) | copy-start | bytes 884740
  7.2 72.4 %all-gather.3.cloned.1.call-start = ((), (), s32[]{:S(2)}) async-start(), calls=%async_computation.11 | async-start | bytes 6580224 | tf_op jit(solution)/shard_map/all_gather | solution.py:129
  13.9 78.0 %copy-start.35 = (f32[128]{0:T(128)}, f32[128]{0:T(128)S(1)}, u32[]{:S(2)}) copy-start(f32[128]{0:T(128)S(1)} %multiply_power_fusion) | copy-start | bytes 1540
  15.9 76.0 %copy-start.37 = (f32[128]{0:T(128)}, f32[128]{0:T(128)S(1)}, u32[]{:S(2)}) copy-start(f32[128]{0:T(128)S(1)} %convert_bitcast_fusion.2) | copy-start | bytes 1540
  16.2 100.6 %copy-start.25 = (pred[128,1024]{0,1:T(8,128)(4,1)}, pred[128,1024]{0,1:T(8,128)(4,1)S(1)}, u32[]{:S(2)}) copy-start(pred[128,1024]{0,1:T(8,128)(4,1)S(1)} %broadcast_compare_fusion.1) | copy-start | bytes 393220
  92.3 10.7 %copy-start.21 = (f32[128,128]{1,0:T(8,128)}, f32[128,128]{1,0:T(8,128)S(1)}, u32[]{:S(2)}) copy-start(f32[128,128]{1,0:T(8,128)S(1)} %get-tuple-element.60) | copy-start | bytes 196612
  92.3 10.7 %copy-start.23 = (f32[128,128]{1,0:T(8,128)}, f32[128,128]{1,0:T(8,128)S(1)}, u32[]{:S(2)}) copy-start(f32[128,128]{1,0:T(8,128)S(1)} %get-tuple-element.61) | copy-start | bytes 196612
  94.8 21.1 %all-to-all-start = ((bf16[8,128,512]{2,1,0:T(8,128)(2,1)}), bf16[8,128,512]{2,1,0:T(8,128)(2,1)S(1)}, u32[]{:S(2)}, u32[]{:S(2)}) async-start(bf16[8,128,512]{2,1,0:T(8,128)(2,1)} %broadcast_in_dim.56), calls=%async_computation | async-start | bytes 2097152 | tf_op jit(solution)/shard_map/all_to_all | solution.py:83
  99.1 77.9 %all-gather.5.cloned.1.call-start = ((), (), s32[]{:S(2)}) async-start(), calls=%async_computation.12 | async-start | bytes 5013504 | tf_op jit(solution)/shard_map/all_gather | solution.py:186
  103.1 13.7 %copy-start.26 = (f32[128,4,128]{2,0,1:T(8,128)}, f32[128,4,128]{2,0,1:T(8,128)S(1)}, u32[]{:S(2)}) copy-start(f32[128,4,128]{2,0,1:T(8,128)S(1)} %get-tuple-element.53) | copy-start | bytes 786436
  103.1 15.2 %copy-start.28 = (f32[128,4,128]{2,0,1:T(8,128)}, f32[128,4,128]{2,0,1:T(8,128)S(1)}, u32[]{:S(2)}) copy-start(f32[128,4,128]{2,0,1:T(8,128)S(1)} %get-tuple-element.54) | copy-start | bytes 786436
  117.7 212.0 %copy-start.30 = (f32[4,128]{1,0:T(4,128)}, f32[4,128]{1,0:T(4,128)S(1)}, u32[]{:S(2)}) copy-start(f32[4,128]{1,0:T(4,128)S(1)} %log_add_fusion) | copy-start | bytes 6148
  118.3 64.0 %copy-start.16 = (bf16[256,4,128]{2,0,1:T(8,128)(2,1)}, bf16[256,4,128]{2,0,1:T(8,128)(2,1)S(1)}, u32[]{:S(2)}) copy-start(bf16[256,4,128]{2,0,1:T(8,128)(2,1)S(1)} %convolution_convert_fusion.8) | copy-start | bytes 786436
  121.1 275.0 %copy-start.10 = (f32[128,1152]{1,0:T(8,128)}, f32[128,1152]{1,0:T(8,128)S(1)}, u32[]{:S(2)}) copy-start(f32[128,1152]{1,0:T(8,128)S(1)} %get-tuple-element.71) | copy-start | bytes 1769476
  121.1 275.0 %copy-start.32 = (f32[128]{0:T(128)}, f32[128]{0:T(128)S(1)}, u32[]{:S(2)}) copy-start(f32[128]{0:T(128)S(1)} %add_rsqrt_fusion.3) | copy-start | bytes 1540
  324.8 67.9 %all-to-all-start.3 = ((bf16[16,128,1152]{2,1,0:T(8,128)(2,1)}), bf16[16,128,1152]{2,1,0:T(8,128)(2,1)}, u32[]{:S(2)}, u32[]{:S(2)}) async-start(bf16[16,128,1152]{2,1,0:T(8,128)(2,1)} %bitcast.205), calls=%async_computation.3 | async-start | bytes 9437184 | tf_op jit(solution)/shard_map/all_to_all | solution.py:77
  396.6 9.3 %copy-start.8 = (f32[128,1152]{1,0:T(8,128)}, f32[128,1152]{1,0:T(8,128)S(1)}, u32[]{:S(2)}) copy-start(f32[128,1152]{1,0:T(8,128)S(1)} %get-tuple-element.39) | copy-start | bytes 1769476
  407.7 8.3 %copy-start.7 = (f32[128,4,256]{2,0,1:T(8,128)S(1)}, f32[128,4,256]{2,0,1:T(8,128)}, u32[]{:S(2)}) copy-start(f32[128,4,256]{2,0,1:T(8,128)} %copy-done.6) | copy-start | bytes 1572868
  409.2 9.1 %copy-start.15 = (bf16[128,1152]{1,0:T(8,128)(2,1)S(1)}, bf16[128,1152]{1,0:T(8,128)(2,1)}, u32[]{:S(2)}) copy-start(bf16[128,1152]{1,0:T(8,128)(2,1)} %copy-done.14) | copy-start | bytes 884740
  409.2 9.1 %copy-start.17 = (bf16[256,4,128]{2,0,1:T(8,128)(2,1)S(1)}, bf16[256,4,128]{2,0,1:T(8,128)(2,1)}, u32[]{:S(2)}) copy-start(bf16[256,4,128]{2,0,1:T(8,128)(2,1)} %copy-done.16) | copy-start | bytes 786436
  409.2 21.0 %all-to-all-start.4 = ((bf16[8,128,512]{2,1,0:T(8,128)(2,1)}), bf16[8,128,512]{2,1,0:T(8,128)(2,1)S(1)}, u32[]{:S(2)}, u32[]{:S(2)}) async-start(bf16[8,128,512]{2,1,0:T(8,128)(2,1)} %pad_maximum_fusion.2), calls=%async_computation.4 | async-start | bytes 2097152 | tf_op jit(solution)/shard_map/all_to_all | solution.py:77
  414.4 159.4 %reduce-scatter.4.cloned.1.call-start = ((), (), s32[]{:S(2)}) async-start(), calls=%async_computation.13 | async-start | bytes 6266880
  418.3 12.0 %copy-start.36 = (f32[128]{0:T(128)S(1)}, f32[128]{0:T(128)}, u32[]{:S(2)}) copy-start(f32[128]{0:T(128)} %copy-done.35) | copy-start | bytes 1540
  418.3 12.0 %copy-start.38 = (f32[128]{0:T(128)S(1)}, f32[128]{0:T(128)}, u32[]{:S(2)}) copy-start(f32[128]{0:T(128)} %copy-done.37) | copy-start | bytes 1540
  418.4 12.7 %copy-start.34 = (f32[128]{0:T(128)S(1)}, f32[128]{0:T(128)}, u32[]{:S(2)}) copy-start(f32[128]{0:T(128)} %copy-done.33) | copy-start | bytes 1540
  509.9 47.4 %all-to-all-start.9 = ((bf16[8,162,1152]{2,1,0:T(8,128)(2,1)}), bf16[8,162,1152]{2,1,0:T(8,128)(2,1)}, u32[]{:S(2)}, u32[]{:S(2)}) async-start(bf16[8,162,1152]{2,1,0:T(8,128)(2,1)} %broadcast_in_dim.117), calls=%async_computation.9 | async-start | bytes 6193152 | tf_op jit(solution)/shard_map/all_to_all | solution.py:274
  557.4 16.4 %all-to-all-start.5 = ((bf16[16,8,72]{2,1,0:T(8,128)(2,1)}), bf16[16,8,72]{2,1,0:T(8,128)(2,1)S(1)}, u32[]{:S(2)}, u32[]{:S(2)}) async-start(bf16[16,8,72]{2,1,0:T(8,128)(2,1)} %copy.100), calls=%async_computation.5 | async-start | bytes 65536 | tf_op jit(solution)/shard_map/all_to_all | solution.py:269
  576.4 12.5 %all-to-all-start.6 = ((bf16[8,321,72]{1,2,0:T(8,128)(2,1)}), bf16[8,321,72]{1,2,0:T(8,128)(2,1)S(1)}, u32[]{:S(2)}, u32[]{:S(2)}) async-start(bf16[8,321,72]{1,2,0:T(8,128)(2,1)} %copy.102), calls=%async_computation.6 | async-start | bytes 884736 | tf_op jit(solution)/shard_map/all_to_all | solution.py:273
  579.9 13.4 %copy-start.9 = (f32[128,1152]{1,0:T(8,128)S(1)}, f32[128,1152]{1,0:T(8,128)}, u32[]{:S(2)}) copy-start(f32[128,1152]{1,0:T(8,128)} %copy-done.8) | copy-start | bytes 1769476
  589.0 16.0 %copy-start.1 = (bf16[432,1152]{1,0:T(8,128)(2,1)S(1)}, bf16[432,1152]{1,0:T(8,128)(2,1)}, u32[]{:S(2)}) copy-start(bf16[432,1152]{1,0:T(8,128)(2,1)} %param.27) | copy-start | bytes 2985988
  589.9 11.9 %all-to-all-start.7 = ((bf16[8,321,72]{1,2,0:T(8,128)(2,1)}), bf16[8,321,72]{1,2,0:T(8,128)(2,1)S(1)}, u32[]{:S(2)}, u32[]{:S(2)}) async-start(bf16[8,321,72]{1,2,0:T(8,128)(2,1)} %broadcast_in_dim.116), calls=%async_computation.7 | async-start | bytes 884736 | tf_op jit(solution)/shard_map/all_to_all | solution.py:274
  (27 other events, 106.0 us)
Sparse Core Ops, SparseCore 0:
  13.2 66.3 all-gather.2
  122.4 54.6 all-gather.4
  445.5 123.0 reduce-scatter.3
